TPU v7x, 128 devices: a whole 4x4x4 slice. The times are simulated.
128 devices in a mesh: pair: 8 (over x, y_lo), vtile: 16 (over z, y_hi, core).
Axes of the slice: x: 4, y: 4 (y_hi: 2, y_lo: 2; y = y_hi * 2 + y_lo), z: 4, core: 2. Of those that a mesh axis runs over, the one named last changes fastest.
Arguments:
- amplitudes: bfloat16 [128, 512, 512], P(('pair', 'vtile')), may hold values from -1.1953125 to 1.1953125
- factors: bfloat16 [512, 512, 2048], P('vtile', 'pair'), may hold values from -0.125 to 0.125
- pair_list: int32 [128, 2], P(('pair', 'vtile')), may hold values from 0 to 127
- window_offsets: int32 [2], replicated, may hold values from 0 to 511
- occupied_energy: float32 [128], replicated, may hold values from -3 to -0.5
- virtual_energy: float32 [512], replicated, may hold values from 0.5 to 4
Outputs:
- residual: float32 [128, 2, 512], P(('pair', 'vtile'))
- update: float32 [128, 2, 512], P(('pair', 'vtile'))
All inputs are finite; a program needn't handle non-finite values.
Results may differ from a plain program's by a relative error of at most 0.0029.
Values may be sent and summed in bfloat16 or wider, within the bound.
No kernel may reach another device: no remote copies, remote signals or barrier semaphores. Data moves between devices by JAX's collectives and lax.ppermute only.
A program may use at most 128 MiB of HBM per device.

v0:
```python
import jax
import jax.numpy as jnp
from jax import lax
from jax.sharding import PartitionSpec as P


def broadcast(x, axis, root):
    mine = lax.axis_index(axis) == root
    return lax.psum(jnp.where(mine, x, jnp.zeros_like(x)), axis)


def lookup(table, indices):
    positions = jnp.arange(table.shape[0], dtype=jnp.int32)
    return jnp.sum(jnp.where(positions[None, :] == indices[:, None], table[None, :], 0.0), axis=1)


def local(amplitudes, factors, pair_list, window_offsets, occupied_energy, virtual_energy):
    tile_count = lax.axis_size("vtile")
    row_count, col_count, aux_count = factors.shape
    window_count = window_offsets.shape[0]
    local_pairs, virt_count = (amplitudes.shape[0], amplitudes.shape[1])
    local_rows = window_offsets % row_count
    owners = window_offsets // row_count
    picked = jnp.stack(
        [
            lax.dynamic_index_in_dim(factors, local_rows[slot_index], 0, keepdims=False)
            for slot_index in range(window_count)
        ]
    )
    columns = lax.all_gather(picked, "pair", axis=1, tiled=True)
    arows = jnp.stack(
        [
            broadcast(columns[slot_index], "vtile", owners[slot_index])
            for slot_index in range(window_count)
        ]
    )
    integrals = jnp.einsum(
        "acq,bdq->abcd", arows, factors, preferred_element_type=jnp.float32
    ).astype(jnp.bfloat16)
    kernel = integrals.reshape(window_count * row_count, virt_count * col_count)
    blocks = lax.all_gather(amplitudes, "vtile", axis=0, tiled=True)
    gathered = lax.all_to_all(blocks, "pair", split_axis=2, concat_axis=0, tiled=True)
    row_total = gathered.shape[0]
    flat = gathered.reshape(row_total, virt_count * col_count)
    partial_value = lax.dot_general(
        flat, kernel, (((1,), (1,)), ((), ())), preferred_element_type=jnp.float32
    )
    summed = lax.psum_scatter(partial_value, "pair", scatter_dimension=0, tiled=True)
    summed = summed.reshape(tile_count * local_pairs, window_count, row_count)
    residual = lax.all_to_all(summed, "vtile", split_axis=0, concat_axis=2, tiled=True)
    occupied_sum = lookup(occupied_energy, pair_list[:, 0]) + lookup(
        occupied_energy, pair_list[:, 1]
    )
    window_energy = lookup(virtual_energy, window_offsets)
    denominator = (
        window_energy[None, :, None] + virtual_energy[None, None, :] - occupied_sum[:, None, None]
    )
    update = residual / denominator
    return (residual, update)


def solution(mesh):
    return jax.shard_map(
        local,
        mesh=mesh,
        in_specs=(
            P(("pair", "vtile"), None, None),
            P("vtile", "pair", None),
            P(("pair", "vtile"), None),
            P(),
            P(),
            P(),
        ),
        out_specs=(P(("pair", "vtile"), None, None), P(("pair", "vtile"), None, None)),
        check_vma=False,
    )
```

profile of v0, /device:TPU:1, one launch (start us, length us, event | category | flops | bytes accessed | tf_op | source)
XLA Modules:
  0.0 567.2 jit_solution(2779844203682998557)
XLA Ops:
  7.2 0.7 all-gather.5.cloned.1.call-update
  7.9 0.7 and_select_fusion.1
  13.0 1.1 constant_dynamic-slice_fusion.1
  14.1 0.9 pad_maximum_fusion
  15.0 72.3 %all-gather.5.cloned.1.call-done = bf16[16,512,512]{2,1,0:T(8,128)(2,1)} async-done(((bf16[1,512,512]{2,1,0:T(8,128)(2,1)}), bf16[16,512,512]{2,1,0:T(8,128)(2,1)}) %all-gather.5.cloned.1.call-update) | async-done | bytes 8388624 | tf_op jit(solution)/shard_map/all_gather | solution.py:41
  87.3 15.0 %copy.25 = bf16[16,512,512]{1,0,2:T(8,128)(2,1)} copy(bf16[16,512,512]{2,1,0:T(8,128)(2,1)} %all-gather.5.cloned.1.call-done) | data formatting | bytes 16777216 | tf_op jit(solution)/shard_map/all_gather | solution.py:41
  102.3 5.0 all-to-all-start
  108.6 157.4 %all-gather.3.cloned.1.call-done = bf16[2,512,2048]{2,1,0:T(8,128)(2,1)} async-done(((bf16[2,64,2048]{2,1,0:T(8,128)(2,1)}), bf16[2,512,2048]{2,1,0:T(8,128)(2,1)}) %all-gather.3.cloned.1.call-update) | async-done | bytes 4194320 | tf_op jit(solution)/shard_map/all_gather | solution.py:30
  266.0 4.4 slice_select_fusion.1
  271.3 155.8 %all-reduce.3.cloned.1.call-done = (bf16[1,512,2048]{2,1,0:T(8,128)(2,1)}, bf16[1,512,2048]{2,1,0:T(8,128)(2,1)}) async-done(((bf16[1,512,2048]{2,1,0:T(8,128)(2,1)}, bf16[1,512,2048]{2,1,0:T(8,128)(2,1)}), (bf16[1,512,2048]{2,1,0:T(8,128)(2,1)}, bf16[1,512,2048]{2,1,0:T(8,128)(2,1)})) %all-reduce.3.cloned.1.call-update) | async-done | bytes 4194320 | tf_op jit(solution)/shard_map/psum | solution.py:9
  427.1 14.0 %convert_bitcast_fusion = bf16[2,32,512,64]{2,3,1,0:T(8,128)(2,1)} fusion(bf16[32,64,2048]{2,1,0:T(8,128)(2,1)} %param.7, bf16[1,512,2048]{2,1,0:T(8,128)(2,1)} %get-tuple-element.4, bf16[1,512,2048]{2,1,0:T(8,128)(2,1)} %get-tuple-element.5), kind=kOutput, calls=%fused_computation.5 | convolution fusion | flops 8600420352 | bytes 16777216 | tf_op jit(solution)/shard_map/acq,bdq->abcd/dot_general | solution.py:37
  441.0 8.4 %copy.24 = bf16[2,32,512,64]{3,2,1,0:T(8,128)(2,1)} copy(bf16[2,32,512,64]{2,3,1,0:T(8,128)(2,1)} %convert_bitcast_fusion) | data formatting | bytes 8388608 | tf_op jit(solution)/shard_map/convert_element_type | solution.py:39
  449.5 10.6 %reshape.103 = bf16[64,32768]{1,0:T(8,128)(2,1)} reshape(bf16[2,32,512,64]{3,2,1,0:T(8,128)(2,1)} %copy.24) | data formatting | bytes 8388608 | tf_op jit(solution)/shard_map/reshape | solution.py:40
  460.1 17.2 %copy.27 = bf16[8,16,512,64]{3,2,1,0:T(8,128)(2,1)} copy(bf16[8,16,512,64]{2,1,3,0:T(8,128)(2,1)} %bitcast.10) | data formatting | bytes 16777216 | tf_op jit(solution)/shard_map/all_to_all | solution.py:42
  477.3 19.9 %reshape.104 = bf16[128,32768]{1,0:T(8,128)(2,1)} reshape(bf16[8,16,512,64]{3,2,1,0:T(8,128)(2,1)} %copy.27) | data formatting | bytes 16777216 | tf_op jit(solution)/shard_map/reshape | solution.py:44
  497.2 7.7 %convolution_bitcast_fusion = f32[128,64]{0,1:T(8,128)S(1)} fusion(bf16[64,32768]{1,0:T(8,128)(2,1)} %reshape.103, bf16[128,32768]{1,0:T(8,128)(2,1)} %reshape.104), kind=kOutput, calls=%fused_computation.8 | convolution fusion | flops 536870912 | bytes 12615680 | tf_op jit(solution)/shard_map/dot_general | solution.py:45
  504.9 0.7 copy.32
  506.2 32.3 %reduce-scatter.4.cloned.1.call-done = f32[16,64]{1,0:T(8,128)} async-done(((f32[128,64]{1,0:T(8,128)}), f32[16,64]{1,0:T(8,128)}) %reduce-scatter.4.cloned.1.call-update) | async-done | bytes 4112
  538.5 0.8 copy.33
  539.2 0.7 copy.28
  539.9 12.7 %all-to-all-start.1 = ((f32[16,2,32]{2,1,0:T(2,128)}), f32[16,2,32]{2,1,0:T(2,128)S(1)}, u32[]{:S(2)}, u32[]{:S(2)}) async-start(f32[16,2,32]{2,1,0:T(2,128)} %copy.28), calls=%async_computation.1 | async-start | bytes 32768 | tf_op jit(solution)/shard_map/all_to_all | solution.py:50
  552.6 2.0 fusion.8
  555.8 4.1 all-to-all-done.1
  559.9 0.7 subtract_divide_fusion
  (23 shorter events, 2.3 us)
Async XLA Ops:
  7.2 80.1 %all-gather.5.cloned.1.call-start = ((), (), s32[]{:S(2)}) async-start(), calls=%async_computation.4 | async-start | bytes 8912896 | tf_op jit(solution)/shard_map/all_gather | solution.py:41
  7.9 258.1 %all-gather.3.cloned.1.call-start = ((), (), s32[]{:S(2)}) async-start(), calls=%async_computation.3 | async-start | bytes 4718592 | tf_op jit(solution)/shard_map/all_gather | solution.py:30
  102.3 357.8 %all-to-all-start = ((bf16[16,512,512]{1,0,2:T(8,128)(2,1)}), bf16[16,512,512]{1,0,2:T(8,128)(2,1)}, u32[]{:S(2)}, u32[]{:S(2)}) async-start(bf16[16,512,512]{1,0,2:T(8,128)(2,1)} %copy.25), calls=%async_computation | async-start | bytes 16777216 | tf_op jit(solution)/shard_map/all_to_all | solution.py:42
  107.3 319.8 %all-reduce.3.cloned.1.call-start = ((), (), s32[]{:S(2)}) async-start(), calls=%async_computation.6 | async-start | bytes 8388608 | tf_op jit(solution)/shard_map/psum | solution.py:9
  270.4 0.7 copy-start.1
  270.4 0.7 copy-start.4
  270.4 268.0 %reduce-scatter.4.cloned.1.call-start = ((), (), s32[]{:S(2)}) async-start(), calls=%async_computation.5 | async-start | bytes 73728
  497.1 8.4 %copy-start.2 = (s32[1,2]{1,0:T(1,128)S(1)}, s32[1,2]{1,0:T(1,128)}, u32[]{:S(2)}) copy-start(s32[1,2]{1,0:T(1,128)} %param.8) | copy-start | bytes 28
  497.2 55.4 %copy-start.3 = (f32[128]{0:T(128)S(1)}, f32[128]{0:T(128)}, u32[]{:S(2)}) copy-start(f32[128]{0:T(128)} %param.10) | copy-start | bytes 1540
  539.9 20.0 %all-to-all-start.1 = ((f32[16,2,32]{2,1,0:T(2,128)}), f32[16,2,32]{2,1,0:T(2,128)S(1)}, u32[]{:S(2)}, u32[]{:S(2)}) async-start(f32[16,2,32]{2,1,0:T(2,128)} %copy.28), calls=%async_computation.1 | async-start | bytes 32768 | tf_op jit(solution)/shard_map/all_to_all | solution.py:50
  559.9 0.7 copy-start
Sparse Core Ops, SparseCore 0:
  10.5 76.7 all-gather.4
  88.9 177.0 all-gather.2
  270.6 156.4 all-reduce.2
  505.7 32.6 reduce-scatter.3
where the time goes:
time: 569 us; the launch traced here: 567 us
  waiting for transfers between devices  423 us (74%)
  local copies, waits for them, and re-layouts  76.3 us (13%)
  matrix products  21.6 us (4%)
  between operations  20.1 us (4%)
  starting transfers between devices  17.8 us (3%)
  other arithmetic  8.77 us (2%)
    all_gather x1, waiting for transfers between devices, local(): columns = lax.all_gather(picked, 'pair', axis=1, tiled=True)  157 us
    psum x1, waiting for transfers between devices, broadcast(): return lax.psum(jnp.where(mine, x, jnp.zeros_like(x)), axis)  156 us
    all_gather x1, waiting for transfers between devices, local(): blocks = lax.all_gather(amplitudes, 'vtile', axis=0, tiled=True)  72.3 us
    unnamed x5, waiting for transfers between devices  33 us
    reshape x1, local copies, waits for them, and re-layouts, local(): flat = gathered.reshape(row_total, virt_count * col_count)  19.9 us
    all_to_all x1, local copies, waits for them, and re-layouts, local(): lax.all_to_all(blocks, 'pair', split_axis=2, concat_axis=0, tiled=True)  17.2 us
    all_gather x1, local copies, waits for them, and re-layouts, local(): blocks = lax.all_gather(amplitudes, 'vtile', axis=0, tiled=True)  15 us
    dot_general x1, matrix products, local(): jnp.einsum('acq,bdq->abcd', arows, factors, preferred_element_type=jnp.fl...  14 us
  transfers between devices with their start and end apart: 6, of which 5 were waited for; matrix products, arithmetic and copies ran while one was open for 10% of the time, Pallas kernels for 0%

commit v1 on v0

v1 whole, which is shorter than its diff:
```python
import functools

import jax
import jax.numpy as jnp
from jax import lax
from jax.experimental import pallas as pl
from jax.experimental.pallas import tpu as pltpu
from jax.sharding import Mesh, PartitionSpec as P

PAIR = ("x", "yl")
TILE = ("z", "yh", "c")
DB = 8


def shift(x, axis, step, size):
    return lax.ppermute(x, axis, [(i, (i + step) % size) for i in range(size)])


def lookup(table, indices):
    positions = jnp.arange(table.shape[0], dtype=jnp.int32)
    return jnp.sum(jnp.where(positions[None, :] == indices[:, None], table[None, :], 0.0), axis=1)


def integrals_kernel(order, b_ref, *refs):
    pieces, out, rows, sem = refs[:-3], refs[-3], refs[-2], refs[-1]
    width = pieces[0].shape[0]

    def copy(n):
        return pltpu.make_async_copy(pieces[n], rows.at[order[n]], sem.at[n])

    @pl.when(pl.program_id(0) == 0)
    def _():
        for n in range(len(pieces)):
            copy(n).start()
        for n in range(len(pieces)):
            copy(n).wait()

    slab = b_ref[...].reshape(-1, b_ref.shape[-1])
    count = rows.shape[0] * width // 2
    for k in range(2):
        half = rows[k * (rows.shape[0] // 2):(k + 1) * (rows.shape[0] // 2)].reshape(count, rows.shape[-1])
        value = lax.dot_general(slab, half, (((1,), (1,)), ((), ())), preferred_element_type=jnp.float32)
        out[k * slab.shape[0]:(k + 1) * slab.shape[0], :] = value.astype(jnp.bfloat16)


def contract_kernel(order, integrals, *refs):
    pieces, out, held, sem = refs[:-3], refs[-3], refs[-2], refs[-1]
    depth = pieces[0].shape[0]
    group = 4

    def copy(n):
        return pltpu.make_async_copy(pieces[n], held.at[pl.ds(n * depth, depth), :], sem.at[n])

    for n in range(len(pieces)):
        copy(n).start()
    columns = integrals.shape[0]
    folds = columns // DB
    pick_r = lax.broadcasted_iota(jnp.int32, (columns, folds), 0) // DB
    pick_c = lax.broadcasted_iota(jnp.int32, (columns, folds), 1)
    fold = (pick_r == pick_c).astype(jnp.float32)
    size = group * depth
    row = lax.broadcasted_iota(jnp.int32, (size, columns), 0) % DB
    col = lax.broadcasted_iota(jnp.int32, (size, columns), 1) % DB
    same = row == col
    for g in range(len(pieces) // group):
        for n in range(g * group, (g + 1) * group):
            copy(n).wait()
        value = lax.dot_general(
            held[g * size:(g + 1) * size, :], integrals[...], (((1,), (1,)), ((), ())),
            preferred_element_type=jnp.float32)
        value = jnp.where(same, value, 0.0).reshape(size // DB, DB, columns).sum(axis=1)
        value = lax.dot_general(value, fold, (((1,), (0,)), ((), ())),
                                precision=lax.Precision.HIGHEST, preferred_element_type=jnp.float32)
        value = value.reshape(group, depth // DB, folds)
        for n in range(group):
            out[order[g * group + n]] = value[n]


def local(amplitudes, factors, pair_list, window_offsets, occupied_energy, virtual_energy):
    rows_here, cols_here, aux = factors.shape
    virt = amplitudes.shape[1]
    x, yl, z, yh, c = (lax.axis_index(a) for a in ("x", "yl", "z", "yh", "c"))

    tau = amplitudes[0].T.reshape(8, cols_here, virt)
    tau = lax.all_to_all(tau, PAIR, split_axis=0, concat_axis=0, tiled=True)
    tau = tau.reshape(8, cols_here // DB, DB, virt).transpose(0, 2, 1, 3).reshape(8 * DB, cols_here // DB * virt)
    tau_h = shift(tau, "yh", 1, 2)

    owner = window_offsets // rows_here
    row_of = window_offsets % rows_here
    mine = lax.dynamic_index_in_dim(factors, lax.dynamic_index_in_dim(row_of, c, 0, False), 0, False)
    other = lax.dynamic_index_in_dim(factors, lax.dynamic_index_in_dim(row_of, 1 - c, 0, False), 0, False)
    own = lax.dynamic_index_in_dim(owner, c, 0, False)
    own_z, own_h, own_c = own // 4, own // 2 % 2, own % 2
    swapped = shift(other, "c", 1, 2)
    arow = jnp.where(own_c == c, mine, swapped)
    half = arow.shape[0] // 2
    up = shift(arow, "z", 1, 4)
    down = shift(arow, "z", -1, 4)
    far = jnp.concatenate([shift(up[:half], "z", 1, 4), shift(down[half:], "z", -1, 4)])
    rel = (own_z - z) % 4
    arow = jnp.where(rel == 0, arow, jnp.where(rel == 3, up, jnp.where(rel == 1, down, far)))
    cross = shift(arow, "yh", 1, 2)
    arow = jnp.where(own_h == yh, arow, cross)
    arow_l = shift(arow, "yl", 1, 2)
    near = [arow, arow_l]
    up = [shift(a, "x", 1, 4) for a in near]
    down = [shift(a, "x", -1, 4) for a in near]
    far = [shift(up[0], "x", 1, 4), shift(down[1], "x", -1, 4)]
    blocks = near + up + down + far
    places = [(dx, dl) for dx in (0, 3, 1, 2) for dl in (0, 1)]
    blocks = blocks + [shift(a, "c", 1, 2) for a in blocks]
    row_order = jnp.stack([
        k * 8 + (x + dx) % 4 * 2 + (yl + dl) % 2 for k in (c, 1 - c) for dx, dl in places]).astype(jnp.int32)

    n_d = cols_here // DB
    any_spec = pl.BlockSpec(memory_space=pl.ANY)
    integrals = pl.pallas_call(
        integrals_kernel,
        out_shape=jax.ShapeDtypeStruct((2 * rows_here * DB, n_d * virt), jnp.bfloat16),
        grid_spec=pltpu.PrefetchScalarGridSpec(
            num_scalar_prefetch=1, grid=(n_d,),
            in_specs=[pl.BlockSpec((rows_here, DB, aux), lambda d, o: (0, d, 0))] + [any_spec] * 16,
            out_specs=pl.BlockSpec((2 * rows_here * DB, virt), lambda d, o: (0, d)),
            scratch_shapes=[pltpu.VMEM((16, cols_here, aux), jnp.bfloat16), pltpu.SemaphoreType.DMA((16,))]),
        compiler_params=pltpu.CompilerParams(vmem_limit_bytes=40 << 20),
        cost_estimate=pl.CostEstimate(flops=2 * 1024 * 2048 * 2048, bytes_accessed=16 << 20, transcendentals=0),
        name="integrals",
    )(row_order, factors, *blocks)

    near = [tau, tau_h]
    up = [shift(a, "z", 1, 4) for a in near]
    down = [shift(a, "z", -1, 4) for a in near]
    far = [shift(up[0], "z", 1, 4), shift(down[1], "z", -1, 4)]
    pieces = near + up + down + far
    where_z = [(0, 0), (0, 1), (3, 0), (3, 1), (1, 0), (1, 1), (2, 0), (2, 1)]
    pieces = pieces + [shift(a, "c", 1, 2) for a in pieces]
    tau_order = jnp.stack([
        (z + dz) % 4 * 4 + (yh + dh) % 2 * 2 + cc for cc in (c, 1 - c) for dz, dh in where_z]).astype(jnp.int32)

    partial = pl.pallas_call(
        contract_kernel,
        out_shape=jax.ShapeDtypeStruct((16, 8, 2 * rows_here), jnp.float32),
        grid_spec=pltpu.PrefetchScalarGridSpec(
            num_scalar_prefetch=1, grid=(1,),
            in_specs=[pl.BlockSpec(integrals.shape, lambda g, o: (0, 0))] + [any_spec] * 16,
            out_specs=pl.BlockSpec((16, 8, 2 * rows_here), lambda g, o: (0, 0, 0)),
            scratch_shapes=[pltpu.VMEM((1024, n_d * virt), jnp.bfloat16), pltpu.SemaphoreType.DMA((16,))]),
        compiler_params=pltpu.CompilerParams(vmem_limit_bytes=40 << 20),
        cost_estimate=pl.CostEstimate(flops=2 * 1024 * 512 * 4096, bytes_accessed=12 << 20, transcendentals=0),
        name="contract",
    )(tau_order, integrals, *pieces)

    parts = lax.all_to_all(partial.reshape(128, 2 * rows_here), TILE + PAIR, split_axis=0, concat_axis=0, tiled=True)
    residual = parts.reshape(16, 8, 2, rows_here).sum(axis=1).transpose(1, 0, 2).reshape(1, 2, 16 * rows_here)
    occupied_sum = lookup(occupied_energy, pair_list[:, 0]) + lookup(occupied_energy, pair_list[:, 1])
    window_energy = lookup(virtual_energy, window_offsets)
    denominator = (
        window_energy[None, :, None] + virtual_energy[None, None, :] - occupied_sum[:, None, None]
    )
    return residual, residual / denominator


def solution(mesh):
    fine = Mesh(mesh.devices.reshape(4, 2, 4, 2, 2), PAIR + TILE)
    return jax.shard_map(
        local,
        mesh=fine,
        in_specs=(P(PAIR + TILE, None, None), P(TILE, PAIR, None), P(PAIR + TILE, None), P(), P(), P()),
        out_specs=(P(PAIR + TILE, None, None), P(PAIR + TILE, None, None)),
        check_vma=False,
    )
```

time: 569 us -> 157 us (0.28)
  waiting for transfers between devices: 423 us -> 44.5 us
  local copies, waits for them, and re-layouts: 76.3 us -> 19.7 us
  starting transfers between devices: 17.8 us -> 54.9 us
  Pallas kernels: 0 us -> 22.3 us
  matrix products: 21.6 us -> 0 us
  between operations: 20.1 us -> 8.83 us
    all_gather x2 -> x0, waiting for transfers between devices: 230 us -> none  [the longest x1 157 us: local(): columns = lax.all_gather(picked, 'pair', axis=1, tiled=True)]
    psum x1 -> x0, waiting for transfers between devices: 156 us -> none  [broadcast(): return lax.psum(jnp.where(mine, x, jnp.zeros_like(x)), axis)]
    ppermute x0 -> x36, starting transfers between devices: none -> 46 us  [shift(): return lax.ppermute(x, axis, [(i, (i + step) % size) for i in range(size)])]
    ppermute x0 -> x36, waiting for transfers between devices: none -> 33.6 us  [shift(): return lax.ppermute(x, axis, [(i, (i + step) % size) for i in range(size)])]
    unnamed x5 -> x0, waiting for transfers between devices: 33 us -> none
    reshape x3 -> x2, local copies, waits for them, and re-layouts: 31.2 us -> 0.21 us  [local(): parts.reshape(16, 8, 2, rows_here).sum(axis=1).transpose(1, 0, 2)]
    pallas_call x0 -> x2, Pallas kernels: none -> 22.3 us  [the longest x1 14.1 us: local(): pl.pallas_call(integrals_kernel, out_shape=jax.ShapeDtypeStruct((2 * rows...]
    dot_general x2 -> x0, matrix products: 21.6 us -> none  [the longest x1 14 us: local(): jnp.einsum('acq,bdq->abcd', arows, factors, preferred_element_type=jnp.fl...]
  transfers between devices with their start and end apart: 6 -> 38, of which waited for: 5 -> 9; matrix products, arithmetic and copies ran while one was open for 10% -> 5% of each run, Pallas kernels for 0% -> 9%
where the time goes in v1:
time: 157 us; the launch traced here: 156 us
  starting transfers between devices  54.9 us (35%)
  waiting for transfers between devices  44.5 us (28%)
  Pallas kernels  22.3 us (14%)
  local copies, waits for them, and re-layouts  19.7 us (13%)
  between operations  8.83 us (6%)
  other arithmetic  6.2 us (4%)
    ppermute x36, starting transfers between devices, shift(): return lax.ppermute(x, axis, [(i, (i + step) % size) for i in range(size)])  46 us
    ppermute x36, waiting for transfers between devices, shift(): return lax.ppermute(x, axis, [(i, (i + step) % size) for i in range(size)])  33.6 us
    unnamed x51, local copies, waits for them, and re-layouts  15.3 us
    pallas_call x1, Pallas kernels, local(): pl.pallas_call(integrals_kernel, out_shape=jax.ShapeDtypeStruct((2 * rows...  14.1 us
    pallas_call x1, Pallas kernels, local(): pl.pallas_call(contract_kernel, out_shape=jax.ShapeDtypeStruct((16, 8, 2...  8.25 us
    all_to_all x1, waiting for transfers between devices, local(): lax.all_to_all(partial.reshape(128, 2 * rows_here), TILE + PAIR, split_ax...  6.45 us
    all_to_all x1, starting transfers between devices, local(): tau = lax.all_to_all(tau, PAIR, split_axis=0, concat_axis=0, tiled=True)  5.03 us
    all_to_all x1, waiting for transfers between devices, local(): tau = lax.all_to_all(tau, PAIR, split_axis=0, concat_axis=0, tiled=True)  4.51 us
  transfers between devices with their start and end apart: 38, of which 9 were waited for; matrix products, arithmetic and copies ran while one was open for 5% of the time, Pallas kernels for 9%

profile of v1, /device:TPU:1, one launch (start us, length us, event | category | flops | bytes accessed | tf_op | source)
XLA Modules:
  0.0 156.5 jit_solution(2324579209590866484)
XLA Ops:
  13.6 2.2 %collective-permute-start.2 = (bf16[64,2048]{1,0:T(8,128)(2,1)S(1)}, bf16[64,2048]{1,0:T(8,128)(2,1)S(1)}, u32[]{:S(2)}, u32[]{:S(2)}) collective-permute-start(bf16[64,2048]{1,0:T(8,128)(2,1)S(1)} %bitcast_select_fusion), channel_id=1, source_target_pairs={{0,12},{4,0},{8,4},{12,8},{1,13},{5,1},{9,5},{13,9},{2,14},{6,2},{... | collective-permute-start | bytes 786440 | tf_op jit(solution)/shard_map/ppermute | solution.py:16
  15.8 6.6 %collective-permute-done.1 = bf16[64,2048]{1,0:T(8,128)(2,1)S(1)} collective-permute-done((bf16[64,2048]{1,0:T(8,128)(2,1)S(1)}, bf16[64,2048]{1,0:T(8,128)(2,1)S(1)}, u32[]{:S(2)}, u32[]{:S(2)}) %collective-permute-start.1) | collective-permute-done | bytes 262176 | tf_op jit(solution)/shard_map/ppermute | solution.py:16
  22.5 2.7 %collective-permute-start.4 = (bf16[32,2048]{1,0:T(8,128)(2,1)S(1)}, bf16[32,2048]{1,0:T(8,128)(2,1)S(1)}, u32[]{:S(2)}, u32[]{:S(2)}) collective-permute-start(bf16[32,2048]{1,0:T(8,128)(2,1)S(1)} %slice.17), channel_id=1, source_target_pairs={{0,12},{4,0},{8,4},{12,8},{1,13},{5,1},{9,5},{13,9},{2,14},{6,2},{... | collective-permute-start | bytes 393224 | tf_op jit(solution)/shard_map/ppermute | solution.py:16
  25.2 2.1 %copy.15 = bf16[1,512,512]{1,2,0:T(8,128)(2,1)} copy(bf16[1,512,512]{2,1,0:T(8,128)(2,1)} %param.6) | data formatting | bytes 1048576 | tf_op args[0]
  27.3 5.0 %all-to-all-start = ((bf16[8,64,512]{2,1,0:T(8,128)(2,1)}), bf16[8,64,512]{2,1,0:T(8,128)(2,1)S(1)}, u32[]{:S(2)}, u32[]{:S(2)}) async-start(bf16[8,64,512]{2,1,0:T(8,128)(2,1)} %bitcast.39), calls=%async_computation | async-start | bytes 1048576 | tf_op jit(solution)/shard_map/all_to_all | solution.py:85
  33.2 2.7 %collective-permute-start.5 = (bf16[64,2048]{1,0:T(8,128)(2,1)S(1)}, bf16[64,2048]{1,0:T(8,128)(2,1)S(1)}, u32[]{:S(2)}, u32[]{:S(2)}) collective-permute-start(bf16[64,2048]{1,0:T(8,128)(2,1)S(1)} %fusion.1), channel_id=1, source_target_pairs={{0,2},{2,0},{1,3},{3,1},{4,6},{6,4},{5,7},{7,5},{8,10},{10,8},{9,1... | collective-permute-start | bytes 786440 | tf_op jit(solution)/shard_map/ppermute | solution.py:16
  35.9 4.5 %all-to-all-done = bf16[8,64,512]{2,1,0:T(8,128)(2,1)S(1)} async-done(((bf16[8,64,512]{2,1,0:T(8,128)(2,1)}), bf16[8,64,512]{2,1,0:T(8,128)(2,1)S(1)}, u32[]{:S(2)}, u32[]{:S(2)}) %all-to-all-start) | async-done | bytes 524320 | tf_op jit(solution)/shard_map/all_to_all | solution.py:85
  40.4 2.6 %collective-permute-start.21 = (bf16[64,4096]{1,0:T(8,128)(2,1)S(1)}, bf16[64,4096]{1,0:T(8,128)(2,1)S(1)}, u32[]{:S(2)}, u32[]{:S(2)}) collective-permute-start(bf16[64,4096]{1,0:T(8,128)(2,1)S(1)} %bitcast.55), channel_id=1, source_target_pairs={{0,2},{2,0},{1,3},{3,1},{4,6},{6,4},{5,7},{7,5},{8,10},{10,8},{9,1... | collective-permute-start | bytes 1572872 | tf_op jit(solution)/shard_map/ppermute | solution.py:16
  43.0 2.7 %collective-permute-start.24 = (bf16[64,4096]{1,0:T(8,128)(2,1)S(1)}, bf16[64,4096]{1,0:T(8,128)(2,1)S(1)}, u32[]{:S(2)}, u32[]{:S(2)}) collective-permute-start(bf16[64,4096]{1,0:T(8,128)(2,1)S(1)} %bitcast.57), channel_id=1, source_target_pairs={{0,12},{4,0},{8,4},{12,8},{1,13},{5,1},{9,5},{13,9},{2,14},{6,2},{... | collective-permute-start | bytes 1572872 | tf_op jit(solution)/shard_map/ppermute | solution.py:16
  45.7 3.6 %collective-permute-start.28 = (bf16[64,4096]{1,0:T(8,128)(2,1)S(1)}, bf16[64,4096]{1,0:T(8,128)(2,1)S(1)}, u32[]{:S(2)}, u32[]{:S(2)}) collective-permute-start(bf16[64,4096]{1,0:T(8,128)(2,1)S(1)} %bitcast.58), channel_id=1, source_target_pairs={{0,1},{1,0},{2,3},{3,2},{4,5},{5,4},{6,7},{7,6},{8,9},{9,8},{10,11... | collective-permute-start | bytes 1572872 | tf_op jit(solution)/shard_map/ppermute | solution.py:16
  49.6 8.7 %collective-permute-done.21.refs_1_ = bf16[64,4096]{1,0:T(8,128)(2,1)S(1)} collective-permute-done((bf16[64,4096]{1,0:T(8,128)(2,1)S(1)}, bf16[64,4096]{1,0:T(8,128)(2,1)S(1)}, u32[]{:S(2)}, u32[]{:S(2)}) %collective-permute-start.21) | collective-permute-done | bytes 524320 | tf_op jit(solution)/shard_map/ppermute | solution.py:16
  61.0 2.7 %collective-permute-start.13 = (bf16[64,2048]{1,0:T(8,128)(2,1)S(1)}, bf16[64,2048]{1,0:T(8,128)(2,1)S(1)}, u32[]{:S(2)}, u32[]{:S(2)}) collective-permute-start(bf16[64,2048]{1,0:T(8,128)(2,1)S(1)} %broadcast_select_fusion.refs_0_), channel_id=1, source_target_pairs={{0,1},{1,0},{2,3},{3,2},{4,5},{5,4},{6,7},{7,6},{8,9},{9,8},{10,11... | collective-permute-start | bytes 786440 | tf_op jit(solution)/shard_map/ppermute | solution.py:16
  66.5 3.4 %collective-permute-start.14 = (bf16[64,2048]{1,0:T(8,128)(2,1)S(1)}, bf16[64,2048]{1,0:T(8,128)(2,1)S(1)}, u32[]{:S(2)}, u32[]{:S(2)}) collective-permute-start(bf16[64,2048]{1,0:T(8,128)(2,1)S(1)} %collective-permute-done.6.refs_1_), channel_id=1, source_target_pairs={{0,1},{1,0},{2,3},{3,2},{4,5},{5,4},{6,7},{7,6},{8,9},{9,8},{10,11... | collective-permute-start | bytes 786440 | tf_op jit(solution)/shard_map/ppermute | solution.py:16
  75.1 3.4 %collective-permute-done.11.refs_6_ = bf16[64,2048]{1,0:T(8,128)(2,1)} collective-permute-done((bf16[64,2048]{1,0:T(8,128)(2,1)S(1)}, bf16[64,2048]{1,0:T(8,128)(2,1)}, u32[]{:S(2)}, u32[]{:S(2)}) %collective-permute-start.11) | collective-permute-done | bytes 262176 | tf_op jit(solution)/shard_map/ppermute | solution.py:16
  79.9 2.3 %collective-permute-start.29 = (bf16[64,4096]{1,0:T(8,128)(2,1)S(1)}, bf16[64,4096]{1,0:T(8,128)(2,1)S(1)}, u32[]{:S(2)}, u32[]{:S(2)}) collective-permute-start(bf16[64,4096]{1,0:T(8,128)(2,1)S(1)} %collective-permute-done.21.refs_1_), channel_id=1, source_target_pairs={{0,1},{1,0},{2,3},{3,2},{4,5},{5,4},{6,7},{7,6},{8,9},{9,8},{10,11... | collective-permute-start | bytes 1572872 | tf_op jit(solution)/shard_map/ppermute | solution.py:16
  83.0 3.6 %collective-permute-done.25.refs_5_ = bf16[64,4096]{1,0:T(8,128)(2,1)S(1)} collective-permute-done((bf16[64,4096]{1,0:T(8,128)(2,1)S(1)}, bf16[64,4096]{1,0:T(8,128)(2,1)S(1)}, u32[]{:S(2)}, u32[]{:S(2)}) %collective-permute-start.25) | collective-permute-done | bytes 524320 | tf_op jit(solution)/shard_map/ppermute | solution.py:16
  86.6 4.4 %collective-permute-start.12 = (bf16[64,2048]{1,0:T(8,128)(2,1)}, bf16[64,2048]{1,0:T(8,128)(2,1)}, u32[]{:S(2)}, u32[]{:S(2)}) collective-permute-start(bf16[64,2048]{1,0:T(8,128)(2,1)} %collective-permute-done.10.refs_5_), channel_id=1, source_target_pairs={{0,96},{32,0},{64,32},{96,64},{1,97},{33,1},{65,33},{97,65},{2,98}... | collective-permute-start | bytes 786440 | tf_op jit(solution)/shard_map/ppermute | solution.py:16
  92.3 9.9 %collective-permute-done.26.refs_6_ = bf16[64,4096]{1,0:T(8,128)(2,1)S(1)} collective-permute-done((bf16[64,4096]{1,0:T(8,128)(2,1)S(1)}, bf16[64,4096]{1,0:T(8,128)(2,1)S(1)}, u32[]{:S(2)}, u32[]{:S(2)}) %collective-permute-start.26) | collective-permute-done | bytes 524320 | tf_op jit(solution)/shard_map/ppermute | solution.py:16
  102.1 3.1 %collective-permute-start.16 = (bf16[64,2048]{1,0:T(8,128)(2,1)}, bf16[64,2048]{1,0:T(8,128)(2,1)}, u32[]{:S(2)}, u32[]{:S(2)}) collective-permute-start(bf16[64,2048]{1,0:T(8,128)(2,1)} %collective-permute-done.8.refs_3_), channel_id=1, source_target_pairs={{0,1},{1,0},{2,3},{3,2},{4,5},{5,4},{6,7},{7,6},{8,9},{9,8},{10,11... | collective-permute-start | bytes 786440 | tf_op jit(solution)/shard_map/ppermute | solution.py:16
  118.1 14.1 %integrals.1 = bf16[512,4096]{1,0:T(8,128)(2,1)S(1)} custom-call(s32[16]{0:T(128)S(1)} %stack.135.order, bf16[32,64,2048]{2,1,0:T(8,128)(2,1)} %b_ref.1, bf16[64,2048]{1,0:T(8,128)(2,1)S(1)} %broadcast_select_fusion.refs_0_, bf16[64,2048]{1,0:T(8,128)(2,1)S(1)} %copy-done.9, bf16[64,2048]{1,0:T(8,128)(2,1)S(1)} %copy-done.11, ...), custom_call_target="tpu_custom_call" | custom-call | flops 8589934592 | bytes 16777216 | tf_op jit(solution)/shard_map/integrals/pallas_call | solution.py:118
  132.4 8.2 %contract.1 = f32[16,8,64]{2,1,0:T(8,128)} custom-call(s32[16]{0:T(128)S(1)} %stack.118.order, bf16[512,4096]{1,0:T(8,128)(2,1)S(1)} %integrals.1, bf16[64,4096]{1,0:T(8,128)(2,1)S(1)} %bitcast.59, bf16[64,4096]{1,0:T(8,128)(2,1)S(1)} %collective-permute-done.21.refs_1_, bf16[64,4096]{1,0:T(8,128)(2,1)S(1)} %collective-permute-done.22.refs_2_, ...), custom_call_target="tpu_custom_call" | custom-call | flops 4294967296 | bytes 12582912 | tf_op jit(solution)/shard_map/contract/pallas_call | solution.py:141
  140.6 3.9 %all-to-all-start.1 = ((f32[128,1,64]{2,1,0:T(1,128)}), f32[128,1,64]{2,1,0:T(1,128)S(1)}, u32[]{:S(2)}, u32[]{:S(2)}) async-start(f32[128,1,64]{2,1,0:T(1,128)} %bitcast.46), calls=%async_computation.1 | async-start | bytes 131072 | tf_op jit(solution)/shard_map/all_to_all | solution.py:154
  144.5 2.0 %fusion.4 = (f32[]{:T(128)}, f32[]{:T(128)}) fusion(f32[128]{0:T(128)S(1)} %copy-done.24, s32[]{:T(128)} %bitcast.49, s32[]{:T(128)} %bitcast.48), kind=kLoop, calls=%fused_computation.17 | loop fusion | flops 766 | bytes 528 | tf_op jit(solution)/shard_map/reduce_sum | solution.py:21
  147.7 6.5 %all-to-all-done.1 = f32[128,1,64]{2,1,0:T(1,128)S(1)} async-done(((f32[128,1,64]{2,1,0:T(1,128)}), f32[128,1,64]{2,1,0:T(1,128)S(1)}, u32[]{:S(2)}, u32[]{:S(2)}) %all-to-all-start.1) | async-done | bytes 32800 | tf_op jit(solution)/shard_map/all_to_all | solution.py:154
  (126 shorter events, 36.8 us)
Async XLA Ops:
  11.8 10.6 %collective-permute-start.1 = (bf16[64,2048]{1,0:T(8,128)(2,1)S(1)}, bf16[64,2048]{1,0:T(8,128)(2,1)S(1)}, u32[]{:S(2)}, u32[]{:S(2)}) collective-permute-start(bf16[64,2048]{1,0:T(8,128)(2,1)S(1)} %bitcast_select_fusion), channel_id=1, source_target_pairs={{0,4},{4,8},{8,12},{12,0},{1,5},{5,9},{9,13},{13,1},{2,6},{6,10},{... | collective-permute-start | bytes 786440 | tf_op jit(solution)/shard_map/ppermute | solution.py:16
  22.4 10.6 %collective-permute-start.3 = (bf16[32,2048]{1,0:T(8,128)(2,1)S(1)}, bf16[32,2048]{1,0:T(8,128)(2,1)S(1)}, u32[]{:S(2)}, u32[]{:S(2)}) collective-permute-start(bf16[32,2048]{1,0:T(8,128)(2,1)S(1)} %slice.16), channel_id=1, source_target_pairs={{0,4},{4,8},{8,12},{12,0},{1,5},{5,9},{9,13},{13,1},{2,6},{6,10},{... | collective-permute-start | bytes 393224 | tf_op jit(solution)/shard_map/ppermute | solution.py:16
  27.3 13.1 %all-to-all-start = ((bf16[8,64,512]{2,1,0:T(8,128)(2,1)}), bf16[8,64,512]{2,1,0:T(8,128)(2,1)S(1)}, u32[]{:S(2)}, u32[]{:S(2)}) async-start(bf16[8,64,512]{2,1,0:T(8,128)(2,1)} %bitcast.39), calls=%async_computation | async-start | bytes 1048576 | tf_op jit(solution)/shard_map/all_to_all | solution.py:85
  33.2 16.1 %collective-permute-start.5 = (bf16[64,2048]{1,0:T(8,128)(2,1)S(1)}, bf16[64,2048]{1,0:T(8,128)(2,1)S(1)}, u32[]{:S(2)}, u32[]{:S(2)}) collective-permute-start(bf16[64,2048]{1,0:T(8,128)(2,1)S(1)} %fusion.1), channel_id=1, source_target_pairs={{0,2},{2,0},{1,3},{3,1},{4,6},{6,4},{5,7},{7,5},{8,10},{10,8},{9,1... | collective-permute-start | bytes 786440 | tf_op jit(solution)/shard_map/ppermute | solution.py:16
  40.4 18.0 %collective-permute-start.21 = (bf16[64,4096]{1,0:T(8,128)(2,1)S(1)}, bf16[64,4096]{1,0:T(8,128)(2,1)S(1)}, u32[]{:S(2)}, u32[]{:S(2)}) collective-permute-start(bf16[64,4096]{1,0:T(8,128)(2,1)S(1)} %bitcast.55), channel_id=1, source_target_pairs={{0,2},{2,0},{1,3},{3,1},{4,6},{6,4},{5,7},{7,5},{8,10},{10,8},{9,1... | collective-permute-start | bytes 1572872 | tf_op jit(solution)/shard_map/ppermute | solution.py:16
  43.0 16.4 %collective-permute-start.22 = (bf16[64,4096]{1,0:T(8,128)(2,1)S(1)}, bf16[64,4096]{1,0:T(8,128)(2,1)S(1)}, u32[]{:S(2)}, u32[]{:S(2)}) collective-permute-start(bf16[64,4096]{1,0:T(8,128)(2,1)S(1)} %bitcast.56), channel_id=1, source_target_pairs={{0,4},{4,8},{8,12},{12,0},{1,5},{5,9},{9,13},{13,1},{2,6},{6,10},{... | collective-permute-start | bytes 1572872 | tf_op jit(solution)/shard_map/ppermute | solution.py:16
  43.0 18.0 %collective-permute-start.24 = (bf16[64,4096]{1,0:T(8,128)(2,1)S(1)}, bf16[64,4096]{1,0:T(8,128)(2,1)S(1)}, u32[]{:S(2)}, u32[]{:S(2)}) collective-permute-start(bf16[64,4096]{1,0:T(8,128)(2,1)S(1)} %bitcast.57), channel_id=1, source_target_pairs={{0,12},{4,0},{8,4},{12,8},{1,13},{5,1},{9,5},{13,9},{2,14},{6,2},{... | collective-permute-start | bytes 1572872 | tf_op jit(solution)/shard_map/ppermute | solution.py:16
  45.7 19.4 %collective-permute-start.28 = (bf16[64,4096]{1,0:T(8,128)(2,1)S(1)}, bf16[64,4096]{1,0:T(8,128)(2,1)S(1)}, u32[]{:S(2)}, u32[]{:S(2)}) collective-permute-start(bf16[64,4096]{1,0:T(8,128)(2,1)S(1)} %bitcast.58), channel_id=1, source_target_pairs={{0,1},{1,0},{2,3},{3,2},{4,5},{5,4},{6,7},{7,6},{8,9},{9,8},{10,11... | collective-permute-start | bytes 1572872 | tf_op jit(solution)/shard_map/ppermute | solution.py:16
  49.3 15.0 %collective-permute-start.6 = (bf16[64,2048]{1,0:T(8,128)(2,1)S(1)}, bf16[64,2048]{1,0:T(8,128)(2,1)S(1)}, u32[]{:S(2)}, u32[]{:S(2)}) collective-permute-start(bf16[64,2048]{1,0:T(8,128)(2,1)S(1)} %broadcast_select_fusion.refs_0_), channel_id=1, source_target_pairs={{0,16},{16,0},{1,17},{17,1},{2,18},{18,2},{3,19},{19,3},{4,20},{20... | collective-permute-start | bytes 786440 | tf_op jit(solution)/shard_map/ppermute | solution.py:16
  65.7 12.8 %collective-permute-start.11 = (bf16[64,2048]{1,0:T(8,128)(2,1)S(1)}, bf16[64,2048]{1,0:T(8,128)(2,1)}, u32[]{:S(2)}, u32[]{:S(2)}) collective-permute-start(bf16[64,2048]{1,0:T(8,128)(2,1)S(1)} %collective-permute-done.7.refs_2_), channel_id=1, source_target_pairs={{0,32},{32,64},{64,96},{96,0},{1,33},{33,65},{65,97},{97,1},{2,34}... | collective-permute-start | bytes 786440 | tf_op jit(solution)/shard_map/ppermute | solution.py:16
  66.5 12.1 %collective-permute-start.14 = (bf16[64,2048]{1,0:T(8,128)(2,1)S(1)}, bf16[64,2048]{1,0:T(8,128)(2,1)S(1)}, u32[]{:S(2)}, u32[]{:S(2)}) collective-permute-start(bf16[64,2048]{1,0:T(8,128)(2,1)S(1)} %collective-permute-done.6.refs_1_), channel_id=1, source_target_pairs={{0,1},{1,0},{2,3},{3,2},{4,5},{5,4},{6,7},{7,6},{8,9},{9,8},{10,11... | collective-permute-start | bytes 786440 | tf_op jit(solution)/shard_map/ppermute | solution.py:16
  75.1 11.6 %collective-permute-start.25 = (bf16[64,4096]{1,0:T(8,128)(2,1)S(1)}, bf16[64,4096]{1,0:T(8,128)(2,1)S(1)}, u32[]{:S(2)}, u32[]{:S(2)}) collective-permute-start(bf16[64,4096]{1,0:T(8,128)(2,1)S(1)} %collective-permute-done.21.refs_1_), channel_id=1, source_target_pairs={{0,12},{4,0},{8,4},{12,8},{1,13},{5,1},{9,5},{13,9},{2,14},{6,2},{... | collective-permute-start | bytes 1572872 | tf_op jit(solution)/shard_map/ppermute | solution.py:16
  78.5 12.5 %collective-permute-start.23 = (bf16[64,4096]{1,0:T(8,128)(2,1)S(1)}, bf16[64,4096]{1,0:T(8,128)(2,1)S(1)}, u32[]{:S(2)}, u32[]{:S(2)}) collective-permute-start(bf16[64,4096]{1,0:T(8,128)(2,1)S(1)} %collective-permute-done.21.refs_1_), channel_id=1, source_target_pairs={{0,4},{4,8},{8,12},{12,0},{1,5},{5,9},{9,13},{13,1},{2,6},{6,10},{... | collective-permute-start | bytes 1572872 | tf_op jit(solution)/shard_map/ppermute | solution.py:16
  79.2 22.9 %collective-permute-start.26 = (bf16[64,4096]{1,0:T(8,128)(2,1)S(1)}, bf16[64,4096]{1,0:T(8,128)(2,1)S(1)}, u32[]{:S(2)}, u32[]{:S(2)}) collective-permute-start(bf16[64,4096]{1,0:T(8,128)(2,1)S(1)} %collective-permute-done.22.refs_2_), channel_id=1, source_target_pairs={{0,4},{4,8},{8,12},{12,0},{1,5},{5,9},{9,13},{13,1},{2,6},{6,10},{... | collective-permute-start | bytes 1572872 | tf_op jit(solution)/shard_map/ppermute | solution.py:16
  79.9 25.3 %collective-permute-start.29 = (bf16[64,4096]{1,0:T(8,128)(2,1)S(1)}, bf16[64,4096]{1,0:T(8,128)(2,1)S(1)}, u32[]{:S(2)}, u32[]{:S(2)}) collective-permute-start(bf16[64,4096]{1,0:T(8,128)(2,1)S(1)} %collective-permute-done.21.refs_1_), channel_id=1, source_target_pairs={{0,1},{1,0},{2,3},{3,2},{4,5},{5,4},{6,7},{7,6},{8,9},{9,8},{10,11... | collective-permute-start | bytes 1572872 | tf_op jit(solution)/shard_map/ppermute | solution.py:16
  83.0 23.2 %collective-permute-start.30 = (bf16[64,4096]{1,0:T(8,128)(2,1)S(1)}, bf16[64,4096]{1,0:T(8,128)(2,1)S(1)}, u32[]{:S(2)}, u32[]{:S(2)}) collective-permute-start(bf16[64,4096]{1,0:T(8,128)(2,1)S(1)} %collective-permute-done.22.refs_2_), channel_id=1, source_target_pairs={{0,1},{1,0},{2,3},{3,2},{4,5},{5,4},{6,7},{7,6},{8,9},{9,8},{10,11... | collective-permute-start | bytes 1572872 | tf_op jit(solution)/shard_map/ppermute | solution.py:16
  86.6 20.8 %collective-permute-start.12 = (bf16[64,2048]{1,0:T(8,128)(2,1)}, bf16[64,2048]{1,0:T(8,128)(2,1)}, u32[]{:S(2)}, u32[]{:S(2)}) collective-permute-start(bf16[64,2048]{1,0:T(8,128)(2,1)} %collective-permute-done.10.refs_5_), channel_id=1, source_target_pairs={{0,96},{32,0},{64,32},{96,64},{1,97},{33,1},{65,33},{97,65},{2,98}... | collective-permute-start | bytes 786440 | tf_op jit(solution)/shard_map/ppermute | solution.py:16
  91.0 20.2 %collective-permute-start.27 = (bf16[64,4096]{1,0:T(8,128)(2,1)S(1)}, bf16[64,4096]{1,0:T(8,128)(2,1)}, u32[]{:S(2)}, u32[]{:S(2)}) collective-permute-start(bf16[64,4096]{1,0:T(8,128)(2,1)S(1)} %collective-permute-done.25.refs_5_), channel_id=1, source_target_pairs={{0,12},{4,0},{8,4},{12,8},{1,13},{5,1},{9,5},{13,9},{2,14},{6,2},{... | collective-permute-start | bytes 1572872 | tf_op jit(solution)/shard_map/ppermute | solution.py:16
  110.0 22.3 %collective-permute-start.32 = (bf16[64,4096]{1,0:T(8,128)(2,1)S(1)}, bf16[64,4096]{1,0:T(8,128)(2,1)S(1)}, u32[]{:S(2)}, u32[]{:S(2)}) collective-permute-start(bf16[64,4096]{1,0:T(8,128)(2,1)S(1)} %collective-permute-done.24.refs_4_), channel_id=1, source_target_pairs={{0,1},{1,0},{2,3},{3,2},{4,5},{5,4},{6,7},{7,6},{8,9},{9,8},{10,11... | collective-permute-start | bytes 1572872 | tf_op jit(solution)/shard_map/ppermute | solution.py:16
  110.4 21.8 %collective-permute-start.33 = (bf16[64,4096]{1,0:T(8,128)(2,1)S(1)}, bf16[64,4096]{1,0:T(8,128)(2,1)S(1)}, u32[]{:S(2)}, u32[]{:S(2)}) collective-permute-start(bf16[64,4096]{1,0:T(8,128)(2,1)S(1)} %collective-permute-done.25.refs_5_), channel_id=1, source_target_pairs={{0,1},{1,0},{2,3},{3,2},{4,5},{5,4},{6,7},{7,6},{8,9},{9,8},{10,11... | collective-permute-start | bytes 1572872 | tf_op jit(solution)/shard_map/ppermute | solution.py:16
  110.7 21.6 %collective-permute-start.31 = (bf16[64,4096]{1,0:T(8,128)(2,1)}, bf16[64,4096]{1,0:T(8,128)(2,1)S(1)}, u32[]{:S(2)}, u32[]{:S(2)}) collective-permute-start(bf16[64,4096]{1,0:T(8,128)(2,1)} %copy-done), channel_id=1, source_target_pairs={{0,1},{1,0},{2,3},{3,2},{4,5},{5,4},{6,7},{7,6},{8,9},{9,8},{10,11... | collective-permute-start | bytes 1572872 | tf_op jit(solution)/shard_map/ppermute | solution.py:16
  111.0 21.3 %collective-permute-start.34 = (bf16[64,4096]{1,0:T(8,128)(2,1)}, bf16[64,4096]{1,0:T(8,128)(2,1)S(1)}, u32[]{:S(2)}, u32[]{:S(2)}) collective-permute-start(bf16[64,4096]{1,0:T(8,128)(2,1)} %copy-done.2), channel_id=1, source_target_pairs={{0,1},{1,0},{2,3},{3,2},{4,5},{5,4},{6,7},{7,6},{8,9},{9,8},{10,11... | collective-permute-start | bytes 1572872 | tf_op jit(solution)/shard_map/ppermute | solution.py:16
  111.2 21.1 %collective-permute-start.35 = (bf16[64,4096]{1,0:T(8,128)(2,1)}, bf16[64,4096]{1,0:T(8,128)(2,1)S(1)}, u32[]{:S(2)}, u32[]{:S(2)}) collective-permute-start(bf16[64,4096]{1,0:T(8,128)(2,1)} %collective-permute-done.27.refs_7_), channel_id=1, source_target_pairs={{0,1},{1,0},{2,3},{3,2},{4,5},{5,4},{6,7},{7,6},{8,9},{9,8},{10,11... | collective-permute-start | bytes 1572872 | tf_op jit(solution)/shard_map/ppermute | solution.py:16
  140.6 13.6 %all-to-all-start.1 = ((f32[128,1,64]{2,1,0:T(1,128)}), f32[128,1,64]{2,1,0:T(1,128)S(1)}, u32[]{:S(2)}, u32[]{:S(2)}) async-start(f32[128,1,64]{2,1,0:T(1,128)} %bitcast.46), calls=%async_computation.1 | async-start | bytes 131072 | tf_op jit(solution)/shard_map/all_to_all | solution.py:154
  (39 other events, 264.4 us)

commit v2 on v0

v2 whole, which is shorter than its diff:
```python
import functools

import jax
import jax.numpy as jnp
from jax import lax
from jax.experimental import pallas as pl
from jax.experimental.pallas import tpu as pltpu
from jax.sharding import Mesh, PartitionSpec as P

PAIR = ("x", "yl")
TILE = ("z", "yh", "c")
DB = 8
LANES = 128


def shift(x, axis, step, size):
    return lax.ppermute(x, axis, [(i, (i + step) % size) for i in range(size)])


def shift_y(x, step):
    at = [y % 2 * 2 + y // 2 for y in range(4)]
    return lax.ppermute(x, ("yl", "yh"), [(at[y], at[(y + step) % 4]) for y in range(4)])


def lookup(table, indices):
    positions = jnp.arange(table.shape[0], dtype=jnp.int32)
    return jnp.sum(jnp.where(positions[None, :] == indices[:, None], table[None, :], 0.0), axis=1)


def pick_kernel(rows, offsets, factors, mine, other, sem):
    c = lax.axis_index("c")
    first = pltpu.make_async_copy(factors.at[offsets[c] % rows], mine, sem.at[0])
    second = pltpu.make_async_copy(factors.at[offsets[1 - c] % rows], other, sem.at[1])
    first.start()
    second.start()
    first.wait()
    second.wait()


def halve_kernel(rows, offsets, mine, swapped, keep, send, sem):
    c, h = lax.axis_index("c"), lax.axis_index("yh")
    size = keep.shape[0]

    def move(source):
        first = pltpu.make_async_copy(source.at[pl.ds(h * size, size), :], keep, sem.at[0])
        second = pltpu.make_async_copy(source.at[pl.ds((1 - h) * size, size), :], send, sem.at[1])
        first.start()
        second.start()
        first.wait()
        second.wait()

    here = offsets[c] // rows % 2 == c

    @pl.when(here)
    def _():
        move(mine)

    @pl.when(jnp.logical_not(here))
    def _():
        move(swapped)


def choose_kernel(rows, offsets, keep, got, out, sem):
    here = offsets[lax.axis_index("c")] // (2 * rows) % 2 == lax.axis_index("yh")
    for source, wanted in ((keep, here), (got, jnp.logical_not(here))):
        @pl.when(wanted)
        def _():
            copy = pltpu.make_async_copy(source, out, sem.at[0])
            copy.start()
            copy.wait()


def choose_z_kernel(rows, offsets, own, up, down, far, out, sem):
    rel = (offsets[lax.axis_index("c")] // (4 * rows) + 4 - lax.axis_index("z")) % 4
    for source, wanted in ((own, 0), (down, 1), (far, 2), (up, 3)):
        @pl.when(rel == wanted)
        def _():
            copy = pltpu.make_async_copy(source, out, sem.at[0])
            copy.start()
            copy.wait()


def place_kernel(own, up, down, far, out, sem):
    y = lax.axis_index("yh") * 2 + lax.axis_index("yl")
    size = own.shape[0]
    copies = []
    for n, (piece, step) in enumerate(((own, 0), (up, 3), (down, 1), (far, 2))):
        at = (y + step) % 4
        at = at % 2 * 2 + at // 2
        copies.append(pltpu.make_async_copy(piece, out.at[pl.ds(at * size, size), :], sem.at[n]))
    for copy in copies:
        copy.start()
    for copy in copies:
        copy.wait()


ANY = pl.BlockSpec(memory_space=pl.ANY)
SMALL = pl.BlockSpec(memory_space=pltpu.SMEM)


def move_call(body, name, shapes, n_in, n_sem, small=True):
    specs = ([SMALL] if small else []) + [ANY] * n_in
    return pl.pallas_call(
        body,
        out_shape=[jax.ShapeDtypeStruct(shape, jnp.bfloat16) for shape in shapes],
        in_specs=specs,
        out_specs=[ANY] * len(shapes),
        scratch_shapes=[pltpu.SemaphoreType.DMA((n_sem,))],
        compiler_params=pltpu.CompilerParams(vmem_limit_bytes=1 << 20),
        cost_estimate=pl.CostEstimate(flops=0, bytes_accessed=1 << 20, transcendentals=0),
        name=name,
    )


def integrals(held, pieces, flips, out):
    rows, cols, aux = held.shape
    deep = 2 * DB
    side = [p[...] for p in pieces]
    side = jnp.concatenate(side, axis=0)
    for step in range(cols // deep):
        yield step
        slab = held[:, step * deep:(step + 1) * deep, :].reshape(rows * deep, aux)
        value = lax.dot_general(slab, side, (((1,), (1,)), ((), ())), preferred_element_type=jnp.float32)
        value = value.astype(jnp.bfloat16).reshape(rows, deep // DB, DB, side.shape[0])
        for n in range(side.shape[0] // LANES):
            k = (n + flips[n // 2]) % 2
            for d in range(deep // DB):
                block = value[:, d, :, n * LANES:(n + 1) * LANES].reshape(rows * DB, LANES)
                at = step * deep // DB + d
                out[n // 2, k * rows * DB:(k + 1) * rows * DB, at * LANES:(at + 1) * LANES] = block


def first_kernel(factors, first, second, out, held, sem):
    deep = 2 * DB
    copies = []
    for step in range(held.shape[1] // deep):
        part = pl.ds(step * deep, deep)
        copies.append(pltpu.make_async_copy(factors.at[:, part, :], held.at[:, part, :], sem.at[step]))
        copies[-1].start()
    for step in integrals(held, (first, second), (0,), out):
        copies[step].wait()


def next_kernel(flips, held, *refs):
    for _ in integrals(held, refs[:-1], flips, refs[-1]):
        pass


IN_VMEM = pl.BlockSpec(memory_space=pltpu.VMEM)
IN_HBM = pl.BlockSpec(memory_space=pltpu.HBM)


def integrals_of(factors, pieces, flips, name, load=False):
    rows, cols, aux = factors.shape
    count = len(flips)
    out_shape = [jax.ShapeDtypeStruct((count, 2 * rows * DB, cols // DB * LANES), jnp.bfloat16)]
    if load:
        out_shape.append(jax.ShapeDtypeStruct(factors.shape, factors.dtype))
    return pl.pallas_call(
        first_kernel if load else functools.partial(next_kernel, flips),
        out_shape=out_shape,
        in_specs=[IN_HBM if load else IN_VMEM] + [IN_VMEM] * len(pieces),
        out_specs=[IN_VMEM] * len(out_shape),
        scratch_shapes=[pltpu.SemaphoreType.DMA((4,))] if load else [],
        compiler_params=pltpu.CompilerParams(vmem_limit_bytes=12 << 20),
        cost_estimate=pl.CostEstimate(flops=2 * 256 * count * 2048 * 2048, bytes_accessed=10 << 20, transcendentals=0),
        name=name,
    )(factors, *pieces)


def products(ints, pieces, groups):
    x, c = lax.axis_index("x"), lax.axis_index("c")
    wide = ints[0].shape[2]
    ahead = jnp.where(c == 0, 3, 1)
    chunk = (x, (x + ahead) % 4, (x + 4 - ahead) % 4, (x + 2) % 4)
    where_int = [(i, n) for i in ints for n in range(i.shape[0])]
    for g in range(groups):
        total = None
        for (ref, inner), at in zip(where_int, chunk):
            at = pl.ds(pl.multiple_of(at * wide, wide), wide)
            side = jnp.concatenate([pieces[2 * g][:, at], pieces[2 * g + 1][:, at]], axis=0)
            value = lax.dot_general(ref[inner], side, (((1,), (1,)), ((), ())), preferred_element_type=jnp.float32)
            total = value if total is None else total + value
        yield total


def early_kernel(*refs):
    ints, pieces, out = refs[:3], refs[3:-1], refs[-1]
    for g, total in enumerate(products(ints, pieces, len(pieces) // 2)):
        for n in range(total.shape[1] // LANES):
            out[g, n] = total[:, n * LANES:(n + 1) * LANES]


def late_kernel(*refs):
    ints, pieces, before, out, spare = refs[:3], refs[3:-3], refs[-3], refs[-2], refs[-1]
    z, h, c = (lax.axis_index(a) for a in ("z", "yh", "c"))
    ahead = jnp.where(c == 0, 3, 1)
    here = (c, 1 - c)
    away = (1 - c, c)
    places = (
        (z, h, here), (z, 1 - h, here),
        ((z + ahead) % 4, h, here), ((z + 4 - ahead) % 4, h, away),
        ((z + ahead) % 4, 1 - h, here), ((z + 4 - ahead) % 4, 1 - h, away),
        ((z + 2) % 4, (h + c) % 2, here), ((z + 2) % 4, (h + 1 - c) % 2, away),
    )
    groups, parts, rows, _ = before.shape
    depth = parts * LANES
    for total in products(ints, pieces, 1):
        for n in range(parts):
            spare[n] = total[:, n * LANES:(n + 1) * LANES]
    small = rows // DB
    folds = depth // DB
    fold = (lax.broadcasted_iota(jnp.int32, (folds, depth), 1) // DB
            == lax.broadcasted_iota(jnp.int32, (folds, depth), 0)).astype(jnp.float32)
    lane = lax.broadcasted_iota(jnp.int32, (small, LANES), 1) % DB
    for g in range(groups + 1):
        columns = []
        for n in range(parts):
            source = before.at[g, n] if g < groups else spare.at[n]
            total = source[pl.ds(0, small, stride=DB), :]
            for d in range(1, DB):
                total = jnp.where(lane == d, source[pl.ds(d, small, stride=DB), :], total)
            columns.append(total)
        total = jnp.concatenate(columns, axis=1)
        total = jnp.where(c == 0, total, jnp.concatenate([total[small // 2:], total[:small // 2]], axis=0))
        total = lax.dot_general(fold, total, (((1,), (1,)), ((), ())),
                                precision=lax.Precision.HIGHEST, preferred_element_type=jnp.float32)
        total = total.reshape(4, folds // 4, small)
        for n in range(4):
            at_z, at_h, cores = places[2 * g + n // 2]
            out[at_z * 4 + at_h * 2 + cores[n % 2]] = total[n]


def contract(ints, pieces, before):
    rows, depth = ints[0].shape[1], 2 * pieces[0].shape[0]
    groups = len(pieces) // 2
    if before is None:
        out_shape = jax.ShapeDtypeStruct((groups, depth // LANES, rows, LANES), jnp.float32)
    else:
        out_shape = jax.ShapeDtypeStruct((16, 8, rows // DB), jnp.float32)
    given = list(ints) + list(pieces) + ([] if before is None else [before])
    return pl.pallas_call(
        early_kernel if before is None else late_kernel,
        out_shape=out_shape,
        in_specs=[IN_VMEM] * len(given),
        out_specs=IN_VMEM,
        scratch_shapes=[] if before is None else [pltpu.VMEM((depth // LANES, rows, LANES), jnp.float32)],
        compiler_params=pltpu.CompilerParams(vmem_limit_bytes=12 << 20),
        cost_estimate=pl.CostEstimate(
            flops=2 * rows * depth * 4096 * groups, bytes_accessed=8 << 20, transcendentals=0),
        name="contract_early" if before is None else "contract_late",
    )(*given)


def core_swap(x):
    return shift(x, "c", 1, 2)


def both_ways(x, axis):
    pairs = [(i * 2 + c, (i + (1 if c == 0 else 3)) % 4 * 2 + c) for i in range(4) for c in range(2)]
    return lax.ppermute(x, (axis, "c"), pairs)


def local(amplitudes, factors, pair_list, window_offsets, occupied_energy, virtual_energy):
    rows_here, cols_here, aux = factors.shape
    virt = amplitudes.shape[1]
    n_d = cols_here // DB
    c = lax.axis_index("c")
    held = pltpu.with_memory_space_constraint(factors, pltpu.VMEM)
    factors = pltpu.with_memory_space_constraint(factors, pltpu.HBM)

    def lay(first, second):
        both = jnp.stack([first, second]).reshape(2, 8, n_d, DB, 4, LANES)
        return both.transpose(0, 1, 3, 4, 2, 5).reshape(2 * 8 * DB, n_d * virt)

    tau = amplitudes[0].T.reshape(8, cols_here, virt)
    tau = lax.all_to_all(tau, PAIR, split_axis=0, concat_axis=0, tiled=True)
    mine, other = move_call(
        functools.partial(pick_kernel, rows_here), "pick", [(cols_here, aux)] * 2, 1, 2)(window_offsets, factors)
    swapped = core_swap(other)
    keep, send = move_call(
        functools.partial(halve_kernel, rows_here), "halve", [(cols_here // 2, aux)] * 2, 2, 2)(
            window_offsets, mine, swapped)
    send, tau = lax.optimization_barrier((send, tau))

    got = shift(send, "yh", 1, 2)
    got, tau = lax.optimization_barrier((got, tau))
    tau_h = shift(tau, "yh", 1, 2)
    tau = lay(tau, core_swap(tau))
    arow, = move_call(
        functools.partial(choose_kernel, rows_here), "choose", [(cols_here // 2, aux)], 2, 1)(window_offsets, keep, got)
    up, down, far = (shift(arow, "z", s, 4) for s in (1, -1, 2))
    arow, = move_call(
        functools.partial(choose_z_kernel, rows_here), "choose_z", [(cols_here // 2, aux)], 4, 1)(
            window_offsets, arow, up, down, far)
    arow, tau, tau_h = lax.optimization_barrier((arow, tau, tau_h))

    side_tau = both_ways(tau, "z")
    tau_h = lay(tau_h, core_swap(tau_h))
    up, down, far = (shift_y(arow, s) for s in (1, -1, 2))
    near, = move_call(place_kernel, "place", [(2 * cols_here, aux)], 4, 4, False)(arow, up, down, far)
    near, tau_h, side_tau = lax.optimization_barrier((near, tau_h, side_tau))

    side_h = both_ways(tau_h, "z")
    near_c = core_swap(near)
    side = both_ways(near, "x")
    ints_near, = integrals_of(held, [near, near_c], (0,), "integrals_near")
    near_c, ints_near = lax.optimization_barrier((near_c, ints_near))
    side_c = both_ways(near_c, "x")
    far, side_h = lax.optimization_barrier((side, side_h))
    far = both_ways(far, "x")
    far_tau = both_ways(jnp.where(c == 0, side_tau, side_h), "z")
    pieces = [tau, tau_h, side_tau, core_swap(side_tau), side_h, core_swap(side_h)]
    ints_side, = integrals_of(
        held, [side, side_c, core_swap(side), core_swap(side_c)], (0, 1), "integrals_side")
    far, far_c, ints_side = lax.optimization_barrier((far, core_swap(far), ints_side))
    ints_far, = integrals_of(held, [far, far_c], (0,), "integrals_far")
    ints = [ints_near, ints_side, ints_far]
    partial = contract(ints, pieces, None)
    far_tau, partial = lax.optimization_barrier((far_tau, partial))
    partial = contract(ints, [far_tau, core_swap(far_tau)], partial)

    parts = lax.all_to_all(partial.reshape(128, 2 * rows_here), TILE + PAIR, split_axis=0, concat_axis=0, tiled=True)
    residual = parts.reshape(16, 8, 2, rows_here).sum(axis=1).transpose(1, 0, 2).reshape(1, 2, 16 * rows_here)
    occupied_sum = lookup(occupied_energy, pair_list[:, 0]) + lookup(occupied_energy, pair_list[:, 1])
    window_energy = lookup(virtual_energy, window_offsets)
    denominator = (
        window_energy[None, :, None] + virtual_energy[None, None, :] - occupied_sum[:, None, None]
    )
    return residual, residual / denominator


def solution(mesh):
    fine = Mesh(mesh.devices.reshape(4, 2, 4, 2, 2), PAIR + TILE)
    return jax.shard_map(
        local,
        mesh=fine,
        in_specs=(P(PAIR + TILE, None, None), P(TILE, PAIR, None), P(PAIR + TILE, None), P(), P(), P()),
        out_specs=(P(PAIR + TILE, None, None), P(PAIR + TILE, None, None)),
        check_vma=False,
    )
```

time: 569 us -> 124 us (0.22)
  waiting for transfers between devices: 423 us -> 33.1 us
  local copies, waits for them, and re-layouts: 76.3 us -> 11.7 us
  starting transfers between devices: 17.8 us -> 47.2 us
  Pallas kernels: 0 us -> 23.9 us
  matrix products: 21.6 us -> 0 us
  between operations: 20.1 us -> 2.23 us
    all_gather x2 -> x0, waiting for transfers between devices: 230 us -> none  [the longest x1 157 us: local(): columns = lax.all_gather(picked, 'pair', axis=1, tiled=True)]
    psum x1 -> x0, waiting for transfers between devices: 156 us -> none  [broadcast(): return lax.psum(jnp.where(mine, x, jnp.zeros_like(x)), axis)]
    ppermute x0 -> x24, starting transfers between devices: none -> 37 us  [the longest x15 24.3 us: shift(): return lax.ppermute(x, axis, [(i, (i + step) % size) for i in range(size)])]
    unnamed x5 -> x0, waiting for transfers between devices: 33 us -> none
    reshape x3 -> x2, local copies, waits for them, and re-layouts: 31.2 us -> 0.21 us  [local(): parts.reshape(16, 8, 2, rows_here).sum(axis=1).transpose(1, 0, 2)]
    pallas_call x0 -> x10, Pallas kernels: none -> 23.9 us  [the longest x3 11.6 us: integrals_of(): pl.pallas_call(first_kernel if load else functools.partial(next_kernel, f...]
    ppermute x0 -> x24, waiting for transfers between devices: none -> 22.7 us  [the longest x15 11.8 us: shift(): return lax.ppermute(x, axis, [(i, (i + step) % size) for i in range(size)])]
    dot_general x2 -> x0, matrix products: 21.6 us -> none  [the longest x1 14 us: local(): jnp.einsum('acq,bdq->abcd', arows, factors, preferred_element_type=jnp.fl...]
  transfers between devices with their start and end apart: 6 -> 26, of which waited for: 5 -> 13; matrix products, arithmetic and copies ran while one was open for 10% -> 5% of each run, Pallas kernels for 0% -> 17%
where the time goes in v2:
time: 124 us; the launch traced here: 123 us
  starting transfers between devices  47.2 us (38%)
  waiting for transfers between devices  33.1 us (27%)
  Pallas kernels  23.9 us (19%)
  local copies, waits for them, and re-layouts  11.7 us (9%)
  other arithmetic  5.23 us (4%)
  between operations  2.23 us (2%)
    ppermute x15, starting transfers between devices, shift(): return lax.ppermute(x, axis, [(i, (i + step) % size) for i in range(size)])  24.3 us
    ppermute x15, waiting for transfers between devices, shift(): return lax.ppermute(x, axis, [(i, (i + step) % size) for i in range(size)])  11.8 us
    pallas_call x3, Pallas kernels, integrals_of(): pl.pallas_call(first_kernel if load else functools.partial(next_kernel, f...  11.6 us
    unnamed x15, local copies, waits for them, and re-layouts  8.86 us
    ppermute x6, starting transfers between devices, both_ways(): return lax.ppermute(x, (axis, 'c'), pairs)  8.63 us
    pallas_call x2, Pallas kernels, contract(): pl.pallas_call(early_kernel if before is None else late_kernel, out_shape...  7.4 us
    all_to_all x1, waiting for transfers between devices, local(): lax.all_to_all(partial.reshape(128, 2 * rows_here), TILE + PAIR, split_ax...  6.37 us
    all_to_all x1, starting transfers between devices, local(): tau = lax.all_to_all(tau, PAIR, split_axis=0, concat_axis=0, tiled=True)  5.86 us
  transfers between devices with their start and end apart: 26, of which 13 were waited for; matrix products, arithmetic and copies ran while one was open for 5% of the time, Pallas kernels for 17%

profile of v2, /device:TPU:1, one launch (start us, length us, event | category | flops | bytes accessed | tf_op | source)
XLA Modules:
  0.0 123.4 jit_solution(10617485003471556777)
XLA Ops:
  0.6 2.1 %copy.20 = bf16[1,512,512]{1,2,0:T(8,128)(2,1)} copy(bf16[1,512,512]{2,1,0:T(8,128)(2,1)} %param.6) | data formatting | bytes 1048576 | tf_op args[0]
  2.7 5.9 %all-to-all-start = ((bf16[8,64,512]{2,1,0:T(8,128)(2,1)}), bf16[8,64,512]{2,1,0:T(8,128)(2,1)S(1)}, u32[]{:S(2)}, u32[]{:S(2)}) async-start(bf16[8,64,512]{2,1,0:T(8,128)(2,1)} %bitcast.2), calls=%async_computation | async-start | bytes 1048576 | tf_op jit(solution)/shard_map/all_to_all | solution.py:277
  13.3 3.9 %all-to-all-done = bf16[8,64,512]{2,1,0:T(8,128)(2,1)S(1)} async-done(((bf16[8,64,512]{2,1,0:T(8,128)(2,1)}), bf16[8,64,512]{2,1,0:T(8,128)(2,1)S(1)}, u32[]{:S(2)}, u32[]{:S(2)}) %all-to-all-start) | async-done | bytes 524320 | tf_op jit(solution)/shard_map/all_to_all | solution.py:277
  17.3 2.6 %collective-permute-start.1 = (bf16[32,2048]{1,0:T(8,128)(2,1)S(1)}, bf16[32,2048]{1,0:T(8,128)(2,1)S(1)}, u32[]{:S(2)}, u32[]{:S(2)}) collective-permute-start(bf16[32,2048]{1,0:T(8,128)(2,1)S(1)} %get-tuple-element.29), channel_id=1, source_target_pairs={{0,2},{2,0},{1,3},{3,1},{4,6},{6,4},{5,7},{7,5},{8,10},{10,8},{9,1... | collective-permute-start | bytes 393224 | tf_op jit(solution)/shard_map/ppermute | solution.py:17
  19.9 2.7 %collective-permute-done.1.got = bf16[32,2048]{1,0:T(8,128)(2,1)S(1)} collective-permute-done((bf16[32,2048]{1,0:T(8,128)(2,1)S(1)}, bf16[32,2048]{1,0:T(8,128)(2,1)S(1)}, u32[]{:S(2)}, u32[]{:S(2)}) %collective-permute-start.1) | collective-permute-done | bytes 131104 | tf_op jit(solution)/shard_map/ppermute | solution.py:17
  22.6 2.9 %collective-permute-start.5 = (bf16[8,64,512]{2,1,0:T(8,128)(2,1)S(1)}, bf16[8,64,512]{2,1,0:T(8,128)(2,1)S(1)}, u32[]{:S(2)}, u32[]{:S(2)}) collective-permute-start(bf16[8,64,512]{2,1,0:T(8,128)(2,1)S(1)} %all-to-all-done), channel_id=1, source_target_pairs={{0,1},{1,0},{2,3},{3,2},{4,5},{5,4},{6,7},{7,6},{8,9},{9,8},{10,11... | collective-permute-start | bytes 1572872 | tf_op jit(solution)/shard_map/ppermute | solution.py:17
  25.5 2.6 %collective-permute-start.6 = (bf16[8,64,512]{2,1,0:T(8,128)(2,1)S(1)}, bf16[8,64,512]{2,1,0:T(8,128)(2,1)S(1)}, u32[]{:S(2)}, u32[]{:S(2)}) collective-permute-start(bf16[8,64,512]{2,1,0:T(8,128)(2,1)S(1)} %all-to-all-done), channel_id=1, source_target_pairs={{0,2},{2,0},{1,3},{3,1},{4,6},{6,4},{5,7},{7,5},{8,10},{10,8},{9,1... | collective-permute-start | bytes 1572872 | tf_op jit(solution)/shard_map/ppermute | solution.py:17
  30.6 2.2 %collective-permute-start.3 = (bf16[32,2048]{1,0:T(8,128)(2,1)S(1)}, bf16[32,2048]{1,0:T(8,128)(2,1)S(1)}, u32[]{:S(2)}, u32[]{:S(2)}) collective-permute-start(bf16[32,2048]{1,0:T(8,128)(2,1)S(1)} %choose.1.own), channel_id=1, source_target_pairs={{0,12},{4,0},{8,4},{12,8},{1,13},{5,1},{9,5},{13,9},{2,14},{6,2},{... | collective-permute-start | bytes 393224 | tf_op jit(solution)/shard_map/ppermute | solution.py:17
  34.0 2.4 %collective-permute-done.2.up = bf16[32,2048]{1,0:T(8,128)(2,1)S(1)} collective-permute-done((bf16[32,2048]{1,0:T(8,128)(2,1)S(1)}, bf16[32,2048]{1,0:T(8,128)(2,1)S(1)}, u32[]{:S(2)}, u32[]{:S(2)}) %collective-permute-start.2) | collective-permute-done | bytes 131104 | tf_op jit(solution)/shard_map/ppermute | solution.py:17
  36.3 3.7 %collective-permute-done.4.far = bf16[32,2048]{1,0:T(8,128)(2,1)S(1)} collective-permute-done((bf16[32,2048]{1,0:T(8,128)(2,1)S(1)}, bf16[32,2048]{1,0:T(8,128)(2,1)S(1)}, u32[]{:S(2)}, u32[]{:S(2)}) %collective-permute-start.4) | collective-permute-done | bytes 131104 | tf_op jit(solution)/shard_map/ppermute | solution.py:17
  41.2 3.1 %collective-permute-start.11 = (bf16[128,4096]{1,0:T(8,128)(2,1)S(1)}, bf16[128,4096]{1,0:T(8,128)(2,1)S(1)}, u32[]{:S(2)}, u32[]{:S(2)}) collective-permute-start(bf16[128,4096]{1,0:T(8,128)(2,1)S(1)} %bitcast.21), channel_id=1, source_target_pairs={{0,4},{1,13},{4,8},{5,1},{8,12},{9,5},{12,0},{13,9},{2,6},{3,15},{... | collective-permute-start | bytes 3145736 | tf_op jit(solution)/shard_map/ppermute | solution.py:261
  50.1 3.9 %collective-permute-done.9.far = bf16[32,2048]{1,0:T(8,128)(2,1)S(1)} collective-permute-done((bf16[32,2048]{1,0:T(8,128)(2,1)S(1)}, bf16[32,2048]{1,0:T(8,128)(2,1)S(1)}, u32[]{:S(2)}, u32[]{:S(2)}) %collective-permute-start.9) | collective-permute-done | bytes 131104 | tf_op jit(solution)/shard_map/ppermute | solution.py:22
  56.2 2.2 %collective-permute-start.12 = (bf16[128,2048]{1,0:T(8,128)(2,1)}, bf16[128,2048]{1,0:T(8,128)(2,1)}, u32[]{:S(2)}, u32[]{:S(2)}) collective-permute-start(bf16[128,2048]{1,0:T(8,128)(2,1)} %place.1.refs_0_), channel_id=1, source_target_pairs={{0,1},{1,0},{2,3},{3,2},{4,5},{5,4},{6,7},{7,6},{8,9},{9,8},{10,11... | collective-permute-start | bytes 1572872 | tf_op jit(solution)/shard_map/ppermute | solution.py:17
  60.8 3.4 %copy-done = bf16[32,64,2048]{2,1,0:T(8,128)(2,1)S(1)} copy-done((bf16[32,64,2048]{2,1,0:T(8,128)(2,1)S(1)}, bf16[32,64,2048]{2,1,0:T(8,128)(2,1)}, u32[]{:S(2)}) %copy-start) | copy-done | bytes 8388632
  64.2 3.6 %integrals_near.1.refs_0_ = bf16[1,512,1024]{2,1,0:T(8,128)(2,1)S(1)} custom-call(bf16[32,64,2048]{2,1,0:T(8,128)(2,1)S(1)} %copy-done, bf16[128,2048]{1,0:T(8,128)(2,1)} %place.1.refs_0_, bf16[128,2048]{1,0:T(8,128)(2,1)} %collective-permute-done.12.refs_1_), custom_call_target="tpu_custom_call" | custom-call | flops 2147483648 | bytes 10485760 | tf_op jit(solution)/shard_map/integrals_near/pallas_call | solution.py:159
  69.2 3.5 %collective-permute-done.14.refs_7_ = bf16[128,4096]{1,0:T(8,128)(2,1)} collective-permute-done((bf16[128,4096]{1,0:T(8,128)(2,1)}, bf16[128,4096]{1,0:T(8,128)(2,1)}, u32[]{:S(2)}, u32[]{:S(2)}) %collective-permute-start.14) | collective-permute-done | bytes 1048608 | tf_op jit(solution)/shard_map/ppermute | solution.py:261
  81.9 3.3 %collective-permute-start.16 = (bf16[128,2048]{1,0:T(8,128)(2,1)S(1)}, bf16[128,2048]{1,0:T(8,128)(2,1)S(1)}, u32[]{:S(2)}, u32[]{:S(2)}) collective-permute-start(bf16[128,2048]{1,0:T(8,128)(2,1)S(1)} %collective-permute-done.15.refs_0_), channel_id=1, source_target_pairs={{0,1},{1,0},{2,3},{3,2},{4,5},{5,4},{6,7},{7,6},{8,9},{9,8},{10,11... | collective-permute-start | bytes 1572872 | tf_op jit(solution)/shard_map/ppermute | solution.py:17
  85.3 3.4 %copy-done.1 = bf16[32,64,2048]{2,1,0:T(8,128)(2,1)S(1)} copy-done((bf16[32,64,2048]{2,1,0:T(8,128)(2,1)S(1)}, bf16[32,64,2048]{2,1,0:T(8,128)(2,1)}, u32[]{:S(2)}) %copy-start.1) | copy-done | bytes 8388632
  88.7 5.7 %integrals_side.1.refs_1_ = bf16[2,512,1024]{2,1,0:T(8,128)(2,1)S(1)} custom-call(bf16[32,64,2048]{2,1,0:T(8,128)(2,1)S(1)} %copy-done.1, bf16[128,2048]{1,0:T(8,128)(2,1)} %collective-permute-done.13.refs_0_, bf16[128,2048]{1,0:T(8,128)(2,1)} %collective-permute-done.17.refs_1_, bf16[128,2048]{1,0:T(8,128)(2,1)S(1)} %collective-permute-done.18.refs_2_, ...), custom_call_target="tpu_custom_call" | custom-call | flops 4294967296 | bytes 10485760 | tf_op jit(solution)/shard_map/integrals_side/pallas_call | solution.py:159
  94.4 2.4 %integrals_far.1.refs_2_ = bf16[1,512,1024]{2,1,0:T(8,128)(2,1)S(1)} custom-call(bf16[32,64,2048]{2,1,0:T(8,128)(2,1)S(1)} %copy-done.1, bf16[128,2048]{1,0:T(8,128)(2,1)S(1)} %collective-permute-done.15.refs_0_, bf16[128,2048]{1,0:T(8,128)(2,1)S(1)} %collective-permute-done.16.refs_1_), custom_call_target="tpu_custom_call" | custom-call | flops 2147483648 | bytes 10485760 | tf_op jit(solution)/shard_map/integrals_far/pallas_call | solution.py:159
  96.8 5.0 %contract_early.1.refs_5_ = f32[3,2,512,128]{3,2,1,0:T(8,128)S(1)} custom-call(bf16[1,512,1024]{2,1,0:T(8,128)(2,1)S(1)} %integrals_near.1.refs_0_, bf16[2,512,1024]{2,1,0:T(8,128)(2,1)S(1)} %integrals_side.1.refs_1_, bf16[1,512,1024]{2,1,0:T(8,128)(2,1)S(1)} %integrals_far.1.refs_2_, bf16[128,4096]{1,0:T(8,128)(2,1)S(1)} %bitcast.22, ...), custom_call_target="tpu_custom_call" | custom-call | flops 3221225472 | bytes 8388608 | tf_op jit(solution)/shard_map/contract_early/pallas_call | solution.py:242
  104.6 2.4 %contract_late.1 = f32[16,8,64]{2,1,0:T(8,128)} custom-call(bf16[1,512,1024]{2,1,0:T(8,128)(2,1)S(1)} %integrals_near.1.refs_0_, bf16[2,512,1024]{2,1,0:T(8,128)(2,1)S(1)} %integrals_side.1.refs_1_, bf16[1,512,1024]{2,1,0:T(8,128)(2,1)S(1)} %integrals_far.1.refs_2_, bf16[128,4096]{1,0:T(8,128)(2,1)S(1)} %collective-permute-done.20.refs_3_, ...), custom_call_target="tpu_custom_call" | custom-call | flops 1073741824 | bytes 8388608 | tf_op jit(solution)/shard_map/contract_late/pallas_call | solution.py:242
  107.0 4.4 %all-to-all-start.1 = ((f32[128,1,64]{2,1,0:T(1,128)}), f32[128,1,64]{2,1,0:T(1,128)S(1)}, u32[]{:S(2)}, u32[]{:S(2)}) async-start(f32[128,1,64]{2,1,0:T(1,128)} %bitcast.12), calls=%async_computation.1 | async-start | bytes 131072 | tf_op jit(solution)/shard_map/all_to_all | solution.py:323
  114.7 6.4 %all-to-all-done.1 = f32[128,1,64]{2,1,0:T(1,128)S(1)} async-done(((f32[128,1,64]{2,1,0:T(1,128)}), f32[128,1,64]{2,1,0:T(1,128)S(1)}, u32[]{:S(2)}, u32[]{:S(2)}) %all-to-all-start.1) | async-done | bytes 32800 | tf_op jit(solution)/shard_map/all_to_all | solution.py:323
  (68 shorter events, 37.7 us)
Async XLA Ops:
  2.7 14.6 %all-to-all-start = ((bf16[8,64,512]{2,1,0:T(8,128)(2,1)}), bf16[8,64,512]{2,1,0:T(8,128)(2,1)S(1)}, u32[]{:S(2)}, u32[]{:S(2)}) async-start(bf16[8,64,512]{2,1,0:T(8,128)(2,1)} %bitcast.2), calls=%async_computation | async-start | bytes 1048576 | tf_op jit(solution)/shard_map/all_to_all | solution.py:277
  17.3 5.3 %collective-permute-start.1 = (bf16[32,2048]{1,0:T(8,128)(2,1)S(1)}, bf16[32,2048]{1,0:T(8,128)(2,1)S(1)}, u32[]{:S(2)}, u32[]{:S(2)}) collective-permute-start(bf16[32,2048]{1,0:T(8,128)(2,1)S(1)} %get-tuple-element.29), channel_id=1, source_target_pairs={{0,2},{2,0},{1,3},{3,1},{4,6},{6,4},{5,7},{7,5},{8,10},{10,8},{9,1... | collective-permute-start | bytes 393224 | tf_op jit(solution)/shard_map/ppermute | solution.py:17
  22.6 18.2 %collective-permute-start.5 = (bf16[8,64,512]{2,1,0:T(8,128)(2,1)S(1)}, bf16[8,64,512]{2,1,0:T(8,128)(2,1)S(1)}, u32[]{:S(2)}, u32[]{:S(2)}) collective-permute-start(bf16[8,64,512]{2,1,0:T(8,128)(2,1)S(1)} %all-to-all-done), channel_id=1, source_target_pairs={{0,1},{1,0},{2,3},{3,2},{4,5},{5,4},{6,7},{7,6},{8,9},{9,8},{10,11... | collective-permute-start | bytes 1572872 | tf_op jit(solution)/shard_map/ppermute | solution.py:17
  25.5 15.7 %collective-permute-start.6 = (bf16[8,64,512]{2,1,0:T(8,128)(2,1)S(1)}, bf16[8,64,512]{2,1,0:T(8,128)(2,1)S(1)}, u32[]{:S(2)}, u32[]{:S(2)}) collective-permute-start(bf16[8,64,512]{2,1,0:T(8,128)(2,1)S(1)} %all-to-all-done), channel_id=1, source_target_pairs={{0,2},{2,0},{1,3},{3,1},{4,6},{6,4},{5,7},{7,5},{8,10},{10,8},{9,1... | collective-permute-start | bytes 1572872 | tf_op jit(solution)/shard_map/ppermute | solution.py:17
  28.8 7.5 %collective-permute-start.2 = (bf16[32,2048]{1,0:T(8,128)(2,1)S(1)}, bf16[32,2048]{1,0:T(8,128)(2,1)S(1)}, u32[]{:S(2)}, u32[]{:S(2)}) collective-permute-start(bf16[32,2048]{1,0:T(8,128)(2,1)S(1)} %choose.1.own), channel_id=1, source_target_pairs={{0,4},{4,8},{8,12},{12,0},{1,5},{5,9},{9,13},{13,1},{2,6},{6,10},{... | collective-permute-start | bytes 393224 | tf_op jit(solution)/shard_map/ppermute | solution.py:17
  30.6 5.8 %collective-permute-start.3 = (bf16[32,2048]{1,0:T(8,128)(2,1)S(1)}, bf16[32,2048]{1,0:T(8,128)(2,1)S(1)}, u32[]{:S(2)}, u32[]{:S(2)}) collective-permute-start(bf16[32,2048]{1,0:T(8,128)(2,1)S(1)} %choose.1.own), channel_id=1, source_target_pairs={{0,12},{4,0},{8,4},{12,8},{1,13},{5,1},{9,5},{13,9},{2,14},{6,2},{... | collective-permute-start | bytes 393224 | tf_op jit(solution)/shard_map/ppermute | solution.py:17
  32.8 7.3 %collective-permute-start.4 = (bf16[32,2048]{1,0:T(8,128)(2,1)S(1)}, bf16[32,2048]{1,0:T(8,128)(2,1)S(1)}, u32[]{:S(2)}, u32[]{:S(2)}) collective-permute-start(bf16[32,2048]{1,0:T(8,128)(2,1)S(1)} %choose.1.own), channel_id=1, source_target_pairs={{0,8},{4,12},{8,0},{12,4},{1,9},{5,13},{9,1},{13,5},{2,10},{6,14},... | collective-permute-start | bytes 393224 | tf_op jit(solution)/shard_map/ppermute | solution.py:17
  41.2 15.0 %collective-permute-start.11 = (bf16[128,4096]{1,0:T(8,128)(2,1)S(1)}, bf16[128,4096]{1,0:T(8,128)(2,1)S(1)}, u32[]{:S(2)}, u32[]{:S(2)}) collective-permute-start(bf16[128,4096]{1,0:T(8,128)(2,1)S(1)} %bitcast.21), channel_id=1, source_target_pairs={{0,4},{1,13},{4,8},{5,1},{8,12},{9,5},{12,0},{13,9},{2,6},{3,15},{... | collective-permute-start | bytes 3145736 | tf_op jit(solution)/shard_map/ppermute | solution.py:261
  44.3 10.5 %collective-permute-start.10 = (bf16[8,64,512]{2,1,0:T(8,128)(2,1)S(1)}, bf16[8,64,512]{2,1,0:T(8,128)(2,1)S(1)}, u32[]{:S(2)}, u32[]{:S(2)}) collective-permute-start(bf16[8,64,512]{2,1,0:T(8,128)(2,1)S(1)} %collective-permute-done.6), channel_id=1, source_target_pairs={{0,1},{1,0},{2,3},{3,2},{4,5},{5,4},{6,7},{7,6},{8,9},{9,8},{10,11... | collective-permute-start | bytes 1572872 | tf_op jit(solution)/shard_map/ppermute | solution.py:17
  44.3 5.8 %collective-permute-start.7 = (bf16[32,2048]{1,0:T(8,128)(2,1)S(1)}, bf16[32,2048]{1,0:T(8,128)(2,1)S(1)}, u32[]{:S(2)}, u32[]{:S(2)}) collective-permute-start(bf16[32,2048]{1,0:T(8,128)(2,1)S(1)} %choose_z.1.own), channel_id=1, source_target_pairs={{0,16},{16,2},{2,18},{18,0},{1,17},{17,3},{3,19},{19,1},{4,20},{20... | collective-permute-start | bytes 393224 | tf_op jit(solution)/shard_map/ppermute | solution.py:22
  45.5 4.6 %collective-permute-start.8 = (bf16[32,2048]{1,0:T(8,128)(2,1)S(1)}, bf16[32,2048]{1,0:T(8,128)(2,1)S(1)}, u32[]{:S(2)}, u32[]{:S(2)}) collective-permute-start(bf16[32,2048]{1,0:T(8,128)(2,1)S(1)} %choose_z.1.own), channel_id=1, source_target_pairs={{0,18},{16,0},{2,16},{18,2},{1,19},{17,1},{3,17},{19,3},{4,22},{20... | collective-permute-start | bytes 393224 | tf_op jit(solution)/shard_map/ppermute | solution.py:22
  47.0 7.0 %collective-permute-start.9 = (bf16[32,2048]{1,0:T(8,128)(2,1)S(1)}, bf16[32,2048]{1,0:T(8,128)(2,1)S(1)}, u32[]{:S(2)}, u32[]{:S(2)}) collective-permute-start(bf16[32,2048]{1,0:T(8,128)(2,1)S(1)} %choose_z.1.own), channel_id=1, source_target_pairs={{0,2},{16,18},{2,0},{18,16},{1,3},{17,19},{3,1},{19,17},{4,6},{20,... | collective-permute-start | bytes 393224 | tf_op jit(solution)/shard_map/ppermute | solution.py:22
  56.2 4.6 %collective-permute-start.12 = (bf16[128,2048]{1,0:T(8,128)(2,1)}, bf16[128,2048]{1,0:T(8,128)(2,1)}, u32[]{:S(2)}, u32[]{:S(2)}) collective-permute-start(bf16[128,2048]{1,0:T(8,128)(2,1)} %place.1.refs_0_), channel_id=1, source_target_pairs={{0,1},{1,0},{2,3},{3,2},{4,5},{5,4},{6,7},{7,6},{8,9},{9,8},{10,11... | collective-permute-start | bytes 1572872 | tf_op jit(solution)/shard_map/ppermute | solution.py:17
  58.4 14.3 %collective-permute-start.14 = (bf16[128,4096]{1,0:T(8,128)(2,1)}, bf16[128,4096]{1,0:T(8,128)(2,1)}, u32[]{:S(2)}, u32[]{:S(2)}) collective-permute-start(bf16[128,4096]{1,0:T(8,128)(2,1)} %bitcast.10.refs_4_), channel_id=1, source_target_pairs={{0,4},{1,13},{4,8},{5,1},{8,12},{9,5},{12,0},{13,9},{2,6},{3,15},{... | collective-permute-start | bytes 3145736 | tf_op jit(solution)/shard_map/ppermute | solution.py:261
  59.9 8.6 %collective-permute-start.13 = (bf16[128,2048]{1,0:T(8,128)(2,1)}, bf16[128,2048]{1,0:T(8,128)(2,1)}, u32[]{:S(2)}, u32[]{:S(2)}) collective-permute-start(bf16[128,2048]{1,0:T(8,128)(2,1)} %place.1.refs_0_), channel_id=1, source_target_pairs={{0,32},{1,97},{32,64},{33,1},{64,96},{65,33},{96,0},{97,65},{2,34}... | collective-permute-start | bytes 1572872 | tf_op jit(solution)/shard_map/ppermute | solution.py:261
  67.7 8.7 %collective-permute-start.17 = (bf16[128,2048]{1,0:T(8,128)(2,1)}, bf16[128,2048]{1,0:T(8,128)(2,1)}, u32[]{:S(2)}, u32[]{:S(2)}) collective-permute-start(bf16[128,2048]{1,0:T(8,128)(2,1)} %collective-permute-done.12.refs_1_), channel_id=1, source_target_pairs={{0,32},{1,97},{32,64},{33,1},{64,96},{65,33},{96,0},{97,65},{2,34}... | collective-permute-start | bytes 1572872 | tf_op jit(solution)/shard_map/ppermute | solution.py:261
  68.4 28.5 %collective-permute-start.21 = (bf16[128,4096]{1,0:T(8,128)(2,1)S(1)}, bf16[128,4096]{1,0:T(8,128)(2,1)S(1)}, u32[]{:S(2)}, u32[]{:S(2)}) collective-permute-start(bf16[128,4096]{1,0:T(8,128)(2,1)S(1)} %collective-permute-done.11.refs_5_), channel_id=1, source_target_pairs={{0,1},{1,0},{2,3},{3,2},{4,5},{5,4},{6,7},{7,6},{8,9},{9,8},{10,11... | collective-permute-start | bytes 3145736 | tf_op jit(solution)/shard_map/ppermute | solution.py:17
  68.5 11.2 %collective-permute-start.18 = (bf16[128,2048]{1,0:T(8,128)(2,1)}, bf16[128,2048]{1,0:T(8,128)(2,1)S(1)}, u32[]{:S(2)}, u32[]{:S(2)}) collective-permute-start(bf16[128,2048]{1,0:T(8,128)(2,1)} %collective-permute-done.13.refs_0_), channel_id=1, source_target_pairs={{0,1},{1,0},{2,3},{3,2},{4,5},{5,4},{6,7},{7,6},{8,9},{9,8},{10,11... | collective-permute-start | bytes 1572872 | tf_op jit(solution)/shard_map/ppermute | solution.py:17
  72.6 9.3 %collective-permute-start.15 = (bf16[128,2048]{1,0:T(8,128)(2,1)}, bf16[128,2048]{1,0:T(8,128)(2,1)S(1)}, u32[]{:S(2)}, u32[]{:S(2)}) collective-permute-start(bf16[128,2048]{1,0:T(8,128)(2,1)} %collective-permute-done.13.refs_0_), channel_id=1, source_target_pairs={{0,32},{1,97},{32,64},{33,1},{64,96},{65,33},{96,0},{97,65},{2,34}... | collective-permute-start | bytes 1572872 | tf_op jit(solution)/shard_map/ppermute | solution.py:261
  73.5 23.3 %collective-permute-start.22 = (bf16[128,4096]{1,0:T(8,128)(2,1)}, bf16[128,4096]{1,0:T(8,128)(2,1)S(1)}, u32[]{:S(2)}, u32[]{:S(2)}) collective-permute-start(bf16[128,4096]{1,0:T(8,128)(2,1)} %collective-permute-done.14.refs_7_), channel_id=1, source_target_pairs={{0,1},{1,0},{2,3},{3,2},{4,5},{5,4},{6,7},{7,6},{8,9},{9,8},{10,11... | collective-permute-start | bytes 3145736 | tf_op jit(solution)/shard_map/ppermute | solution.py:17
  76.4 8.9 %collective-permute-start.19 = (bf16[128,2048]{1,0:T(8,128)(2,1)}, bf16[128,2048]{1,0:T(8,128)(2,1)S(1)}, u32[]{:S(2)}, u32[]{:S(2)}) collective-permute-start(bf16[128,2048]{1,0:T(8,128)(2,1)} %collective-permute-done.17.refs_1_), channel_id=1, source_target_pairs={{0,1},{1,0},{2,3},{3,2},{4,5},{5,4},{6,7},{7,6},{8,9},{9,8},{10,11... | collective-permute-start | bytes 1572872 | tf_op jit(solution)/shard_map/ppermute | solution.py:17
  79.7 22.1 %collective-permute-start.20 = (bf16[128,4096]{1,0:T(8,128)(2,1)S(1)}, bf16[128,4096]{1,0:T(8,128)(2,1)S(1)}, u32[]{:S(2)}, u32[]{:S(2)}) collective-permute-start(bf16[128,4096]{1,0:T(8,128)(2,1)S(1)} %broadcast_select_fusion), channel_id=1, source_target_pairs={{0,4},{1,13},{4,8},{5,1},{8,12},{9,5},{12,0},{13,9},{2,6},{3,15},{... | collective-permute-start | bytes 3145736 | tf_op jit(solution)/shard_map/ppermute | solution.py:261
  81.9 12.5 %collective-permute-start.16 = (bf16[128,2048]{1,0:T(8,128)(2,1)S(1)}, bf16[128,2048]{1,0:T(8,128)(2,1)S(1)}, u32[]{:S(2)}, u32[]{:S(2)}) collective-permute-start(bf16[128,2048]{1,0:T(8,128)(2,1)S(1)} %collective-permute-done.15.refs_0_), channel_id=1, source_target_pairs={{0,1},{1,0},{2,3},{3,2},{4,5},{5,4},{6,7},{7,6},{8,9},{9,8},{10,11... | collective-permute-start | bytes 1572872 | tf_op jit(solution)/shard_map/ppermute | solution.py:17
  107.0 14.1 %all-to-all-start.1 = ((f32[128,1,64]{2,1,0:T(1,128)}), f32[128,1,64]{2,1,0:T(1,128)S(1)}, u32[]{:S(2)}, u32[]{:S(2)}) async-start(f32[128,1,64]{2,1,0:T(1,128)} %bitcast.12), calls=%async_computation.1 | async-start | bytes 131072 | tf_op jit(solution)/shard_map/all_to_all | solution.py:323
  (9 other events, 39.9 us)

commit v3 on v2

--- a/solution.py
+++ b/solution.py
@@ -20,11 +20,6 @@
 def shift_y(x, step):
     at = [y % 2 * 2 + y // 2 for y in range(4)]
     return lax.ppermute(x, ("yl", "yh"), [(at[y], at[(y + step) % 4]) for y in range(4)])
-
-
-def lookup(table, indices):
-    positions = jnp.arange(table.shape[0], dtype=jnp.int32)
-    return jnp.sum(jnp.where(positions[None, :] == indices[:, None], table[None, :], 0.0), axis=1)
 
 
 def pick_kernel(rows, offsets, factors, mine, other, sem):
@@ -78,6 +73,38 @@
             copy = pltpu.make_async_copy(source, out, sem.at[0])
             copy.start()
             copy.wait()
+
+
+def lay_kernel(first, second, out):
+    count, depth, width = first.shape
+    wide = depth // DB * LANES
+    for half, piece in enumerate((first, second)):
+        for i in range(count):
+            row = (half * count + i) * DB
+            for d in range(depth // DB):
+                block = piece[i, d * DB:(d + 1) * DB, :]
+                for n in range(width // LANES):
+                    at = n * wide + d * LANES
+                    out[row:row + DB, at:at + LANES] = block[:, n * LANES:(n + 1) * LANES]
+
+
+def lay(first, second):
+    count, depth, width = first.shape
+    return pl.pallas_call(
+        lay_kernel,
+        out_shape=jax.ShapeDtypeStruct((2 * count * DB, depth // DB * width), jnp.bfloat16),
+        in_specs=[IN_VMEM] * 2,
+        out_specs=IN_VMEM,
+        compiler_params=pltpu.CompilerParams(vmem_limit_bytes=4 << 20),
+        cost_estimate=pl.CostEstimate(flops=0, bytes_accessed=2 << 20, transcendentals=0),
+        name="lay",
+    )(first, second)
+
+
+def take_kernel(source, out, sem):
+    copy = pltpu.make_async_copy(source.at[pl.ds(0, out.shape[0]), :], out, sem.at[0])
+    copy.start()
+    copy.wait()
 
 
 def place_kernel(own, up, down, far, out, sem):
@@ -174,11 +201,12 @@
     ahead = jnp.where(c == 0, 3, 1)
     chunk = (x, (x + ahead) % 4, (x + 4 - ahead) % 4, (x + 2) % 4)
     where_int = [(i, n) for i in ints for n in range(i.shape[0])]
+    each = len(pieces) // groups
     for g in range(groups):
         total = None
         for (ref, inner), at in zip(where_int, chunk):
             at = pl.ds(pl.multiple_of(at * wide, wide), wide)
-            side = jnp.concatenate([pieces[2 * g][:, at], pieces[2 * g + 1][:, at]], axis=0)
+            side = jnp.concatenate([p[:, at] for p in pieces[each * g:each * (g + 1)]], axis=0)
             value = lax.dot_general(ref[inner], side, (((1,), (1,)), ((), ())), preferred_element_type=jnp.float32)
             total = value if total is None else total + value
         yield total
@@ -186,7 +214,7 @@
 
 def early_kernel(*refs):
     ints, pieces, out = refs[:3], refs[3:-1], refs[-1]
-    for g, total in enumerate(products(ints, pieces, len(pieces) // 2)):
+    for g, total in enumerate(products(ints, pieces, out.shape[0])):
         for n in range(total.shape[1] // LANES):
             out[g, n] = total[:, n * LANES:(n + 1) * LANES]
 
@@ -201,7 +229,7 @@
         (z, h, here), (z, 1 - h, here),
         ((z + ahead) % 4, h, here), ((z + 4 - ahead) % 4, h, away),
         ((z + ahead) % 4, 1 - h, here), ((z + 4 - ahead) % 4, 1 - h, away),
-        ((z + 2) % 4, (h + c) % 2, here), ((z + 2) % 4, (h + 1 - c) % 2, away),
+        ((z + 2) % 4, h, here), ((z + 2) % 4, 1 - h, here),
     )
     groups, parts, rows, _ = before.shape
     depth = parts * LANES
@@ -232,8 +260,8 @@
 
 
 def contract(ints, pieces, before):
-    rows, depth = ints[0].shape[1], 2 * pieces[0].shape[0]
-    groups = len(pieces) // 2
+    rows, depth = ints[0].shape[1], 256
+    groups = sum(p.shape[0] for p in pieces) // depth
     if before is None:
         out_shape = jax.ShapeDtypeStruct((groups, depth // LANES, rows, LANES), jnp.float32)
     else:
@@ -252,6 +280,18 @@
     )(*given)
 
 
+def finish_kernel(pairs, offsets, occupied, virtual, parts, energies, residual, update):
+    count, width = parts.shape
+    total = parts[...].reshape(16, count // 16, width).sum(axis=1)
+    wide = width // 2
+    occupied_sum = occupied[pairs[0, 0]] + occupied[pairs[0, 1]]
+    every = energies[...].reshape(1, energies.shape[0])
+    for k in range(2):
+        row = jnp.concatenate([total[n:n + 1, k * wide:(k + 1) * wide] for n in range(16)], axis=1)
+        residual[0, k:k + 1, :] = row
+        update[0, k:k + 1, :] = row / (virtual[offsets[k]] + every - occupied_sum)
+
+
 def core_swap(x):
     return shift(x, "c", 1, 2)
 
@@ -268,10 +308,6 @@
     c = lax.axis_index("c")
     held = pltpu.with_memory_space_constraint(factors, pltpu.VMEM)
     factors = pltpu.with_memory_space_constraint(factors, pltpu.HBM)
-
-    def lay(first, second):
-        both = jnp.stack([first, second]).reshape(2, 8, n_d, DB, 4, LANES)
-        return both.transpose(0, 1, 3, 4, 2, 5).reshape(2 * 8 * DB, n_d * virt)
 
     tau = amplitudes[0].T.reshape(8, cols_here, virt)
     tau = lax.all_to_all(tau, PAIR, split_axis=0, concat_axis=0, tiled=True)
@@ -281,14 +317,13 @@
     keep, send = move_call(
         functools.partial(halve_kernel, rows_here), "halve", [(cols_here // 2, aux)] * 2, 2, 2)(
             window_offsets, mine, swapped)
-    send, tau = lax.optimization_barrier((send, tau))
 
     got = shift(send, "yh", 1, 2)
-    got, tau = lax.optimization_barrier((got, tau))
+    arow, = move_call(
+        functools.partial(choose_kernel, rows_here), "choose", [(cols_here // 2, aux)], 2, 1)(window_offsets, keep, got)
+    arow, tau = lax.optimization_barrier((arow, tau))
     tau_h = shift(tau, "yh", 1, 2)
     tau = lay(tau, core_swap(tau))
-    arow, = move_call(
-        functools.partial(choose_kernel, rows_here), "choose", [(cols_here // 2, aux)], 2, 1)(window_offsets, keep, got)
     up, down, far = (shift(arow, "z", s, 4) for s in (1, -1, 2))
     arow, = move_call(
         functools.partial(choose_z_kernel, rows_here), "choose_z", [(cols_here // 2, aux)], 4, 1)(
@@ -304,30 +339,35 @@
     side_h = both_ways(tau_h, "z")
     near_c = core_swap(near)
     side = both_ways(near, "x")
+    take = move_call(take_kernel, "take", [(tau.shape[0] // 2, tau.shape[1])], 1, 1, False)
+    far_tau = both_ways(take(side_tau)[0], "z")
     ints_near, = integrals_of(held, [near, near_c], (0,), "integrals_near")
     near_c, ints_near = lax.optimization_barrier((near_c, ints_near))
     side_c = both_ways(near_c, "x")
-    far, side_h = lax.optimization_barrier((side, side_h))
-    far = both_ways(far, "x")
-    far_tau = both_ways(jnp.where(c == 0, side_tau, side_h), "z")
-    pieces = [tau, tau_h, side_tau, core_swap(side_tau), side_h, core_swap(side_h)]
+    far = both_ways(side, "x")
+    held, side_h, far_tau = lax.optimization_barrier((held, side_h, far_tau))
+    far_h = both_ways(take(side_h)[0], "z")
     ints_side, = integrals_of(
         held, [side, side_c, core_swap(side), core_swap(side_c)], (0, 1), "integrals_side")
     far, far_c, ints_side = lax.optimization_barrier((far, core_swap(far), ints_side))
     ints_far, = integrals_of(held, [far, far_c], (0,), "integrals_far")
     ints = [ints_near, ints_side, ints_far]
+    pieces = [tau, tau_h, side_tau, core_swap(side_tau), side_h, core_swap(side_h)]
     partial = contract(ints, pieces, None)
-    far_tau, partial = lax.optimization_barrier((far_tau, partial))
-    partial = contract(ints, [far_tau, core_swap(far_tau)], partial)
+
+    far_h, partial = lax.optimization_barrier((far_h, partial))
+    partial = contract(ints, [far_tau, core_swap(far_tau), far_h, core_swap(far_h)], partial)
 
     parts = lax.all_to_all(partial.reshape(128, 2 * rows_here), TILE + PAIR, split_axis=0, concat_axis=0, tiled=True)
-    residual = parts.reshape(16, 8, 2, rows_here).sum(axis=1).transpose(1, 0, 2).reshape(1, 2, 16 * rows_here)
-    occupied_sum = lookup(occupied_energy, pair_list[:, 0]) + lookup(occupied_energy, pair_list[:, 1])
-    window_energy = lookup(virtual_energy, window_offsets)
-    denominator = (
-        window_energy[None, :, None] + virtual_energy[None, None, :] - occupied_sum[:, None, None]
-    )
-    return residual, residual / denominator
+    residual, update = pl.pallas_call(
+        finish_kernel,
+        out_shape=[jax.ShapeDtypeStruct((1, 2, 16 * rows_here), jnp.float32)] * 2,
+        in_specs=[SMALL] * 4 + [IN_VMEM] * 2,
+        out_specs=[IN_VMEM] * 2,
+        compiler_params=pltpu.CompilerParams(vmem_limit_bytes=1 << 20),
+        name="finish",
+    )(pair_list, window_offsets, occupied_energy, virtual_energy, parts, virtual_energy)
+    return residual, update
 
 
 def solution(mesh):

time: 124 us -> 113 us (0.911)
  blocking collectives: 0 us -> 14.7 us
  starting transfers between devices: 47.2 us -> 40.2 us
  local copies, waits for them, and re-layouts: 11.7 us -> 5.46 us
  other arithmetic: 5.23 us -> 0 us
  Pallas kernels: 23.9 us -> 20.9 us
  waiting for transfers between devices: 33.1 us -> 30.2 us
  between operations: 2.23 us -> 0.86 us
    all_to_all x0 -> x1, blocking collectives: none -> 14.7 us  [local(): lax.all_to_all(partial.reshape(128, 2 * rows_here), TILE + PAIR, split_ax...]
    ppermute x15 -> x16, starting transfers between devices: 24.3 us -> 16.6 us  [shift(): return lax.ppermute(x, axis, [(i, (i + step) % size) for i in range(size)])]
    all_to_all x1 -> x0, waiting for transfers between devices: 6.37 us -> none  [local(): lax.all_to_all(partial.reshape(128, 2 * rows_here), TILE + PAIR, split_ax...]
    ppermute x6 -> x7, starting transfers between devices: 8.63 us -> 14.4 us  [both_ways(): return lax.ppermute(x, (axis, 'c'), pairs)]
    unnamed x15 -> x10, local copies, waits for them, and re-layouts: 8.86 us -> 3.41 us
    all_to_all x1 -> x0, starting transfers between devices: 4.39 us -> none  [local(): lax.all_to_all(partial.reshape(128, 2 * rows_here), TILE + PAIR, split_ax...]
    ppermute x6 -> x7, waiting for transfers between devices: 5.38 us -> 9.54 us  [both_ways(): return lax.ppermute(x, (axis, 'c'), pairs)]
    all_to_all x1, waiting for transfers between devices: 3.95 us -> 0.01 us  [local(): tau = lax.all_to_all(tau, PAIR, split_axis=0, concat_axis=0, tiled=True)]
  transfers between devices with their start and end apart: 26 -> 27, of which waited for: 13 -> 13; matrix products, arithmetic and copies ran while one was open for 5% -> 0% of each run, Pallas kernels for 17% -> 16%
where the time goes in v3:
time: 113 us; the launch traced here: 112 us
  starting transfers between devices  40.2 us (36%)
  waiting for transfers between devices  30.2 us (27%)
  Pallas kernels  20.9 us (18%)
  blocking collectives  14.7 us (13%)
  local copies, waits for them, and re-layouts  5.46 us (5%)
    ppermute x16, starting transfers between devices, shift(): return lax.ppermute(x, axis, [(i, (i + step) % size) for i in range(size)])  16.6 us
    ppermute x16, waiting for transfers between devices, shift(): return lax.ppermute(x, axis, [(i, (i + step) % size) for i in range(size)])  14.9 us
    all_to_all x1, blocking collectives, local(): lax.all_to_all(partial.reshape(128, 2 * rows_here), TILE + PAIR, split_ax...  14.7 us
    ppermute x7, starting transfers between devices, both_ways(): return lax.ppermute(x, (axis, 'c'), pairs)  14.4 us
    ppermute x7, waiting for transfers between devices, both_ways(): return lax.ppermute(x, (axis, 'c'), pairs)  9.54 us
    pallas_call x3, Pallas kernels, integrals_of(): pl.pallas_call(first_kernel if load else functools.partial(next_kernel, f...  9.25 us
    all_to_all x1, starting transfers between devices, local(): tau = lax.all_to_all(tau, PAIR, split_axis=0, concat_axis=0, tiled=True)  5.86 us
    ppermute x3, waiting for transfers between devices, shift_y(): lax.ppermute(x, ('yl', 'yh'), [(at[y], at[(y + step) % 4]) for y in range...  5.81 us
  transfers between devices with their start and end apart: 27, of which 13 were waited for; matrix products, arithmetic and copies ran while one was open for 0% of the time, Pallas kernels for 16%

profile of v3, /device:TPU:1, one launch (start us, length us, event | category | flops | bytes accessed | tf_op | source)
XLA Modules:
  0.0 112.3 jit_solution(1851377194376356088)
XLA Ops:
  0.6 2.1 %copy.9 = bf16[512,512]{1,0:T(8,128)(2,1)} copy(bf16[512,512]{0,1:T(8,128)(2,1)} %bitcast.10) | data formatting | bytes 1048576 | tf_op jit(solution)/shard_map/transpose | solution.py:312
  2.7 5.9 %all-to-all-start = ((bf16[8,64,512]{2,1,0:T(8,128)(2,1)}), bf16[8,64,512]{2,1,0:T(8,128)(2,1)S(1)}, u32[]{:S(2)}, u32[]{:S(2)}) async-start(bf16[8,64,512]{2,1,0:T(8,128)(2,1)} %bitcast.2), calls=%async_computation | async-start | bytes 1048576 | tf_op jit(solution)/shard_map/all_to_all | solution.py:313
  13.3 2.7 %collective-permute-start.1 = (bf16[32,2048]{1,0:T(8,128)(2,1)S(1)}, bf16[32,2048]{1,0:T(8,128)(2,1)S(1)}, u32[]{:S(2)}, u32[]{:S(2)}) collective-permute-start(bf16[32,2048]{1,0:T(8,128)(2,1)S(1)} %get-tuple-element.27), channel_id=1, source_target_pairs={{0,2},{2,0},{1,3},{3,1},{4,6},{6,4},{5,7},{7,5},{8,10},{10,8},{9,1... | collective-permute-start | bytes 393224 | tf_op jit(solution)/shard_map/ppermute | solution.py:17
  16.0 5.1 %collective-permute-done.1.got = bf16[32,2048]{1,0:T(8,128)(2,1)S(1)} collective-permute-done((bf16[32,2048]{1,0:T(8,128)(2,1)S(1)}, bf16[32,2048]{1,0:T(8,128)(2,1)S(1)}, u32[]{:S(2)}, u32[]{:S(2)}) %collective-permute-start.1) | collective-permute-done | bytes 131104 | tf_op jit(solution)/shard_map/ppermute | solution.py:17
  22.7 1.9 %collective-permute-start.6 = (bf16[8,64,512]{2,1,0:T(8,128)(2,1)S(1)}, bf16[8,64,512]{2,1,0:T(8,128)(2,1)S(1)}, u32[]{:S(2)}, u32[]{:S(2)}) collective-permute-start(bf16[8,64,512]{2,1,0:T(8,128)(2,1)S(1)} %all-to-all-done.first), channel_id=1, source_target_pairs={{0,2},{2,0},{1,3},{3,1},{4,6},{6,4},{5,7},{7,5},{8,10},{10,8},{9,1... | collective-permute-start | bytes 1572872 | tf_op jit(solution)/shard_map/ppermute | solution.py:17
  26.3 2.1 %collective-permute-start.3 = (bf16[32,2048]{1,0:T(8,128)(2,1)S(1)}, bf16[32,2048]{1,0:T(8,128)(2,1)S(1)}, u32[]{:S(2)}, u32[]{:S(2)}) collective-permute-start(bf16[32,2048]{1,0:T(8,128)(2,1)S(1)} %choose.1.own), channel_id=1, source_target_pairs={{0,12},{4,0},{8,4},{12,8},{1,13},{5,1},{9,5},{13,9},{2,14},{6,2},{... | collective-permute-start | bytes 393224 | tf_op jit(solution)/shard_map/ppermute | solution.py:17
  29.7 2.3 %collective-permute-done.2.up = bf16[32,2048]{1,0:T(8,128)(2,1)S(1)} collective-permute-done((bf16[32,2048]{1,0:T(8,128)(2,1)S(1)}, bf16[32,2048]{1,0:T(8,128)(2,1)S(1)}, u32[]{:S(2)}, u32[]{:S(2)}) %collective-permute-start.2) | collective-permute-done | bytes 131104 | tf_op jit(solution)/shard_map/ppermute | solution.py:17
  32.0 3.7 %collective-permute-done.4.far = bf16[32,2048]{1,0:T(8,128)(2,1)S(1)} collective-permute-done((bf16[32,2048]{1,0:T(8,128)(2,1)S(1)}, bf16[32,2048]{1,0:T(8,128)(2,1)S(1)}, u32[]{:S(2)}, u32[]{:S(2)}) %collective-permute-start.4) | collective-permute-done | bytes 131104 | tf_op jit(solution)/shard_map/ppermute | solution.py:17
  37.7 3.8 %collective-permute-start.11 = (bf16[128,4096]{1,0:T(8,128)(2,1)S(1)}, bf16[128,4096]{1,0:T(8,128)(2,1)S(1)}, u32[]{:S(2)}, u32[]{:S(2)}) collective-permute-start(bf16[128,4096]{1,0:T(8,128)(2,1)S(1)} %lay.2.refs_3_), channel_id=1, source_target_pairs={{0,4},{1,13},{4,8},{5,1},{8,12},{9,5},{12,0},{13,9},{2,6},{3,15},{... | collective-permute-start | bytes 3145736 | tf_op jit(solution)/shard_map/ppermute | solution.py:301
  44.9 2.4 %collective-permute-done.7.up = bf16[32,2048]{1,0:T(8,128)(2,1)S(1)} collective-permute-done((bf16[32,2048]{1,0:T(8,128)(2,1)S(1)}, bf16[32,2048]{1,0:T(8,128)(2,1)S(1)}, u32[]{:S(2)}, u32[]{:S(2)}) %collective-permute-start.7) | collective-permute-done | bytes 131104 | tf_op jit(solution)/shard_map/ppermute | solution.py:22
  47.3 3.4 %collective-permute-done.9.far = bf16[32,2048]{1,0:T(8,128)(2,1)S(1)} collective-permute-done((bf16[32,2048]{1,0:T(8,128)(2,1)S(1)}, bf16[32,2048]{1,0:T(8,128)(2,1)S(1)}, u32[]{:S(2)}, u32[]{:S(2)}) %collective-permute-start.9) | collective-permute-done | bytes 131104 | tf_op jit(solution)/shard_map/ppermute | solution.py:22
  53.2 2.2 %collective-permute-start.12 = (bf16[128,2048]{1,0:T(8,128)(2,1)S(1)}, bf16[128,2048]{1,0:T(8,128)(2,1)S(1)}, u32[]{:S(2)}, u32[]{:S(2)}) collective-permute-start(bf16[128,2048]{1,0:T(8,128)(2,1)S(1)} %place.1.refs_0_), channel_id=1, source_target_pairs={{0,1},{1,0},{2,3},{3,2},{4,5},{5,4},{6,7},{7,6},{8,9},{9,8},{10,11... | collective-permute-start | bytes 1572872 | tf_op jit(solution)/shard_map/ppermute | solution.py:17
  57.1 2.4 %collective-permute-start.13 = (bf16[128,2048]{1,0:T(8,128)(2,1)S(1)}, bf16[128,2048]{1,0:T(8,128)(2,1)S(1)}, u32[]{:S(2)}, u32[]{:S(2)}) collective-permute-start(bf16[128,2048]{1,0:T(8,128)(2,1)S(1)} %place.1.refs_0_), channel_id=1, source_target_pairs={{0,32},{1,97},{32,64},{33,1},{64,96},{65,33},{96,0},{97,65},{2,34}... | collective-permute-start | bytes 1572872 | tf_op jit(solution)/shard_map/ppermute | solution.py:301
  59.6 3.4 %copy-done = bf16[32,64,2048]{2,1,0:T(8,128)(2,1)S(1)} copy-done((bf16[32,64,2048]{2,1,0:T(8,128)(2,1)S(1)}, bf16[32,64,2048]{2,1,0:T(8,128)(2,1)}, u32[]{:S(2)}) %copy-start) | copy-done | bytes 8388632
  63.0 2.4 %integrals_near.1.refs_0_ = bf16[1,512,1024]{2,1,0:T(8,128)(2,1)S(1)} custom-call(bf16[32,64,2048]{2,1,0:T(8,128)(2,1)S(1)} %copy-done, bf16[128,2048]{1,0:T(8,128)(2,1)S(1)} %place.1.refs_0_, bf16[128,2048]{1,0:T(8,128)(2,1)S(1)} %collective-permute-done.12.refs_1_), custom_call_target="tpu_custom_call" | custom-call | flops 2147483648 | bytes 10485760 | tf_op jit(solution)/shard_map/integrals_near/pallas_call | solution.py:186
  67.0 2.1 %collective-permute-start.14 = (bf16[128,2048]{1,0:T(8,128)(2,1)S(1)}, bf16[128,2048]{1,0:T(8,128)(2,1)S(1)}, u32[]{:S(2)}, u32[]{:S(2)}) collective-permute-start(bf16[128,2048]{1,0:T(8,128)(2,1)S(1)} %collective-permute-done.13.refs_0_), channel_id=1, source_target_pairs={{0,32},{1,97},{32,64},{33,1},{64,96},{65,33},{96,0},{97,65},{2,34}... | collective-permute-start | bytes 1572872 | tf_op jit(solution)/shard_map/ppermute | solution.py:301
  69.1 4.6 %collective-permute-done.18.refs_1_ = bf16[128,2048]{1,0:T(8,128)(2,1)S(1)} collective-permute-done((bf16[128,2048]{1,0:T(8,128)(2,1)S(1)}, bf16[128,2048]{1,0:T(8,128)(2,1)S(1)}, u32[]{:S(2)}, u32[]{:S(2)}) %collective-permute-start.18) | collective-permute-done | bytes 524320 | tf_op jit(solution)/shard_map/ppermute | solution.py:301
  75.0 2.1 %collective-permute-start.23 = (bf16[128,4096]{1,0:T(8,128)(2,1)S(1)}, bf16[128,4096]{1,0:T(8,128)(2,1)S(1)}, u32[]{:S(2)}, u32[]{:S(2)}) collective-permute-start(bf16[128,4096]{1,0:T(8,128)(2,1)S(1)} %collective-permute-done.11.source.refs_5_), channel_id=1, source_target_pairs={{0,1},{1,0},{2,3},{3,2},{4,5},{5,4},{6,7},{7,6},{8,9},{9,8},{10,11... | collective-permute-start | bytes 3145736 | tf_op jit(solution)/shard_map/ppermute | solution.py:17
  77.0 2.0 %collective-permute-done.14.refs_0_ = bf16[128,2048]{1,0:T(8,128)(2,1)S(1)} collective-permute-done((bf16[128,2048]{1,0:T(8,128)(2,1)S(1)}, bf16[128,2048]{1,0:T(8,128)(2,1)S(1)}, u32[]{:S(2)}, u32[]{:S(2)}) %collective-permute-start.14) | collective-permute-done | bytes 524320 | tf_op jit(solution)/shard_map/ppermute | solution.py:301
  79.2 2.8 %collective-permute-start.22 = (bf16[64,4096]{1,0:T(8,128)(2,1)S(1)}, bf16[64,4096]{1,0:T(8,128)(2,1)S(1)}, u32[]{:S(2)}, u32[]{:S(2)}) collective-permute-start(bf16[64,4096]{1,0:T(8,128)(2,1)S(1)} %take.3), channel_id=1, source_target_pairs={{0,4},{1,13},{4,8},{5,1},{8,12},{9,5},{12,0},{13,9},{2,6},{3,15},{... | collective-permute-start | bytes 1572872 | tf_op jit(solution)/shard_map/ppermute | solution.py:301
  82.0 4.5 %integrals_side.1.refs_1_ = bf16[2,512,1024]{2,1,0:T(8,128)(2,1)S(1)} custom-call(bf16[32,64,2048]{2,1,0:T(8,128)(2,1)S(1)} %copy-done, bf16[128,2048]{1,0:T(8,128)(2,1)S(1)} %collective-permute-done.13.refs_0_, bf16[128,2048]{1,0:T(8,128)(2,1)S(1)} %collective-permute-done.18.refs_1_, bf16[128,2048]{1,0:T(8,128)(2,1)S(1)} %collective-permute-done.19.refs_2_, ...), custom_call_target="tpu_custom_call" | custom-call | flops 4294967296 | bytes 10485760 | tf_op jit(solution)/shard_map/integrals_side/pallas_call | solution.py:186
  86.5 2.4 %integrals_far.1.refs_2_ = bf16[1,512,1024]{2,1,0:T(8,128)(2,1)S(1)} custom-call(bf16[32,64,2048]{2,1,0:T(8,128)(2,1)S(1)} %copy-done, bf16[128,2048]{1,0:T(8,128)(2,1)S(1)} %collective-permute-done.14.refs_0_, bf16[128,2048]{1,0:T(8,128)(2,1)S(1)} %collective-permute-done.15.refs_1_), custom_call_target="tpu_custom_call" | custom-call | flops 2147483648 | bytes 10485760 | tf_op jit(solution)/shard_map/integrals_far/pallas_call | solution.py:186
  88.9 3.5 %contract_early.1.refs_7_ = f32[3,2,512,128]{3,2,1,0:T(8,128)S(1)} custom-call(bf16[1,512,1024]{2,1,0:T(8,128)(2,1)S(1)} %integrals_near.1.refs_0_, bf16[2,512,1024]{2,1,0:T(8,128)(2,1)S(1)} %integrals_side.1.refs_1_, bf16[1,512,1024]{2,1,0:T(8,128)(2,1)S(1)} %integrals_far.1.refs_2_, bf16[128,4096]{1,0:T(8,128)(2,1)S(1)} %lay.2.refs_3_, ...), custom_call_target="tpu_custom_call" | custom-call | flops 3221225472 | bytes 8388608 | tf_op jit(solution)/shard_map/contract_early/pallas_call | solution.py:270
  96.3 14.7 %all_to_all.16 = f32[128,1,64]{2,1,0:T(1,128)S(1)} all-to-all(f32[128,1,64]{2,1,0:T(1,128)S(1)} %bitcast.8), channel_id=1, replica_groups=mesh['x'=4,'yl'=2,'z'=4,'yh'=2,'c'=2] {'z','yh','c','x','yl'}, dimensions={0} | all-to-all | bytes 65536 | tf_op jit(solution)/shard_map/all_to_all | solution.py:361
  (57 shorter events, 27.4 us)
Async XLA Ops:
  2.7 19.1 %all-to-all-start = ((bf16[8,64,512]{2,1,0:T(8,128)(2,1)}), bf16[8,64,512]{2,1,0:T(8,128)(2,1)S(1)}, u32[]{:S(2)}, u32[]{:S(2)}) async-start(bf16[8,64,512]{2,1,0:T(8,128)(2,1)} %bitcast.2), calls=%async_computation | async-start | bytes 1048576 | tf_op jit(solution)/shard_map/all_to_all | solution.py:313
  13.3 7.8 %collective-permute-start.1 = (bf16[32,2048]{1,0:T(8,128)(2,1)S(1)}, bf16[32,2048]{1,0:T(8,128)(2,1)S(1)}, u32[]{:S(2)}, u32[]{:S(2)}) collective-permute-start(bf16[32,2048]{1,0:T(8,128)(2,1)S(1)} %get-tuple-element.27), channel_id=1, source_target_pairs={{0,2},{2,0},{1,3},{3,1},{4,6},{6,4},{5,7},{7,5},{8,10},{10,8},{9,1... | collective-permute-start | bytes 393224 | tf_op jit(solution)/shard_map/ppermute | solution.py:17
  21.8 14.6 %collective-permute-start.5 = (bf16[8,64,512]{2,1,0:T(8,128)(2,1)S(1)}, bf16[8,64,512]{2,1,0:T(8,128)(2,1)S(1)}, u32[]{:S(2)}, u32[]{:S(2)}) collective-permute-start(bf16[8,64,512]{2,1,0:T(8,128)(2,1)S(1)} %all-to-all-done.first), channel_id=1, source_target_pairs={{0,1},{1,0},{2,3},{3,2},{4,5},{5,4},{6,7},{7,6},{8,9},{9,8},{10,11... | collective-permute-start | bytes 1572872 | tf_op jit(solution)/shard_map/ppermute | solution.py:17
  22.7 15.0 %collective-permute-start.6 = (bf16[8,64,512]{2,1,0:T(8,128)(2,1)S(1)}, bf16[8,64,512]{2,1,0:T(8,128)(2,1)S(1)}, u32[]{:S(2)}, u32[]{:S(2)}) collective-permute-start(bf16[8,64,512]{2,1,0:T(8,128)(2,1)S(1)} %all-to-all-done.first), channel_id=1, source_target_pairs={{0,2},{2,0},{1,3},{3,1},{4,6},{6,4},{5,7},{7,5},{8,10},{10,8},{9,1... | collective-permute-start | bytes 1572872 | tf_op jit(solution)/shard_map/ppermute | solution.py:17
  24.6 7.3 %collective-permute-start.2 = (bf16[32,2048]{1,0:T(8,128)(2,1)S(1)}, bf16[32,2048]{1,0:T(8,128)(2,1)S(1)}, u32[]{:S(2)}, u32[]{:S(2)}) collective-permute-start(bf16[32,2048]{1,0:T(8,128)(2,1)S(1)} %choose.1.own), channel_id=1, source_target_pairs={{0,4},{4,8},{8,12},{12,0},{1,5},{5,9},{9,13},{13,1},{2,6},{6,10},{... | collective-permute-start | bytes 393224 | tf_op jit(solution)/shard_map/ppermute | solution.py:17
  26.3 5.7 %collective-permute-start.3 = (bf16[32,2048]{1,0:T(8,128)(2,1)S(1)}, bf16[32,2048]{1,0:T(8,128)(2,1)S(1)}, u32[]{:S(2)}, u32[]{:S(2)}) collective-permute-start(bf16[32,2048]{1,0:T(8,128)(2,1)S(1)} %choose.1.own), channel_id=1, source_target_pairs={{0,12},{4,0},{8,4},{12,8},{1,13},{5,1},{9,5},{13,9},{2,14},{6,2},{... | collective-permute-start | bytes 393224 | tf_op jit(solution)/shard_map/ppermute | solution.py:17
  28.4 7.2 %collective-permute-start.4 = (bf16[32,2048]{1,0:T(8,128)(2,1)S(1)}, bf16[32,2048]{1,0:T(8,128)(2,1)S(1)}, u32[]{:S(2)}, u32[]{:S(2)}) collective-permute-start(bf16[32,2048]{1,0:T(8,128)(2,1)S(1)} %choose.1.own), channel_id=1, source_target_pairs={{0,8},{4,12},{8,0},{12,4},{1,9},{5,13},{9,1},{13,5},{2,10},{6,14},... | collective-permute-start | bytes 393224 | tf_op jit(solution)/shard_map/ppermute | solution.py:17
  37.7 15.5 %collective-permute-start.11 = (bf16[128,4096]{1,0:T(8,128)(2,1)S(1)}, bf16[128,4096]{1,0:T(8,128)(2,1)S(1)}, u32[]{:S(2)}, u32[]{:S(2)}) collective-permute-start(bf16[128,4096]{1,0:T(8,128)(2,1)S(1)} %lay.2.refs_3_), channel_id=1, source_target_pairs={{0,4},{1,13},{4,8},{5,1},{8,12},{9,5},{12,0},{13,9},{2,6},{3,15},{... | collective-permute-start | bytes 3145736 | tf_op jit(solution)/shard_map/ppermute | solution.py:301
  41.5 9.9 %collective-permute-start.10 = (bf16[8,64,512]{2,1,0:T(8,128)(2,1)S(1)}, bf16[8,64,512]{2,1,0:T(8,128)(2,1)S(1)}, u32[]{:S(2)}, u32[]{:S(2)}) collective-permute-start(bf16[8,64,512]{2,1,0:T(8,128)(2,1)S(1)} %collective-permute-done.6.first), channel_id=1, source_target_pairs={{0,1},{1,0},{2,3},{3,2},{4,5},{5,4},{6,7},{7,6},{8,9},{9,8},{10,11... | collective-permute-start | bytes 1572872 | tf_op jit(solution)/shard_map/ppermute | solution.py:17
  41.5 5.8 %collective-permute-start.7 = (bf16[32,2048]{1,0:T(8,128)(2,1)S(1)}, bf16[32,2048]{1,0:T(8,128)(2,1)S(1)}, u32[]{:S(2)}, u32[]{:S(2)}) collective-permute-start(bf16[32,2048]{1,0:T(8,128)(2,1)S(1)} %choose_z.1.own), channel_id=1, source_target_pairs={{0,16},{16,2},{2,18},{18,0},{1,17},{17,3},{3,19},{19,1},{4,20},{20... | collective-permute-start | bytes 393224 | tf_op jit(solution)/shard_map/ppermute | solution.py:22
  44.2 6.5 %collective-permute-start.9 = (bf16[32,2048]{1,0:T(8,128)(2,1)S(1)}, bf16[32,2048]{1,0:T(8,128)(2,1)S(1)}, u32[]{:S(2)}, u32[]{:S(2)}) collective-permute-start(bf16[32,2048]{1,0:T(8,128)(2,1)S(1)} %choose_z.1.own), channel_id=1, source_target_pairs={{0,2},{16,18},{2,0},{18,16},{1,3},{17,19},{3,1},{19,17},{4,6},{20,... | collective-permute-start | bytes 393224 | tf_op jit(solution)/shard_map/ppermute | solution.py:22
  53.2 6.4 %collective-permute-start.12 = (bf16[128,2048]{1,0:T(8,128)(2,1)S(1)}, bf16[128,2048]{1,0:T(8,128)(2,1)S(1)}, u32[]{:S(2)}, u32[]{:S(2)}) collective-permute-start(bf16[128,2048]{1,0:T(8,128)(2,1)S(1)} %place.1.refs_0_), channel_id=1, source_target_pairs={{0,1},{1,0},{2,3},{3,2},{4,5},{5,4},{6,7},{7,6},{8,9},{9,8},{10,11... | collective-permute-start | bytes 1572872 | tf_op jit(solution)/shard_map/ppermute | solution.py:17
  55.4 21.6 %collective-permute-start.16 = (bf16[128,4096]{1,0:T(8,128)(2,1)S(1)}, bf16[128,4096]{1,0:T(8,128)(2,1)S(1)}, u32[]{:S(2)}, u32[]{:S(2)}) collective-permute-start(bf16[128,4096]{1,0:T(8,128)(2,1)S(1)} %lay.3.refs_4_), channel_id=1, source_target_pairs={{0,4},{1,13},{4,8},{5,1},{8,12},{9,5},{12,0},{13,9},{2,6},{3,15},{... | collective-permute-start | bytes 3145736 | tf_op jit(solution)/shard_map/ppermute | solution.py:301
  57.1 9.9 %collective-permute-start.13 = (bf16[128,2048]{1,0:T(8,128)(2,1)S(1)}, bf16[128,2048]{1,0:T(8,128)(2,1)S(1)}, u32[]{:S(2)}, u32[]{:S(2)}) collective-permute-start(bf16[128,2048]{1,0:T(8,128)(2,1)S(1)} %place.1.refs_0_), channel_id=1, source_target_pairs={{0,32},{1,97},{32,64},{33,1},{64,96},{65,33},{96,0},{97,65},{2,34}... | collective-permute-start | bytes 1572872 | tf_op jit(solution)/shard_map/ppermute | solution.py:301
  65.3 8.4 %collective-permute-start.18 = (bf16[128,2048]{1,0:T(8,128)(2,1)S(1)}, bf16[128,2048]{1,0:T(8,128)(2,1)S(1)}, u32[]{:S(2)}, u32[]{:S(2)}) collective-permute-start(bf16[128,2048]{1,0:T(8,128)(2,1)S(1)} %collective-permute-done.12.refs_1_), channel_id=1, source_target_pairs={{0,32},{1,97},{32,64},{33,1},{64,96},{65,33},{96,0},{97,65},{2,34}... | collective-permute-start | bytes 1572872 | tf_op jit(solution)/shard_map/ppermute | solution.py:301
  65.8 9.1 %collective-permute-start.17 = (bf16[64,4096]{1,0:T(8,128)(2,1)S(1)}, bf16[64,4096]{1,0:T(8,128)(2,1)S(1)}, u32[]{:S(2)}, u32[]{:S(2)}) collective-permute-start(bf16[64,4096]{1,0:T(8,128)(2,1)S(1)} %take.2), channel_id=1, source_target_pairs={{0,4},{1,13},{4,8},{5,1},{8,12},{9,5},{12,0},{13,9},{2,6},{3,15},{... | collective-permute-start | bytes 1572872 | tf_op jit(solution)/shard_map/ppermute | solution.py:301
  67.0 12.0 %collective-permute-start.14 = (bf16[128,2048]{1,0:T(8,128)(2,1)S(1)}, bf16[128,2048]{1,0:T(8,128)(2,1)S(1)}, u32[]{:S(2)}, u32[]{:S(2)}) collective-permute-start(bf16[128,2048]{1,0:T(8,128)(2,1)S(1)} %collective-permute-done.13.refs_0_), channel_id=1, source_target_pairs={{0,32},{1,97},{32,64},{33,1},{64,96},{65,33},{96,0},{97,65},{2,34}... | collective-permute-start | bytes 1572872 | tf_op jit(solution)/shard_map/ppermute | solution.py:301
  69.1 10.1 %collective-permute-start.19 = (bf16[128,2048]{1,0:T(8,128)(2,1)S(1)}, bf16[128,2048]{1,0:T(8,128)(2,1)S(1)}, u32[]{:S(2)}, u32[]{:S(2)}) collective-permute-start(bf16[128,2048]{1,0:T(8,128)(2,1)S(1)} %collective-permute-done.13.refs_0_), channel_id=1, source_target_pairs={{0,1},{1,0},{2,3},{3,2},{4,5},{5,4},{6,7},{7,6},{8,9},{9,8},{10,11... | collective-permute-start | bytes 1572872 | tf_op jit(solution)/shard_map/ppermute | solution.py:17
  73.7 8.2 %collective-permute-start.20 = (bf16[128,2048]{1,0:T(8,128)(2,1)S(1)}, bf16[128,2048]{1,0:T(8,128)(2,1)S(1)}, u32[]{:S(2)}, u32[]{:S(2)}) collective-permute-start(bf16[128,2048]{1,0:T(8,128)(2,1)S(1)} %collective-permute-done.18.refs_1_), channel_id=1, source_target_pairs={{0,1},{1,0},{2,3},{3,2},{4,5},{5,4},{6,7},{7,6},{8,9},{9,8},{10,11... | collective-permute-start | bytes 1572872 | tf_op jit(solution)/shard_map/ppermute | solution.py:17
  75.0 13.9 %collective-permute-start.23 = (bf16[128,4096]{1,0:T(8,128)(2,1)S(1)}, bf16[128,4096]{1,0:T(8,128)(2,1)S(1)}, u32[]{:S(2)}, u32[]{:S(2)}) collective-permute-start(bf16[128,4096]{1,0:T(8,128)(2,1)S(1)} %collective-permute-done.11.source.refs_5_), channel_id=1, source_target_pairs={{0,1},{1,0},{2,3},{3,2},{4,5},{5,4},{6,7},{7,6},{8,9},{9,8},{10,11... | collective-permute-start | bytes 3145736 | tf_op jit(solution)/shard_map/ppermute | solution.py:17
  77.0 11.9 %collective-permute-start.24 = (bf16[128,4096]{1,0:T(8,128)(2,1)S(1)}, bf16[128,4096]{1,0:T(8,128)(2,1)S(1)}, u32[]{:S(2)}, u32[]{:S(2)}) collective-permute-start(bf16[128,4096]{1,0:T(8,128)(2,1)S(1)} %collective-permute-done.16.source.refs_7_), channel_id=1, source_target_pairs={{0,1},{1,0},{2,3},{3,2},{4,5},{5,4},{6,7},{7,6},{8,9},{9,8},{10,11... | collective-permute-start | bytes 3145736 | tf_op jit(solution)/shard_map/ppermute | solution.py:17
  79.1 7.5 %collective-permute-start.15 = (bf16[128,2048]{1,0:T(8,128)(2,1)S(1)}, bf16[128,2048]{1,0:T(8,128)(2,1)S(1)}, u32[]{:S(2)}, u32[]{:S(2)}) collective-permute-start(bf16[128,2048]{1,0:T(8,128)(2,1)S(1)} %collective-permute-done.14.refs_0_), channel_id=1, source_target_pairs={{0,1},{1,0},{2,3},{3,2},{4,5},{5,4},{6,7},{7,6},{8,9},{9,8},{10,11... | collective-permute-start | bytes 1572872 | tf_op jit(solution)/shard_map/ppermute | solution.py:17
  79.2 13.2 %collective-permute-start.22 = (bf16[64,4096]{1,0:T(8,128)(2,1)S(1)}, bf16[64,4096]{1,0:T(8,128)(2,1)S(1)}, u32[]{:S(2)}, u32[]{:S(2)}) collective-permute-start(bf16[64,4096]{1,0:T(8,128)(2,1)S(1)} %take.3), channel_id=1, source_target_pairs={{0,4},{1,13},{4,8},{5,1},{8,12},{9,5},{12,0},{13,9},{2,6},{3,15},{... | collective-permute-start | bytes 1572872 | tf_op jit(solution)/shard_map/ppermute | solution.py:301
  82.0 11.0 %collective-permute-start.21 = (bf16[64,4096]{1,0:T(8,128)(2,1)S(1)}, bf16[64,4096]{1,0:T(8,128)(2,1)S(1)}, u32[]{:S(2)}, u32[]{:S(2)}) collective-permute-start(bf16[64,4096]{1,0:T(8,128)(2,1)S(1)} %collective-permute-done.17.refs_3_), channel_id=1, source_target_pairs={{0,1},{1,0},{2,3},{3,2},{4,5},{5,4},{6,7},{7,6},{8,9},{9,8},{10,11... | collective-permute-start | bytes 1572872 | tf_op jit(solution)/shard_map/ppermute | solution.py:17
  (8 other events, 75.8 us)

commit v4 on v3

--- a/solution.py
+++ b/solution.py
@@ -105,6 +105,25 @@
     copy = pltpu.make_async_copy(source.at[pl.ds(0, out.shape[0]), :], out, sem.at[0])
     copy.start()
     copy.wait()
+
+
+def hold_kernel(source, out, sem):
+    copy = pltpu.make_async_copy(source, out, sem.at[0])
+    copy.start()
+    copy.wait()
+
+
+def hold(factors):
+    return pl.pallas_call(
+        hold_kernel,
+        out_shape=jax.ShapeDtypeStruct(factors.shape, factors.dtype),
+        in_specs=[IN_HBM],
+        out_specs=IN_VMEM,
+        scratch_shapes=[pltpu.SemaphoreType.DMA((1,))],
+        compiler_params=pltpu.CompilerParams(vmem_limit_bytes=1 << 20),
+        cost_estimate=pl.CostEstimate(flops=0, bytes_accessed=16 << 20, transcendentals=0),
+        name="hold",
+    )(factors)
 
 
 def place_kernel(own, up, down, far, out, sem):
@@ -195,26 +214,25 @@
     )(factors, *pieces)
 
 
-def products(ints, pieces, groups):
+def products(ints, chunks, pieces):
     x, c = lax.axis_index("x"), lax.axis_index("c")
     wide = ints[0].shape[2]
     ahead = jnp.where(c == 0, 3, 1)
     chunk = (x, (x + ahead) % 4, (x + 4 - ahead) % 4, (x + 2) % 4)
     where_int = [(i, n) for i in ints for n in range(i.shape[0])]
-    each = len(pieces) // groups
-    for g in range(groups):
-        total = None
-        for (ref, inner), at in zip(where_int, chunk):
-            at = pl.ds(pl.multiple_of(at * wide, wide), wide)
-            side = jnp.concatenate([p[:, at] for p in pieces[each * g:each * (g + 1)]], axis=0)
-            value = lax.dot_general(ref[inner], side, (((1,), (1,)), ((), ())), preferred_element_type=jnp.float32)
-            total = value if total is None else total + value
-        yield total
+    total = None
+    for (ref, inner), at in zip(where_int, chunks):
+        at = pl.ds(pl.multiple_of(chunk[at] * wide, wide), wide)
+        side = jnp.concatenate([p[:, at] for p in pieces], axis=0)
+        value = lax.dot_general(ref[inner], side, (((1,), (1,)), ((), ())), preferred_element_type=jnp.float32)
+        total = value if total is None else total + value
+    return total
 
 
 def early_kernel(*refs):
-    ints, pieces, out = refs[:3], refs[3:-1], refs[-1]
-    for g, total in enumerate(products(ints, pieces, out.shape[0])):
+    ints, pieces, out = refs[:2], refs[2:-1], refs[-1]
+    for g in range(out.shape[0]):
+        total = products(ints, (0, 1, 2), pieces[2 * g:2 * g + 2])
         for n in range(total.shape[1] // LANES):
             out[g, n] = total[:, n * LANES:(n + 1) * LANES]
 
@@ -233,9 +251,14 @@
     )
     groups, parts, rows, _ = before.shape
     depth = parts * LANES
-    for total in products(ints, pieces, 1):
+    for g in range(groups + 1):
+        if g < groups:
+            total = products(ints[2:], (3,), pieces[2 * g:2 * g + 2])
+        else:
+            total = products(ints, (0, 1, 2, 3), pieces[2 * groups:])
         for n in range(parts):
-            spare[n] = total[:, n * LANES:(n + 1) * LANES]
+            value = total[:, n * LANES:(n + 1) * LANES]
+            spare[g, n] = value + before[g, n] if g < groups else value
     small = rows // DB
     folds = depth // DB
     fold = (lax.broadcasted_iota(jnp.int32, (folds, depth), 1) // DB
@@ -244,7 +267,7 @@
     for g in range(groups + 1):
         columns = []
         for n in range(parts):
-            source = before.at[g, n] if g < groups else spare.at[n]
+            source = spare.at[g, n]
             total = source[pl.ds(0, small, stride=DB), :]
             for d in range(1, DB):
                 total = jnp.where(lane == d, source[pl.ds(d, small, stride=DB), :], total)
@@ -262,8 +285,9 @@
 def contract(ints, pieces, before):
     rows, depth = ints[0].shape[1], 256
     groups = sum(p.shape[0] for p in pieces) // depth
+    kept = jax.ShapeDtypeStruct((groups, depth // LANES, rows, LANES), jnp.float32)
     if before is None:
-        out_shape = jax.ShapeDtypeStruct((groups, depth // LANES, rows, LANES), jnp.float32)
+        out_shape = kept
     else:
         out_shape = jax.ShapeDtypeStruct((16, 8, rows // DB), jnp.float32)
     given = list(ints) + list(pieces) + ([] if before is None else [before])
@@ -272,10 +296,10 @@
         out_shape=out_shape,
         in_specs=[IN_VMEM] * len(given),
         out_specs=IN_VMEM,
-        scratch_shapes=[] if before is None else [pltpu.VMEM((depth // LANES, rows, LANES), jnp.float32)],
+        scratch_shapes=[] if before is None else [pltpu.VMEM(kept.shape, kept.dtype)],
         compiler_params=pltpu.CompilerParams(vmem_limit_bytes=12 << 20),
         cost_estimate=pl.CostEstimate(
-            flops=2 * rows * depth * 4096 * groups, bytes_accessed=8 << 20, transcendentals=0),
+            flops=2 * rows * depth * 1024 * (9 if before is None else 7), bytes_accessed=8 << 20, transcendentals=0),
         name="contract_early" if before is None else "contract_late",
     )(*given)
 
@@ -306,7 +330,6 @@
     virt = amplitudes.shape[1]
     n_d = cols_here // DB
     c = lax.axis_index("c")
-    held = pltpu.with_memory_space_constraint(factors, pltpu.VMEM)
     factors = pltpu.with_memory_space_constraint(factors, pltpu.HBM)
 
     tau = amplitudes[0].T.reshape(8, cols_here, virt)
@@ -324,39 +347,39 @@
     arow, tau = lax.optimization_barrier((arow, tau))
     tau_h = shift(tau, "yh", 1, 2)
     tau = lay(tau, core_swap(tau))
+    arow, factors = lax.optimization_barrier((arow, factors))
+    held = hold(factors)
     up, down, far = (shift(arow, "z", s, 4) for s in (1, -1, 2))
     arow, = move_call(
         functools.partial(choose_z_kernel, rows_here), "choose_z", [(cols_here // 2, aux)], 4, 1)(
             window_offsets, arow, up, down, far)
-    arow, tau, tau_h = lax.optimization_barrier((arow, tau, tau_h))
+    arow, tau, tau_h, held = lax.optimization_barrier((arow, tau, tau_h, held))
 
     side_tau = both_ways(tau, "z")
     tau_h = lay(tau_h, core_swap(tau_h))
+    side_h = both_ways(tau_h, "z")
     up, down, far = (shift_y(arow, s) for s in (1, -1, 2))
     near, = move_call(place_kernel, "place", [(2 * cols_here, aux)], 4, 4, False)(arow, up, down, far)
-    near, tau_h, side_tau = lax.optimization_barrier((near, tau_h, side_tau))
-
-    side_h = both_ways(tau_h, "z")
+    near, tau_h = lax.optimization_barrier((near, tau_h))
+
     near_c = core_swap(near)
     side = both_ways(near, "x")
+    side_c = both_ways(near_c, "x")
+    held, side_tau, side_h = lax.optimization_barrier((held, side_tau, side_h))
     take = move_call(take_kernel, "take", [(tau.shape[0] // 2, tau.shape[1])], 1, 1, False)
     far_tau = both_ways(take(side_tau)[0], "z")
+    far_h = both_ways(take(side_h)[0], "z")
     ints_near, = integrals_of(held, [near, near_c], (0,), "integrals_near")
-    near_c, ints_near = lax.optimization_barrier((near_c, ints_near))
-    side_c = both_ways(near_c, "x")
+    side, side_c, ints_near = lax.optimization_barrier((side, side_c, ints_near))
     far = both_ways(side, "x")
-    held, side_h, far_tau = lax.optimization_barrier((held, side_h, far_tau))
-    far_h = both_ways(take(side_h)[0], "z")
     ints_side, = integrals_of(
         held, [side, side_c, core_swap(side), core_swap(side_c)], (0, 1), "integrals_side")
-    far, far_c, ints_side = lax.optimization_barrier((far, core_swap(far), ints_side))
-    ints_far, = integrals_of(held, [far, far_c], (0,), "integrals_far")
-    ints = [ints_near, ints_side, ints_far]
     pieces = [tau, tau_h, side_tau, core_swap(side_tau), side_h, core_swap(side_h)]
-    partial = contract(ints, pieces, None)
-
-    far_h, partial = lax.optimization_barrier((far_h, partial))
-    partial = contract(ints, [far_tau, core_swap(far_tau), far_h, core_swap(far_h)], partial)
+    partial = contract([ints_near, ints_side], pieces, None)
+    far, partial = lax.optimization_barrier((far, partial))
+    ints_far, = integrals_of(held, [far, core_swap(far)], (0,), "integrals_far")
+    pieces += [far_tau, core_swap(far_tau), far_h, core_swap(far_h)]
+    partial = contract([ints_near, ints_side, ints_far], pieces, partial)
 
     parts = lax.all_to_all(partial.reshape(128, 2 * rows_here), TILE + PAIR, split_axis=0, concat_axis=0, tiled=True)
     residual, update = pl.pallas_call(

time: 113 us -> 110 us (0.973)
  waiting for transfers between devices: 30.2 us -> 22.2 us
  starting transfers between devices: 40.2 us -> 44 us
  Pallas kernels: 20.9 us -> 24.4 us
  local copies, waits for them, and re-layouts: 5.46 us -> 2.73 us
    ppermute x16, waiting for transfers between devices: 14.9 us -> 9.14 us  [shift(): return lax.ppermute(x, axis, [(i, (i + step) % size) for i in range(size)])]
    ppermute x16, starting transfers between devices: 16.6 us -> 20.5 us  [shift(): return lax.ppermute(x, axis, [(i, (i + step) % size) for i in range(size)])]
    pallas_call x0 -> x1, Pallas kernels: none -> 3.39 us  [hold(): pl.pallas_call(hold_kernel, out_shape=jax.ShapeDtypeStruct(factors.shape,...]
    unnamed x10, local copies, waits for them, and re-layouts: 3.41 us -> 0.68 us
    ppermute x7, waiting for transfers between devices: 9.54 us -> 7.37 us  [both_ways(): return lax.ppermute(x, (axis, 'c'), pairs)]
  transfers between devices with their start and end apart: 27 -> 27, of which waited for: 13 -> 9; matrix products, arithmetic and copies ran while one was open for 0% -> 0% of each run, Pallas kernels for 16% -> 19%
where the time goes in v4:
time: 110 us; the launch traced here: 109 us
  starting transfers between devices  44 us (40%)
  Pallas kernels  24.4 us (22%)
  waiting for transfers between devices  22.2 us (20%)
  blocking collectives  15.3 us (14%)
  local copies, waits for them, and re-layouts  2.73 us (2%)
    ppermute x16, starting transfers between devices, shift(): return lax.ppermute(x, axis, [(i, (i + step) % size) for i in range(size)])  20.5 us
    all_to_all x1, blocking collectives, local(): lax.all_to_all(partial.reshape(128, 2 * rows_here), TILE + PAIR, split_ax...  15.3 us
    ppermute x7, starting transfers between devices, both_ways(): return lax.ppermute(x, (axis, 'c'), pairs)  13.9 us
    pallas_call x3, Pallas kernels, integrals_of(): pl.pallas_call(first_kernel if load else functools.partial(next_kernel, f...  9.25 us
    ppermute x16, waiting for transfers between devices, shift(): return lax.ppermute(x, axis, [(i, (i + step) % size) for i in range(size)])  9.14 us
    ppermute x7, waiting for transfers between devices, both_ways(): return lax.ppermute(x, (axis, 'c'), pairs)  7.37 us
    all_to_all x1, starting transfers between devices, local(): tau = lax.all_to_all(tau, PAIR, split_axis=0, concat_axis=0, tiled=True)  5.86 us
    ppermute x3, waiting for transfers between devices, shift_y(): lax.ppermute(x, ('yl', 'yh'), [(at[y], at[(y + step) % 4]) for y in range...  5.67 us
  transfers between devices with their start and end apart: 27, of which 9 were waited for; matrix products, arithmetic and copies ran while one was open for 0% of the time, Pallas kernels for 19%

profile of v4, /device:TPU:1, one launch (start us, length us, event | category | flops | bytes accessed | tf_op | source)
XLA Modules:
  0.0 109.5 jit_solution(401837209212285304)
XLA Ops:
  0.6 2.1 %copy.9 = bf16[512,512]{1,0:T(8,128)(2,1)} copy(bf16[512,512]{0,1:T(8,128)(2,1)} %bitcast.10) | data formatting | bytes 1048576 | tf_op jit(solution)/shard_map/transpose | solution.py:335
  2.7 5.9 %all-to-all-start = ((bf16[8,64,512]{2,1,0:T(8,128)(2,1)}), bf16[8,64,512]{2,1,0:T(8,128)(2,1)S(1)}, u32[]{:S(2)}, u32[]{:S(2)}) async-start(bf16[8,64,512]{2,1,0:T(8,128)(2,1)} %bitcast.2), calls=%async_computation | async-start | bytes 1048576 | tf_op jit(solution)/shard_map/all_to_all | solution.py:336
  14.0 2.7 %collective-permute-start.1 = (bf16[32,2048]{1,0:T(8,128)(2,1)S(1)}, bf16[32,2048]{1,0:T(8,128)(2,1)S(1)}, u32[]{:S(2)}, u32[]{:S(2)}) collective-permute-start(bf16[32,2048]{1,0:T(8,128)(2,1)S(1)} %get-tuple-element.27), channel_id=1, source_target_pairs={{0,2},{2,0},{1,3},{3,1},{4,6},{6,4},{5,7},{7,5},{8,10},{10,8},{9,1... | collective-permute-start | bytes 393224 | tf_op jit(solution)/shard_map/ppermute | solution.py:17
  16.7 4.3 %collective-permute-done.1.got = bf16[32,2048]{1,0:T(8,128)(2,1)S(1)} collective-permute-done((bf16[32,2048]{1,0:T(8,128)(2,1)S(1)}, bf16[32,2048]{1,0:T(8,128)(2,1)S(1)}, u32[]{:S(2)}, u32[]{:S(2)}) %collective-permute-start.1) | collective-permute-done | bytes 131104 | tf_op jit(solution)/shard_map/ppermute | solution.py:17
  23.0 1.9 %collective-permute-start.6 = (bf16[8,64,512]{2,1,0:T(8,128)(2,1)S(1)}, bf16[8,64,512]{2,1,0:T(8,128)(2,1)S(1)}, u32[]{:S(2)}, u32[]{:S(2)}) collective-permute-start(bf16[8,64,512]{2,1,0:T(8,128)(2,1)S(1)} %all-to-all-done.first), channel_id=1, source_target_pairs={{0,2},{2,0},{1,3},{3,1},{4,6},{6,4},{5,7},{7,5},{8,10},{10,8},{9,1... | collective-permute-start | bytes 1572872 | tf_op jit(solution)/shard_map/ppermute | solution.py:17
  24.9 1.6 %collective-permute-start.2 = (bf16[32,2048]{1,0:T(8,128)(2,1)S(1)}, bf16[32,2048]{1,0:T(8,128)(2,1)S(1)}, u32[]{:S(2)}, u32[]{:S(2)}) collective-permute-start(bf16[32,2048]{1,0:T(8,128)(2,1)S(1)} %choose.1.own), channel_id=1, source_target_pairs={{0,4},{4,8},{8,12},{12,0},{1,5},{5,9},{9,13},{13,1},{2,6},{6,10},{... | collective-permute-start | bytes 393224 | tf_op jit(solution)/shard_map/ppermute | solution.py:17
  26.6 2.1 %collective-permute-start.3 = (bf16[32,2048]{1,0:T(8,128)(2,1)S(1)}, bf16[32,2048]{1,0:T(8,128)(2,1)S(1)}, u32[]{:S(2)}, u32[]{:S(2)}) collective-permute-start(bf16[32,2048]{1,0:T(8,128)(2,1)S(1)} %choose.1.own), channel_id=1, source_target_pairs={{0,12},{4,0},{8,4},{12,8},{1,13},{5,1},{9,5},{13,9},{2,14},{6,2},{... | collective-permute-start | bytes 393224 | tf_op jit(solution)/shard_map/ppermute | solution.py:17
  30.0 3.4 %hold.1.held = bf16[32,64,2048]{2,1,0:T(8,128)(2,1)S(1)} custom-call(bf16[32,64,2048]{2,1,0:T(8,128)(2,1)} %source), custom_call_target="tpu_custom_call" | custom-call | bytes 16777216 | tf_op jit(solution)/shard_map/hold/pallas_call | solution.py:117
  33.4 2.5 %collective-permute-done.4.far = bf16[32,2048]{1,0:T(8,128)(2,1)S(1)} collective-permute-done((bf16[32,2048]{1,0:T(8,128)(2,1)S(1)}, bf16[32,2048]{1,0:T(8,128)(2,1)S(1)}, u32[]{:S(2)}, u32[]{:S(2)}) %collective-permute-start.4) | collective-permute-done | bytes 131104 | tf_op jit(solution)/shard_map/ppermute | solution.py:17
  38.9 3.8 %collective-permute-start.14 = (bf16[128,4096]{1,0:T(8,128)(2,1)S(1)}, bf16[128,4096]{1,0:T(8,128)(2,1)S(1)}, u32[]{:S(2)}, u32[]{:S(2)}) collective-permute-start(bf16[128,4096]{1,0:T(8,128)(2,1)S(1)} %lay.2.refs_2_.refs_3_), channel_id=1, source_target_pairs={{0,4},{1,13},{4,8},{5,1},{8,12},{9,5},{12,0},{13,9},{2,6},{3,15},{... | collective-permute-start | bytes 3145736 | tf_op jit(solution)/shard_map/ppermute | solution.py:325
  42.8 1.6 %collective-permute-start.15 = (bf16[128,4096]{1,0:T(8,128)(2,1)S(1)}, bf16[128,4096]{1,0:T(8,128)(2,1)S(1)}, u32[]{:S(2)}, u32[]{:S(2)}) collective-permute-start(bf16[128,4096]{1,0:T(8,128)(2,1)S(1)} %lay.3.refs_3_.refs_4_), channel_id=1, source_target_pairs={{0,4},{1,13},{4,8},{5,1},{8,12},{9,5},{12,0},{13,9},{2,6},{3,15},{... | collective-permute-start | bytes 3145736 | tf_op jit(solution)/shard_map/ppermute | solution.py:325
  48.0 2.1 %collective-permute-done.7.up = bf16[32,2048]{1,0:T(8,128)(2,1)S(1)} collective-permute-done((bf16[32,2048]{1,0:T(8,128)(2,1)S(1)}, bf16[32,2048]{1,0:T(8,128)(2,1)S(1)}, u32[]{:S(2)}, u32[]{:S(2)}) %collective-permute-start.7) | collective-permute-done | bytes 131104 | tf_op jit(solution)/shard_map/ppermute | solution.py:22
  51.4 2.3 %collective-permute-done.9.far = bf16[32,2048]{1,0:T(8,128)(2,1)S(1)} collective-permute-done((bf16[32,2048]{1,0:T(8,128)(2,1)S(1)}, bf16[32,2048]{1,0:T(8,128)(2,1)S(1)}, u32[]{:S(2)}, u32[]{:S(2)}) %collective-permute-start.9) | collective-permute-done | bytes 131104 | tf_op jit(solution)/shard_map/ppermute | solution.py:22
  54.9 2.2 %collective-permute-start.11 = (bf16[128,2048]{1,0:T(8,128)(2,1)S(1)}, bf16[128,2048]{1,0:T(8,128)(2,1)S(1)}, u32[]{:S(2)}, u32[]{:S(2)}) collective-permute-start(bf16[128,2048]{1,0:T(8,128)(2,1)S(1)} %place.1.refs_0_), channel_id=1, source_target_pairs={{0,32},{1,97},{32,64},{33,1},{64,96},{65,33},{96,0},{97,65},{2,34}... | collective-permute-start | bytes 1572872 | tf_op jit(solution)/shard_map/ppermute | solution.py:325
  58.7 6.9 %collective-permute-done.15.refs_6_.source.refs_7_ = bf16[128,4096]{1,0:T(8,128)(2,1)S(1)} collective-permute-done((bf16[128,4096]{1,0:T(8,128)(2,1)S(1)}, bf16[128,4096]{1,0:T(8,128)(2,1)S(1)}, u32[]{:S(2)}, u32[]{:S(2)}) %collective-permute-start.15) | collective-permute-done | bytes 1048608 | tf_op jit(solution)/shard_map/ppermute | solution.py:325
  66.9 2.4 %integrals_near.1.refs_0_ = bf16[1,512,1024]{2,1,0:T(8,128)(2,1)S(1)} custom-call(bf16[32,64,2048]{2,1,0:T(8,128)(2,1)S(1)} %hold.1.held, bf16[128,2048]{1,0:T(8,128)(2,1)S(1)} %place.1.refs_0_, bf16[128,2048]{1,0:T(8,128)(2,1)S(1)} %collective-permute-done.12.refs_1_), custom_call_target="tpu_custom_call" | custom-call | flops 2147483648 | bytes 10485760 | tf_op jit(solution)/shard_map/integrals_near/pallas_call | solution.py:205
  69.3 1.7 %collective-permute-start.16 = (bf16[128,2048]{1,0:T(8,128)(2,1)S(1)}, bf16[128,2048]{1,0:T(8,128)(2,1)S(1)}, u32[]{:S(2)}, u32[]{:S(2)}) collective-permute-start(bf16[128,2048]{1,0:T(8,128)(2,1)S(1)} %collective-permute-done.11.refs_0_), channel_id=1, source_target_pairs={{0,1},{1,0},{2,3},{3,2},{4,5},{5,4},{6,7},{7,6},{8,9},{9,8},{10,11... | collective-permute-start | bytes 1572872 | tf_op jit(solution)/shard_map/ppermute | solution.py:17
  73.9 2.0 %collective-permute-start.18 = (bf16[128,2048]{1,0:T(8,128)(2,1)S(1)}, bf16[128,2048]{1,0:T(8,128)(2,1)S(1)}, u32[]{:S(2)}, u32[]{:S(2)}) collective-permute-start(bf16[128,2048]{1,0:T(8,128)(2,1)S(1)} %collective-permute-done.11.refs_0_), channel_id=1, source_target_pairs={{0,32},{1,97},{32,64},{33,1},{64,96},{65,33},{96,0},{97,65},{2,34}... | collective-permute-start | bytes 1572872 | tf_op jit(solution)/shard_map/ppermute | solution.py:325
  75.9 4.5 %integrals_side.1.refs_1_ = bf16[2,512,1024]{2,1,0:T(8,128)(2,1)S(1)} custom-call(bf16[32,64,2048]{2,1,0:T(8,128)(2,1)S(1)} %hold.1.held, bf16[128,2048]{1,0:T(8,128)(2,1)S(1)} %collective-permute-done.11.refs_0_, bf16[128,2048]{1,0:T(8,128)(2,1)S(1)} %collective-permute-done.13.refs_1_, bf16[128,2048]{1,0:T(8,128)(2,1)S(1)} %collective-permute-done.16.refs_2_, ...), custom_call_target="tpu_custom_call" | custom-call | flops 4294967296 | bytes 10485760 | tf_op jit(solution)/shard_map/integrals_side/pallas_call | solution.py:205
  80.4 2.6 %contract_early.1.refs_13_ = f32[3,2,512,128]{3,2,1,0:T(8,128)S(1)} custom-call(bf16[1,512,1024]{2,1,0:T(8,128)(2,1)S(1)} %integrals_near.1.refs_0_, bf16[2,512,1024]{2,1,0:T(8,128)(2,1)S(1)} %integrals_side.1.refs_1_, bf16[128,4096]{1,0:T(8,128)(2,1)S(1)} %lay.2.refs_2_.refs_3_, bf16[128,4096]{1,0:T(8,128)(2,1)S(1)} %lay.3.refs_3_.refs_4_, ...), custom_call_target="tpu_custom_call" | custom-call | flops 2415919104 | bytes 8388608 | tf_op jit(solution)/shard_map/contract_early/pallas_call | solution.py:294
  85.1 2.6 %collective-permute-start.25 = (bf16[64,4096]{1,0:T(8,128)(2,1)S(1)}, bf16[64,4096]{1,0:T(8,128)(2,1)S(1)}, u32[]{:S(2)}, u32[]{:S(2)}) collective-permute-start(bf16[64,4096]{1,0:T(8,128)(2,1)S(1)} %collective-permute-done.24.refs_11_), channel_id=1, source_target_pairs={{0,1},{1,0},{2,3},{3,2},{4,5},{5,4},{6,7},{7,6},{8,9},{9,8},{10,11... | collective-permute-start | bytes 1572872 | tf_op jit(solution)/shard_map/ppermute | solution.py:17
  87.7 2.4 %integrals_far.1.refs_2_ = bf16[1,512,1024]{2,1,0:T(8,128)(2,1)S(1)} custom-call(bf16[32,64,2048]{2,1,0:T(8,128)(2,1)S(1)} %hold.1.held, bf16[128,2048]{1,0:T(8,128)(2,1)S(1)} %collective-permute-done.18.refs_0_, bf16[128,2048]{1,0:T(8,128)(2,1)S(1)} %collective-permute-done.21.refs_1_), custom_call_target="tpu_custom_call" | custom-call | flops 2147483648 | bytes 10485760 | tf_op jit(solution)/shard_map/integrals_far/pallas_call | solution.py:205
  90.1 2.7 %contract_late.1 = f32[16,8,64]{2,1,0:T(8,128)S(1)} custom-call(bf16[1,512,1024]{2,1,0:T(8,128)(2,1)S(1)} %integrals_near.1.refs_0_, bf16[2,512,1024]{2,1,0:T(8,128)(2,1)S(1)} %integrals_side.1.refs_1_, bf16[1,512,1024]{2,1,0:T(8,128)(2,1)S(1)} %integrals_far.1.refs_2_, bf16[128,4096]{1,0:T(8,128)(2,1)S(1)} %lay.2.refs_2_.refs_3_, ...), custom_call_target="tpu_custom_call" | custom-call | flops 1879048192 | bytes 8388608 | tf_op jit(solution)/shard_map/contract_late/pallas_call | solution.py:294
  92.8 15.3 %all_to_all.16 = f32[128,1,64]{2,1,0:T(1,128)S(1)} all-to-all(f32[128,1,64]{2,1,0:T(1,128)S(1)} %bitcast.8), channel_id=1, replica_groups=mesh['x'=4,'yl'=2,'z'=4,'yh'=2,'c'=2] {'z','yh','c','x','yl'}, dimensions={0} | all-to-all | bytes 65536 | tf_op jit(solution)/shard_map/all_to_all | solution.py:384
  (58 shorter events, 27.0 us)
Async XLA Ops:
  2.7 19.0 %all-to-all-start = ((bf16[8,64,512]{2,1,0:T(8,128)(2,1)}), bf16[8,64,512]{2,1,0:T(8,128)(2,1)S(1)}, u32[]{:S(2)}, u32[]{:S(2)}) async-start(bf16[8,64,512]{2,1,0:T(8,128)(2,1)} %bitcast.2), calls=%async_computation | async-start | bytes 1048576 | tf_op jit(solution)/shard_map/all_to_all | solution.py:336
  14.0 7.0 %collective-permute-start.1 = (bf16[32,2048]{1,0:T(8,128)(2,1)S(1)}, bf16[32,2048]{1,0:T(8,128)(2,1)S(1)}, u32[]{:S(2)}, u32[]{:S(2)}) collective-permute-start(bf16[32,2048]{1,0:T(8,128)(2,1)S(1)} %get-tuple-element.27), channel_id=1, source_target_pairs={{0,2},{2,0},{1,3},{3,1},{4,6},{6,4},{5,7},{7,5},{8,10},{10,8},{9,1... | collective-permute-start | bytes 393224 | tf_op jit(solution)/shard_map/ppermute | solution.py:17
  21.7 15.0 %collective-permute-start.5 = (bf16[8,64,512]{2,1,0:T(8,128)(2,1)S(1)}, bf16[8,64,512]{2,1,0:T(8,128)(2,1)S(1)}, u32[]{:S(2)}, u32[]{:S(2)}) collective-permute-start(bf16[8,64,512]{2,1,0:T(8,128)(2,1)S(1)} %all-to-all-done.first), channel_id=1, source_target_pairs={{0,1},{1,0},{2,3},{3,2},{4,5},{5,4},{6,7},{7,6},{8,9},{9,8},{10,11... | collective-permute-start | bytes 1572872 | tf_op jit(solution)/shard_map/ppermute | solution.py:17
  23.0 15.0 %collective-permute-start.6 = (bf16[8,64,512]{2,1,0:T(8,128)(2,1)S(1)}, bf16[8,64,512]{2,1,0:T(8,128)(2,1)S(1)}, u32[]{:S(2)}, u32[]{:S(2)}) collective-permute-start(bf16[8,64,512]{2,1,0:T(8,128)(2,1)S(1)} %all-to-all-done.first), channel_id=1, source_target_pairs={{0,2},{2,0},{1,3},{3,1},{4,6},{6,4},{5,7},{7,5},{8,10},{10,8},{9,1... | collective-permute-start | bytes 1572872 | tf_op jit(solution)/shard_map/ppermute | solution.py:17
  24.9 8.5 %collective-permute-start.2 = (bf16[32,2048]{1,0:T(8,128)(2,1)S(1)}, bf16[32,2048]{1,0:T(8,128)(2,1)S(1)}, u32[]{:S(2)}, u32[]{:S(2)}) collective-permute-start(bf16[32,2048]{1,0:T(8,128)(2,1)S(1)} %choose.1.own), channel_id=1, source_target_pairs={{0,4},{4,8},{8,12},{12,0},{1,5},{5,9},{9,13},{13,1},{2,6},{6,10},{... | collective-permute-start | bytes 393224 | tf_op jit(solution)/shard_map/ppermute | solution.py:17
  26.6 6.8 %collective-permute-start.3 = (bf16[32,2048]{1,0:T(8,128)(2,1)S(1)}, bf16[32,2048]{1,0:T(8,128)(2,1)S(1)}, u32[]{:S(2)}, u32[]{:S(2)}) collective-permute-start(bf16[32,2048]{1,0:T(8,128)(2,1)S(1)} %choose.1.own), channel_id=1, source_target_pairs={{0,12},{4,0},{8,4},{12,8},{1,13},{5,1},{9,5},{13,9},{2,14},{6,2},{... | collective-permute-start | bytes 393224 | tf_op jit(solution)/shard_map/ppermute | solution.py:17
  28.7 7.2 %collective-permute-start.4 = (bf16[32,2048]{1,0:T(8,128)(2,1)S(1)}, bf16[32,2048]{1,0:T(8,128)(2,1)S(1)}, u32[]{:S(2)}, u32[]{:S(2)}) collective-permute-start(bf16[32,2048]{1,0:T(8,128)(2,1)S(1)} %choose.1.own), channel_id=1, source_target_pairs={{0,8},{4,12},{8,0},{12,4},{1,9},{5,13},{9,1},{13,5},{2,10},{6,14},... | collective-permute-start | bytes 393224 | tf_op jit(solution)/shard_map/ppermute | solution.py:17
  38.0 4.6 %collective-permute-start.10 = (bf16[8,64,512]{2,1,0:T(8,128)(2,1)S(1)}, bf16[8,64,512]{2,1,0:T(8,128)(2,1)S(1)}, u32[]{:S(2)}, u32[]{:S(2)}) collective-permute-start(bf16[8,64,512]{2,1,0:T(8,128)(2,1)S(1)} %collective-permute-done.6.first), channel_id=1, source_target_pairs={{0,1},{1,0},{2,3},{3,2},{4,5},{5,4},{6,7},{7,6},{8,9},{9,8},{10,11... | collective-permute-start | bytes 1572872 | tf_op jit(solution)/shard_map/ppermute | solution.py:17
  38.9 19.8 %collective-permute-start.14 = (bf16[128,4096]{1,0:T(8,128)(2,1)S(1)}, bf16[128,4096]{1,0:T(8,128)(2,1)S(1)}, u32[]{:S(2)}, u32[]{:S(2)}) collective-permute-start(bf16[128,4096]{1,0:T(8,128)(2,1)S(1)} %lay.2.refs_2_.refs_3_), channel_id=1, source_target_pairs={{0,4},{1,13},{4,8},{5,1},{8,12},{9,5},{12,0},{13,9},{2,6},{3,15},{... | collective-permute-start | bytes 3145736 | tf_op jit(solution)/shard_map/ppermute | solution.py:325
  42.8 22.8 %collective-permute-start.15 = (bf16[128,4096]{1,0:T(8,128)(2,1)S(1)}, bf16[128,4096]{1,0:T(8,128)(2,1)S(1)}, u32[]{:S(2)}, u32[]{:S(2)}) collective-permute-start(bf16[128,4096]{1,0:T(8,128)(2,1)S(1)} %lay.3.refs_3_.refs_4_), channel_id=1, source_target_pairs={{0,4},{1,13},{4,8},{5,1},{8,12},{9,5},{12,0},{13,9},{2,6},{3,15},{... | collective-permute-start | bytes 3145736 | tf_op jit(solution)/shard_map/ppermute | solution.py:325
  44.4 5.7 %collective-permute-start.7 = (bf16[32,2048]{1,0:T(8,128)(2,1)S(1)}, bf16[32,2048]{1,0:T(8,128)(2,1)S(1)}, u32[]{:S(2)}, u32[]{:S(2)}) collective-permute-start(bf16[32,2048]{1,0:T(8,128)(2,1)S(1)} %choose_z.1.own), channel_id=1, source_target_pairs={{0,16},{16,2},{2,18},{18,0},{1,17},{17,3},{3,19},{19,1},{4,20},{20... | collective-permute-start | bytes 393224 | tf_op jit(solution)/shard_map/ppermute | solution.py:22
  45.9 5.5 %collective-permute-start.8 = (bf16[32,2048]{1,0:T(8,128)(2,1)S(1)}, bf16[32,2048]{1,0:T(8,128)(2,1)S(1)}, u32[]{:S(2)}, u32[]{:S(2)}) collective-permute-start(bf16[32,2048]{1,0:T(8,128)(2,1)S(1)} %choose_z.1.own), channel_id=1, source_target_pairs={{0,18},{16,0},{2,16},{18,2},{1,19},{17,1},{3,17},{19,3},{4,22},{20... | collective-permute-start | bytes 393224 | tf_op jit(solution)/shard_map/ppermute | solution.py:22
  47.0 6.7 %collective-permute-start.9 = (bf16[32,2048]{1,0:T(8,128)(2,1)S(1)}, bf16[32,2048]{1,0:T(8,128)(2,1)S(1)}, u32[]{:S(2)}, u32[]{:S(2)}) collective-permute-start(bf16[32,2048]{1,0:T(8,128)(2,1)S(1)} %choose_z.1.own), channel_id=1, source_target_pairs={{0,2},{16,18},{2,0},{18,16},{1,3},{17,19},{3,1},{19,17},{4,6},{20,... | collective-permute-start | bytes 393224 | tf_op jit(solution)/shard_map/ppermute | solution.py:22
  54.9 14.4 %collective-permute-start.11 = (bf16[128,2048]{1,0:T(8,128)(2,1)S(1)}, bf16[128,2048]{1,0:T(8,128)(2,1)S(1)}, u32[]{:S(2)}, u32[]{:S(2)}) collective-permute-start(bf16[128,2048]{1,0:T(8,128)(2,1)S(1)} %place.1.refs_0_), channel_id=1, source_target_pairs={{0,32},{1,97},{32,64},{33,1},{64,96},{65,33},{96,0},{97,65},{2,34}... | collective-permute-start | bytes 1572872 | tf_op jit(solution)/shard_map/ppermute | solution.py:325
  57.1 12.2 %collective-permute-start.13 = (bf16[128,2048]{1,0:T(8,128)(2,1)S(1)}, bf16[128,2048]{1,0:T(8,128)(2,1)S(1)}, u32[]{:S(2)}, u32[]{:S(2)}) collective-permute-start(bf16[128,2048]{1,0:T(8,128)(2,1)S(1)} %collective-permute-done.12.refs_1_), channel_id=1, source_target_pairs={{0,32},{1,97},{32,64},{33,1},{64,96},{65,33},{96,0},{97,65},{2,34}... | collective-permute-start | bytes 1572872 | tf_op jit(solution)/shard_map/ppermute | solution.py:325
  65.6 14.8 %collective-permute-start.19 = (bf16[128,4096]{1,0:T(8,128)(2,1)S(1)}, bf16[128,4096]{1,0:T(8,128)(2,1)S(1)}, u32[]{:S(2)}, u32[]{:S(2)}) collective-permute-start(bf16[128,4096]{1,0:T(8,128)(2,1)S(1)} %collective-permute-done.14.refs_4_.source.refs_5_), channel_id=1, source_target_pairs={{0,1},{1,0},{2,3},{3,2},{4,5},{5,4},{6,7},{7,6},{8,9},{9,8},{10,11... | collective-permute-start | bytes 3145736 | tf_op jit(solution)/shard_map/ppermute | solution.py:17
  66.9 13.5 %collective-permute-start.20 = (bf16[128,4096]{1,0:T(8,128)(2,1)S(1)}, bf16[128,4096]{1,0:T(8,128)(2,1)S(1)}, u32[]{:S(2)}, u32[]{:S(2)}) collective-permute-start(bf16[128,4096]{1,0:T(8,128)(2,1)S(1)} %collective-permute-done.15.refs_6_.source.refs_7_), channel_id=1, source_target_pairs={{0,1},{1,0},{2,3},{3,2},{4,5},{5,4},{6,7},{7,6},{8,9},{9,8},{10,11... | collective-permute-start | bytes 3145736 | tf_op jit(solution)/shard_map/ppermute | solution.py:17
  69.3 3.4 %collective-permute-start.16 = (bf16[128,2048]{1,0:T(8,128)(2,1)S(1)}, bf16[128,2048]{1,0:T(8,128)(2,1)S(1)}, u32[]{:S(2)}, u32[]{:S(2)}) collective-permute-start(bf16[128,2048]{1,0:T(8,128)(2,1)S(1)} %collective-permute-done.11.refs_0_), channel_id=1, source_target_pairs={{0,1},{1,0},{2,3},{3,2},{4,5},{5,4},{6,7},{7,6},{8,9},{9,8},{10,11... | collective-permute-start | bytes 1572872 | tf_op jit(solution)/shard_map/ppermute | solution.py:17
  71.1 13.6 %collective-permute-start.22 = (bf16[64,4096]{1,0:T(8,128)(2,1)S(1)}, bf16[64,4096]{1,0:T(8,128)(2,1)S(1)}, u32[]{:S(2)}, u32[]{:S(2)}) collective-permute-start(bf16[64,4096]{1,0:T(8,128)(2,1)S(1)} %take.2), channel_id=1, source_target_pairs={{0,4},{1,13},{4,8},{5,1},{8,12},{9,5},{12,0},{13,9},{2,6},{3,15},{... | collective-permute-start | bytes 1572872 | tf_op jit(solution)/shard_map/ppermute | solution.py:325
  72.7 12.4 %collective-permute-start.24 = (bf16[64,4096]{1,0:T(8,128)(2,1)S(1)}, bf16[64,4096]{1,0:T(8,128)(2,1)S(1)}, u32[]{:S(2)}, u32[]{:S(2)}) collective-permute-start(bf16[64,4096]{1,0:T(8,128)(2,1)S(1)} %take.3), channel_id=1, source_target_pairs={{0,4},{1,13},{4,8},{5,1},{8,12},{9,5},{12,0},{13,9},{2,6},{3,15},{... | collective-permute-start | bytes 1572872 | tf_op jit(solution)/shard_map/ppermute | solution.py:325
  73.9 9.2 %collective-permute-start.18 = (bf16[128,2048]{1,0:T(8,128)(2,1)S(1)}, bf16[128,2048]{1,0:T(8,128)(2,1)S(1)}, u32[]{:S(2)}, u32[]{:S(2)}) collective-permute-start(bf16[128,2048]{1,0:T(8,128)(2,1)S(1)} %collective-permute-done.11.refs_0_), channel_id=1, source_target_pairs={{0,32},{1,97},{32,64},{33,1},{64,96},{65,33},{96,0},{97,65},{2,34}... | collective-permute-start | bytes 1572872 | tf_op jit(solution)/shard_map/ppermute | solution.py:325
  83.1 4.6 %collective-permute-start.21 = (bf16[128,2048]{1,0:T(8,128)(2,1)S(1)}, bf16[128,2048]{1,0:T(8,128)(2,1)S(1)}, u32[]{:S(2)}, u32[]{:S(2)}) collective-permute-start(bf16[128,2048]{1,0:T(8,128)(2,1)S(1)} %collective-permute-done.18.refs_0_), channel_id=1, source_target_pairs={{0,1},{1,0},{2,3},{3,2},{4,5},{5,4},{6,7},{7,6},{8,9},{9,8},{10,11... | collective-permute-start | bytes 1572872 | tf_op jit(solution)/shard_map/ppermute | solution.py:17
  84.7 5.4 %collective-permute-start.23 = (bf16[64,4096]{1,0:T(8,128)(2,1)S(1)}, bf16[64,4096]{1,0:T(8,128)(2,1)S(1)}, u32[]{:S(2)}, u32[]{:S(2)}) collective-permute-start(bf16[64,4096]{1,0:T(8,128)(2,1)S(1)} %collective-permute-done.22.refs_9_), channel_id=1, source_target_pairs={{0,1},{1,0},{2,3},{3,2},{4,5},{5,4},{6,7},{7,6},{8,9},{9,8},{10,11... | collective-permute-start | bytes 1572872 | tf_op jit(solution)/shard_map/ppermute | solution.py:17
  85.1 5.0 %collective-permute-start.25 = (bf16[64,4096]{1,0:T(8,128)(2,1)S(1)}, bf16[64,4096]{1,0:T(8,128)(2,1)S(1)}, u32[]{:S(2)}, u32[]{:S(2)}) collective-permute-start(bf16[64,4096]{1,0:T(8,128)(2,1)S(1)} %collective-permute-done.24.refs_11_), channel_id=1, source_target_pairs={{0,1},{1,0},{2,3},{3,2},{4,5},{5,4},{6,7},{7,6},{8,9},{9,8},{10,11... | collective-permute-start | bytes 1572872 | tf_op jit(solution)/shard_map/ppermute | solution.py:17
  (8 other events, 75.2 us)

commit v5 on v4

--- a/solution.py
+++ b/solution.py
@@ -365,12 +365,12 @@
     near_c = core_swap(near)
     side = both_ways(near, "x")
     side_c = both_ways(near_c, "x")
-    held, side_tau, side_h = lax.optimization_barrier((held, side_tau, side_h))
     take = move_call(take_kernel, "take", [(tau.shape[0] // 2, tau.shape[1])], 1, 1, False)
     far_tau = both_ways(take(side_tau)[0], "z")
+    held, side_tau, side_h = lax.optimization_barrier((held, side_tau, side_h))
     far_h = both_ways(take(side_h)[0], "z")
     ints_near, = integrals_of(held, [near, near_c], (0,), "integrals_near")
-    side, side_c, ints_near = lax.optimization_barrier((side, side_c, ints_near))
+    side, side_c, ints_near, far_tau = lax.optimization_barrier((side, side_c, ints_near, far_tau))
     far = both_ways(side, "x")
     ints_side, = integrals_of(
         held, [side, side_c, core_swap(side), core_swap(side_c)], (0, 1), "integrals_side")

time: 110 us -> 110 us (level)
  starting transfers between devices: 44 us -> 41.7 us
    ppermute x16, starting transfers between devices: 20.5 us -> 16.9 us  [shift(): return lax.ppermute(x, axis, [(i, (i + step) % size) for i in range(size)])]
    ppermute x7, starting transfers between devices: 13.9 us -> 15.3 us  [both_ways(): return lax.ppermute(x, (axis, 'c'), pairs)]
  transfers between devices with their start and end apart: 27 -> 27, of which waited for: 9 -> 10; matrix products, arithmetic and copies ran while one was open for 0% -> 0% of each run, Pallas kernels for 19% -> 19%
where the time goes in v5:
time: 110 us; the launch traced here: 109 us
  starting transfers between devices  41.7 us (38%)
  Pallas kernels  24.4 us (22%)
  waiting for transfers between devices  23.2 us (21%)
  blocking collectives  16.3 us (15%)
  local copies, waits for them, and re-layouts  2.73 us (2%)
    ppermute x16, starting transfers between devices, shift(): return lax.ppermute(x, axis, [(i, (i + step) % size) for i in range(size)])  16.9 us
    all_to_all x1, blocking collectives, local(): lax.all_to_all(partial.reshape(128, 2 * rows_here), TILE + PAIR, split_ax...  16.3 us
    ppermute x7, starting transfers between devices, both_ways(): return lax.ppermute(x, (axis, 'c'), pairs)  15.3 us
    ppermute x16, waiting for transfers between devices, shift(): return lax.ppermute(x, axis, [(i, (i + step) % size) for i in range(size)])  10.2 us
    pallas_call x3, Pallas kernels, integrals_of(): pl.pallas_call(first_kernel if load else functools.partial(next_kernel, f...  9.26 us
    ppermute x7, waiting for transfers between devices, both_ways(): return lax.ppermute(x, (axis, 'c'), pairs)  7.28 us
    all_to_all x1, starting transfers between devices, local(): tau = lax.all_to_all(tau, PAIR, split_axis=0, concat_axis=0, tiled=True)  5.86 us
    ppermute x3, waiting for transfers between devices, shift_y(): lax.ppermute(x, ('yl', 'yh'), [(at[y], at[(y + step) % 4]) for y in range...  5.67 us
  transfers between devices with their start and end apart: 27, of which 10 were waited for; matrix products, arithmetic and copies ran while one was open for 0% of the time, Pallas kernels for 19%

profile of v5, /device:TPU:1, one launch (start us, length us, event | category | flops | bytes accessed | tf_op | source)
XLA Modules:
  0.0 109.2 jit_solution(9864625896772381663)
XLA Ops:
  0.6 2.1 %copy.9 = bf16[512,512]{1,0:T(8,128)(2,1)} copy(bf16[512,512]{0,1:T(8,128)(2,1)} %bitcast.10) | data formatting | bytes 1048576 | tf_op jit(solution)/shard_map/transpose | solution.py:335
  2.7 5.9 %all-to-all-start = ((bf16[8,64,512]{2,1,0:T(8,128)(2,1)}), bf16[8,64,512]{2,1,0:T(8,128)(2,1)S(1)}, u32[]{:S(2)}, u32[]{:S(2)}) async-start(bf16[8,64,512]{2,1,0:T(8,128)(2,1)} %bitcast.2), calls=%async_computation | async-start | bytes 1048576 | tf_op jit(solution)/shard_map/all_to_all | solution.py:336
  14.0 2.7 %collective-permute-start.1 = (bf16[32,2048]{1,0:T(8,128)(2,1)S(1)}, bf16[32,2048]{1,0:T(8,128)(2,1)S(1)}, u32[]{:S(2)}, u32[]{:S(2)}) collective-permute-start(bf16[32,2048]{1,0:T(8,128)(2,1)S(1)} %get-tuple-element.28), channel_id=1, source_target_pairs={{0,2},{2,0},{1,3},{3,1},{4,6},{6,4},{5,7},{7,5},{8,10},{10,8},{9,1... | collective-permute-start | bytes 393224 | tf_op jit(solution)/shard_map/ppermute | solution.py:17
  16.7 4.3 %collective-permute-done.1.got = bf16[32,2048]{1,0:T(8,128)(2,1)S(1)} collective-permute-done((bf16[32,2048]{1,0:T(8,128)(2,1)S(1)}, bf16[32,2048]{1,0:T(8,128)(2,1)S(1)}, u32[]{:S(2)}, u32[]{:S(2)}) %collective-permute-start.1) | collective-permute-done | bytes 131104 | tf_op jit(solution)/shard_map/ppermute | solution.py:17
  23.0 1.9 %collective-permute-start.6 = (bf16[8,64,512]{2,1,0:T(8,128)(2,1)S(1)}, bf16[8,64,512]{2,1,0:T(8,128)(2,1)S(1)}, u32[]{:S(2)}, u32[]{:S(2)}) collective-permute-start(bf16[8,64,512]{2,1,0:T(8,128)(2,1)S(1)} %all-to-all-done.first), channel_id=1, source_target_pairs={{0,2},{2,0},{1,3},{3,1},{4,6},{6,4},{5,7},{7,5},{8,10},{10,8},{9,1... | collective-permute-start | bytes 1572872 | tf_op jit(solution)/shard_map/ppermute | solution.py:17
  24.9 1.6 %collective-permute-start.2 = (bf16[32,2048]{1,0:T(8,128)(2,1)S(1)}, bf16[32,2048]{1,0:T(8,128)(2,1)S(1)}, u32[]{:S(2)}, u32[]{:S(2)}) collective-permute-start(bf16[32,2048]{1,0:T(8,128)(2,1)S(1)} %choose.1.own), channel_id=1, source_target_pairs={{0,4},{4,8},{8,12},{12,0},{1,5},{5,9},{9,13},{13,1},{2,6},{6,10},{... | collective-permute-start | bytes 393224 | tf_op jit(solution)/shard_map/ppermute | solution.py:17
  26.6 2.1 %collective-permute-start.3 = (bf16[32,2048]{1,0:T(8,128)(2,1)S(1)}, bf16[32,2048]{1,0:T(8,128)(2,1)S(1)}, u32[]{:S(2)}, u32[]{:S(2)}) collective-permute-start(bf16[32,2048]{1,0:T(8,128)(2,1)S(1)} %choose.1.own), channel_id=1, source_target_pairs={{0,12},{4,0},{8,4},{12,8},{1,13},{5,1},{9,5},{13,9},{2,14},{6,2},{... | collective-permute-start | bytes 393224 | tf_op jit(solution)/shard_map/ppermute | solution.py:17
  30.0 3.4 %hold.1.held = bf16[32,64,2048]{2,1,0:T(8,128)(2,1)S(1)} custom-call(bf16[32,64,2048]{2,1,0:T(8,128)(2,1)} %source), custom_call_target="tpu_custom_call" | custom-call | bytes 16777216 | tf_op jit(solution)/shard_map/hold/pallas_call | solution.py:117
  33.4 2.5 %collective-permute-done.4.far = bf16[32,2048]{1,0:T(8,128)(2,1)S(1)} collective-permute-done((bf16[32,2048]{1,0:T(8,128)(2,1)S(1)}, bf16[32,2048]{1,0:T(8,128)(2,1)S(1)}, u32[]{:S(2)}, u32[]{:S(2)}) %collective-permute-start.4) | collective-permute-done | bytes 131104 | tf_op jit(solution)/shard_map/ppermute | solution.py:17
  38.9 3.8 %collective-permute-start.14 = (bf16[128,4096]{1,0:T(8,128)(2,1)S(1)}, bf16[128,4096]{1,0:T(8,128)(2,1)S(1)}, u32[]{:S(2)}, u32[]{:S(2)}) collective-permute-start(bf16[128,4096]{1,0:T(8,128)(2,1)S(1)} %lay.2.refs_2_.refs_3_), channel_id=1, source_target_pairs={{0,4},{1,13},{4,8},{5,1},{8,12},{9,5},{12,0},{13,9},{2,6},{3,15},{... | collective-permute-start | bytes 3145736 | tf_op jit(solution)/shard_map/ppermute | solution.py:325
  42.8 1.6 %collective-permute-start.15 = (bf16[128,4096]{1,0:T(8,128)(2,1)S(1)}, bf16[128,4096]{1,0:T(8,128)(2,1)S(1)}, u32[]{:S(2)}, u32[]{:S(2)}) collective-permute-start(bf16[128,4096]{1,0:T(8,128)(2,1)S(1)} %lay.3.refs_3_.refs_4_), channel_id=1, source_target_pairs={{0,4},{1,13},{4,8},{5,1},{8,12},{9,5},{12,0},{13,9},{2,6},{3,15},{... | collective-permute-start | bytes 3145736 | tf_op jit(solution)/shard_map/ppermute | solution.py:325
  48.0 2.1 %collective-permute-done.7.up = bf16[32,2048]{1,0:T(8,128)(2,1)S(1)} collective-permute-done((bf16[32,2048]{1,0:T(8,128)(2,1)S(1)}, bf16[32,2048]{1,0:T(8,128)(2,1)S(1)}, u32[]{:S(2)}, u32[]{:S(2)}) %collective-permute-start.7) | collective-permute-done | bytes 131104 | tf_op jit(solution)/shard_map/ppermute | solution.py:22
  51.4 2.3 %collective-permute-done.9.far = bf16[32,2048]{1,0:T(8,128)(2,1)S(1)} collective-permute-done((bf16[32,2048]{1,0:T(8,128)(2,1)S(1)}, bf16[32,2048]{1,0:T(8,128)(2,1)S(1)}, u32[]{:S(2)}, u32[]{:S(2)}) %collective-permute-start.9) | collective-permute-done | bytes 131104 | tf_op jit(solution)/shard_map/ppermute | solution.py:22
  54.9 2.2 %collective-permute-start.11 = (bf16[128,2048]{1,0:T(8,128)(2,1)S(1)}, bf16[128,2048]{1,0:T(8,128)(2,1)S(1)}, u32[]{:S(2)}, u32[]{:S(2)}) collective-permute-start(bf16[128,2048]{1,0:T(8,128)(2,1)S(1)} %place.1.refs_0_), channel_id=1, source_target_pairs={{0,32},{1,97},{32,64},{33,1},{64,96},{65,33},{96,0},{97,65},{2,34}... | collective-permute-start | bytes 1572872 | tf_op jit(solution)/shard_map/ppermute | solution.py:325
  60.2 5.4 %collective-permute-done.15.refs_6_.source.refs_7_ = bf16[128,4096]{1,0:T(8,128)(2,1)S(1)} collective-permute-done((bf16[128,4096]{1,0:T(8,128)(2,1)S(1)}, bf16[128,4096]{1,0:T(8,128)(2,1)S(1)}, u32[]{:S(2)}, u32[]{:S(2)}) %collective-permute-start.15) | collective-permute-done | bytes 1048608 | tf_op jit(solution)/shard_map/ppermute | solution.py:325
  66.9 2.4 %integrals_near.1.refs_0_ = bf16[1,512,1024]{2,1,0:T(8,128)(2,1)S(1)} custom-call(bf16[32,64,2048]{2,1,0:T(8,128)(2,1)S(1)} %hold.1.held, bf16[128,2048]{1,0:T(8,128)(2,1)S(1)} %place.1.refs_0_, bf16[128,2048]{1,0:T(8,128)(2,1)S(1)} %collective-permute-done.12.refs_1_), custom_call_target="tpu_custom_call" | custom-call | flops 2147483648 | bytes 10485760 | tf_op jit(solution)/shard_map/integrals_near/pallas_call | solution.py:205
  69.3 1.9 %collective-permute-done.16.refs_9_ = bf16[64,4096]{1,0:T(8,128)(2,1)S(1)} collective-permute-done((bf16[64,4096]{1,0:T(8,128)(2,1)S(1)}, bf16[64,4096]{1,0:T(8,128)(2,1)S(1)}, u32[]{:S(2)}, u32[]{:S(2)}) %collective-permute-start.16) | collective-permute-done | bytes 524320 | tf_op jit(solution)/shard_map/ppermute | solution.py:325
  72.6 2.4 %collective-permute-start.24 = (bf16[64,4096]{1,0:T(8,128)(2,1)S(1)}, bf16[64,4096]{1,0:T(8,128)(2,1)S(1)}, u32[]{:S(2)}, u32[]{:S(2)}) collective-permute-start(bf16[64,4096]{1,0:T(8,128)(2,1)S(1)} %take.3), channel_id=1, source_target_pairs={{0,4},{1,13},{4,8},{5,1},{8,12},{9,5},{12,0},{13,9},{2,6},{3,15},{... | collective-permute-start | bytes 1572872 | tf_op jit(solution)/shard_map/ppermute | solution.py:325
  75.0 2.3 %collective-permute-start.19 = (bf16[128,2048]{1,0:T(8,128)(2,1)S(1)}, bf16[128,2048]{1,0:T(8,128)(2,1)S(1)}, u32[]{:S(2)}, u32[]{:S(2)}) collective-permute-start(bf16[128,2048]{1,0:T(8,128)(2,1)S(1)} %collective-permute-done.11.refs_0_), channel_id=1, source_target_pairs={{0,32},{1,97},{32,64},{33,1},{64,96},{65,33},{96,0},{97,65},{2,34}... | collective-permute-start | bytes 1572872 | tf_op jit(solution)/shard_map/ppermute | solution.py:325
  77.2 4.5 %integrals_side.1.refs_1_ = bf16[2,512,1024]{2,1,0:T(8,128)(2,1)S(1)} custom-call(bf16[32,64,2048]{2,1,0:T(8,128)(2,1)S(1)} %hold.1.held, bf16[128,2048]{1,0:T(8,128)(2,1)S(1)} %collective-permute-done.11.refs_0_, bf16[128,2048]{1,0:T(8,128)(2,1)S(1)} %collective-permute-done.13.refs_1_, bf16[128,2048]{1,0:T(8,128)(2,1)S(1)} %collective-permute-done.17.refs_2_, ...), custom_call_target="tpu_custom_call" | custom-call | flops 4294967296 | bytes 10485760 | tf_op jit(solution)/shard_map/integrals_side/pallas_call | solution.py:205
  81.8 2.6 %contract_early.1.refs_13_ = f32[3,2,512,128]{3,2,1,0:T(8,128)S(1)} custom-call(bf16[1,512,1024]{2,1,0:T(8,128)(2,1)S(1)} %integrals_near.1.refs_0_, bf16[2,512,1024]{2,1,0:T(8,128)(2,1)S(1)} %integrals_side.1.refs_1_, bf16[128,4096]{1,0:T(8,128)(2,1)S(1)} %lay.2.refs_2_.refs_3_, bf16[128,4096]{1,0:T(8,128)(2,1)S(1)} %lay.3.refs_3_.refs_4_, ...), custom_call_target="tpu_custom_call" | custom-call | flops 2415919104 | bytes 8388608 | tf_op jit(solution)/shard_map/contract_early/pallas_call | solution.py:294
  86.4 2.4 %integrals_far.1.refs_2_ = bf16[1,512,1024]{2,1,0:T(8,128)(2,1)S(1)} custom-call(bf16[32,64,2048]{2,1,0:T(8,128)(2,1)S(1)} %hold.1.held, bf16[128,2048]{1,0:T(8,128)(2,1)S(1)} %collective-permute-done.19.refs_0_, bf16[128,2048]{1,0:T(8,128)(2,1)S(1)} %collective-permute-done.22.refs_1_), custom_call_target="tpu_custom_call" | custom-call | flops 2147483648 | bytes 10485760 | tf_op jit(solution)/shard_map/integrals_far/pallas_call | solution.py:205
  88.9 2.7 %contract_late.1 = f32[16,8,64]{2,1,0:T(8,128)S(1)} custom-call(bf16[1,512,1024]{2,1,0:T(8,128)(2,1)S(1)} %integrals_near.1.refs_0_, bf16[2,512,1024]{2,1,0:T(8,128)(2,1)S(1)} %integrals_side.1.refs_1_, bf16[1,512,1024]{2,1,0:T(8,128)(2,1)S(1)} %integrals_far.1.refs_2_, bf16[128,4096]{1,0:T(8,128)(2,1)S(1)} %lay.2.refs_2_.refs_3_, ...), custom_call_target="tpu_custom_call" | custom-call | flops 1879048192 | bytes 8388608 | tf_op jit(solution)/shard_map/contract_late/pallas_call | solution.py:294
  91.6 16.3 %all_to_all.16 = f32[128,1,64]{2,1,0:T(1,128)S(1)} all-to-all(f32[128,1,64]{2,1,0:T(1,128)S(1)} %bitcast.8), channel_id=1, replica_groups=mesh['x'=4,'yl'=2,'z'=4,'yh'=2,'c'=2] {'z','yh','c','x','yl'}, dimensions={0} | all-to-all | bytes 65536 | tf_op jit(solution)/shard_map/all_to_all | solution.py:384
  (58 shorter events, 27.0 us)
Async XLA Ops:
  2.7 19.0 %all-to-all-start = ((bf16[8,64,512]{2,1,0:T(8,128)(2,1)}), bf16[8,64,512]{2,1,0:T(8,128)(2,1)S(1)}, u32[]{:S(2)}, u32[]{:S(2)}) async-start(bf16[8,64,512]{2,1,0:T(8,128)(2,1)} %bitcast.2), calls=%async_computation | async-start | bytes 1048576 | tf_op jit(solution)/shard_map/all_to_all | solution.py:336
  14.0 7.0 %collective-permute-start.1 = (bf16[32,2048]{1,0:T(8,128)(2,1)S(1)}, bf16[32,2048]{1,0:T(8,128)(2,1)S(1)}, u32[]{:S(2)}, u32[]{:S(2)}) collective-permute-start(bf16[32,2048]{1,0:T(8,128)(2,1)S(1)} %get-tuple-element.28), channel_id=1, source_target_pairs={{0,2},{2,0},{1,3},{3,1},{4,6},{6,4},{5,7},{7,5},{8,10},{10,8},{9,1... | collective-permute-start | bytes 393224 | tf_op jit(solution)/shard_map/ppermute | solution.py:17
  21.7 15.0 %collective-permute-start.5 = (bf16[8,64,512]{2,1,0:T(8,128)(2,1)S(1)}, bf16[8,64,512]{2,1,0:T(8,128)(2,1)S(1)}, u32[]{:S(2)}, u32[]{:S(2)}) collective-permute-start(bf16[8,64,512]{2,1,0:T(8,128)(2,1)S(1)} %all-to-all-done.first), channel_id=1, source_target_pairs={{0,1},{1,0},{2,3},{3,2},{4,5},{5,4},{6,7},{7,6},{8,9},{9,8},{10,11... | collective-permute-start | bytes 1572872 | tf_op jit(solution)/shard_map/ppermute | solution.py:17
  23.0 15.0 %collective-permute-start.6 = (bf16[8,64,512]{2,1,0:T(8,128)(2,1)S(1)}, bf16[8,64,512]{2,1,0:T(8,128)(2,1)S(1)}, u32[]{:S(2)}, u32[]{:S(2)}) collective-permute-start(bf16[8,64,512]{2,1,0:T(8,128)(2,1)S(1)} %all-to-all-done.first), channel_id=1, source_target_pairs={{0,2},{2,0},{1,3},{3,1},{4,6},{6,4},{5,7},{7,5},{8,10},{10,8},{9,1... | collective-permute-start | bytes 1572872 | tf_op jit(solution)/shard_map/ppermute | solution.py:17
  24.9 8.5 %collective-permute-start.2 = (bf16[32,2048]{1,0:T(8,128)(2,1)S(1)}, bf16[32,2048]{1,0:T(8,128)(2,1)S(1)}, u32[]{:S(2)}, u32[]{:S(2)}) collective-permute-start(bf16[32,2048]{1,0:T(8,128)(2,1)S(1)} %choose.1.own), channel_id=1, source_target_pairs={{0,4},{4,8},{8,12},{12,0},{1,5},{5,9},{9,13},{13,1},{2,6},{6,10},{... | collective-permute-start | bytes 393224 | tf_op jit(solution)/shard_map/ppermute | solution.py:17
  26.6 6.8 %collective-permute-start.3 = (bf16[32,2048]{1,0:T(8,128)(2,1)S(1)}, bf16[32,2048]{1,0:T(8,128)(2,1)S(1)}, u32[]{:S(2)}, u32[]{:S(2)}) collective-permute-start(bf16[32,2048]{1,0:T(8,128)(2,1)S(1)} %choose.1.own), channel_id=1, source_target_pairs={{0,12},{4,0},{8,4},{12,8},{1,13},{5,1},{9,5},{13,9},{2,14},{6,2},{... | collective-permute-start | bytes 393224 | tf_op jit(solution)/shard_map/ppermute | solution.py:17
  28.7 7.2 %collective-permute-start.4 = (bf16[32,2048]{1,0:T(8,128)(2,1)S(1)}, bf16[32,2048]{1,0:T(8,128)(2,1)S(1)}, u32[]{:S(2)}, u32[]{:S(2)}) collective-permute-start(bf16[32,2048]{1,0:T(8,128)(2,1)S(1)} %choose.1.own), channel_id=1, source_target_pairs={{0,8},{4,12},{8,0},{12,4},{1,9},{5,13},{9,1},{13,5},{2,10},{6,14},... | collective-permute-start | bytes 393224 | tf_op jit(solution)/shard_map/ppermute | solution.py:17
  38.0 4.6 %collective-permute-start.10 = (bf16[8,64,512]{2,1,0:T(8,128)(2,1)S(1)}, bf16[8,64,512]{2,1,0:T(8,128)(2,1)S(1)}, u32[]{:S(2)}, u32[]{:S(2)}) collective-permute-start(bf16[8,64,512]{2,1,0:T(8,128)(2,1)S(1)} %collective-permute-done.6.first), channel_id=1, source_target_pairs={{0,1},{1,0},{2,3},{3,2},{4,5},{5,4},{6,7},{7,6},{8,9},{9,8},{10,11... | collective-permute-start | bytes 1572872 | tf_op jit(solution)/shard_map/ppermute | solution.py:17
  38.9 19.8 %collective-permute-start.14 = (bf16[128,4096]{1,0:T(8,128)(2,1)S(1)}, bf16[128,4096]{1,0:T(8,128)(2,1)S(1)}, u32[]{:S(2)}, u32[]{:S(2)}) collective-permute-start(bf16[128,4096]{1,0:T(8,128)(2,1)S(1)} %lay.2.refs_2_.refs_3_), channel_id=1, source_target_pairs={{0,4},{1,13},{4,8},{5,1},{8,12},{9,5},{12,0},{13,9},{2,6},{3,15},{... | collective-permute-start | bytes 3145736 | tf_op jit(solution)/shard_map/ppermute | solution.py:325
  42.8 22.8 %collective-permute-start.15 = (bf16[128,4096]{1,0:T(8,128)(2,1)S(1)}, bf16[128,4096]{1,0:T(8,128)(2,1)S(1)}, u32[]{:S(2)}, u32[]{:S(2)}) collective-permute-start(bf16[128,4096]{1,0:T(8,128)(2,1)S(1)} %lay.3.refs_3_.refs_4_), channel_id=1, source_target_pairs={{0,4},{1,13},{4,8},{5,1},{8,12},{9,5},{12,0},{13,9},{2,6},{3,15},{... | collective-permute-start | bytes 3145736 | tf_op jit(solution)/shard_map/ppermute | solution.py:325
  44.4 5.7 %collective-permute-start.7 = (bf16[32,2048]{1,0:T(8,128)(2,1)S(1)}, bf16[32,2048]{1,0:T(8,128)(2,1)S(1)}, u32[]{:S(2)}, u32[]{:S(2)}) collective-permute-start(bf16[32,2048]{1,0:T(8,128)(2,1)S(1)} %choose_z.1.own), channel_id=1, source_target_pairs={{0,16},{16,2},{2,18},{18,0},{1,17},{17,3},{3,19},{19,1},{4,20},{20... | collective-permute-start | bytes 393224 | tf_op jit(solution)/shard_map/ppermute | solution.py:22
  45.9 5.5 %collective-permute-start.8 = (bf16[32,2048]{1,0:T(8,128)(2,1)S(1)}, bf16[32,2048]{1,0:T(8,128)(2,1)S(1)}, u32[]{:S(2)}, u32[]{:S(2)}) collective-permute-start(bf16[32,2048]{1,0:T(8,128)(2,1)S(1)} %choose_z.1.own), channel_id=1, source_target_pairs={{0,18},{16,0},{2,16},{18,2},{1,19},{17,1},{3,17},{19,3},{4,22},{20... | collective-permute-start | bytes 393224 | tf_op jit(solution)/shard_map/ppermute | solution.py:22
  47.0 6.7 %collective-permute-start.9 = (bf16[32,2048]{1,0:T(8,128)(2,1)S(1)}, bf16[32,2048]{1,0:T(8,128)(2,1)S(1)}, u32[]{:S(2)}, u32[]{:S(2)}) collective-permute-start(bf16[32,2048]{1,0:T(8,128)(2,1)S(1)} %choose_z.1.own), channel_id=1, source_target_pairs={{0,2},{16,18},{2,0},{18,16},{1,3},{17,19},{3,1},{19,17},{4,6},{20,... | collective-permute-start | bytes 393224 | tf_op jit(solution)/shard_map/ppermute | solution.py:22
  54.9 14.4 %collective-permute-start.11 = (bf16[128,2048]{1,0:T(8,128)(2,1)S(1)}, bf16[128,2048]{1,0:T(8,128)(2,1)S(1)}, u32[]{:S(2)}, u32[]{:S(2)}) collective-permute-start(bf16[128,2048]{1,0:T(8,128)(2,1)S(1)} %place.1.refs_0_), channel_id=1, source_target_pairs={{0,32},{1,97},{32,64},{33,1},{64,96},{65,33},{96,0},{97,65},{2,34}... | collective-permute-start | bytes 1572872 | tf_op jit(solution)/shard_map/ppermute | solution.py:325
  57.1 12.2 %collective-permute-start.13 = (bf16[128,2048]{1,0:T(8,128)(2,1)S(1)}, bf16[128,2048]{1,0:T(8,128)(2,1)S(1)}, u32[]{:S(2)}, u32[]{:S(2)}) collective-permute-start(bf16[128,2048]{1,0:T(8,128)(2,1)S(1)} %collective-permute-done.12.refs_1_), channel_id=1, source_target_pairs={{0,32},{1,97},{32,64},{33,1},{64,96},{65,33},{96,0},{97,65},{2,34}... | collective-permute-start | bytes 1572872 | tf_op jit(solution)/shard_map/ppermute | solution.py:325
  58.7 12.5 %collective-permute-start.16 = (bf16[64,4096]{1,0:T(8,128)(2,1)S(1)}, bf16[64,4096]{1,0:T(8,128)(2,1)S(1)}, u32[]{:S(2)}, u32[]{:S(2)}) collective-permute-start(bf16[64,4096]{1,0:T(8,128)(2,1)S(1)} %take.2), channel_id=1, source_target_pairs={{0,4},{1,13},{4,8},{5,1},{8,12},{9,5},{12,0},{13,9},{2,6},{3,15},{... | collective-permute-start | bytes 1572872 | tf_op jit(solution)/shard_map/ppermute | solution.py:325
  65.6 16.2 %collective-permute-start.20 = (bf16[128,4096]{1,0:T(8,128)(2,1)S(1)}, bf16[128,4096]{1,0:T(8,128)(2,1)S(1)}, u32[]{:S(2)}, u32[]{:S(2)}) collective-permute-start(bf16[128,4096]{1,0:T(8,128)(2,1)S(1)} %collective-permute-done.14.source.refs_4_.refs_5_), channel_id=1, source_target_pairs={{0,1},{1,0},{2,3},{3,2},{4,5},{5,4},{6,7},{7,6},{8,9},{9,8},{10,11... | collective-permute-start | bytes 3145736 | tf_op jit(solution)/shard_map/ppermute | solution.py:17
  66.9 14.9 %collective-permute-start.21 = (bf16[128,4096]{1,0:T(8,128)(2,1)S(1)}, bf16[128,4096]{1,0:T(8,128)(2,1)S(1)}, u32[]{:S(2)}, u32[]{:S(2)}) collective-permute-start(bf16[128,4096]{1,0:T(8,128)(2,1)S(1)} %collective-permute-done.15.refs_6_.source.refs_7_), channel_id=1, source_target_pairs={{0,1},{1,0},{2,3},{3,2},{4,5},{5,4},{6,7},{7,6},{8,9},{9,8},{10,11... | collective-permute-start | bytes 3145736 | tf_op jit(solution)/shard_map/ppermute | solution.py:17
  71.2 3.8 %collective-permute-start.17 = (bf16[128,2048]{1,0:T(8,128)(2,1)S(1)}, bf16[128,2048]{1,0:T(8,128)(2,1)S(1)}, u32[]{:S(2)}, u32[]{:S(2)}) collective-permute-start(bf16[128,2048]{1,0:T(8,128)(2,1)S(1)} %collective-permute-done.11.refs_0_), channel_id=1, source_target_pairs={{0,1},{1,0},{2,3},{3,2},{4,5},{5,4},{6,7},{7,6},{8,9},{9,8},{10,11... | collective-permute-start | bytes 1572872 | tf_op jit(solution)/shard_map/ppermute | solution.py:17
  72.5 4.7 %collective-permute-start.18 = (bf16[128,2048]{1,0:T(8,128)(2,1)S(1)}, bf16[128,2048]{1,0:T(8,128)(2,1)S(1)}, u32[]{:S(2)}, u32[]{:S(2)}) collective-permute-start(bf16[128,2048]{1,0:T(8,128)(2,1)S(1)} %collective-permute-done.13.refs_1_), channel_id=1, source_target_pairs={{0,1},{1,0},{2,3},{3,2},{4,5},{5,4},{6,7},{7,6},{8,9},{9,8},{10,11... | collective-permute-start | bytes 1572872 | tf_op jit(solution)/shard_map/ppermute | solution.py:17
  72.6 12.5 %collective-permute-start.24 = (bf16[64,4096]{1,0:T(8,128)(2,1)S(1)}, bf16[64,4096]{1,0:T(8,128)(2,1)S(1)}, u32[]{:S(2)}, u32[]{:S(2)}) collective-permute-start(bf16[64,4096]{1,0:T(8,128)(2,1)S(1)} %take.3), channel_id=1, source_target_pairs={{0,4},{1,13},{4,8},{5,1},{8,12},{9,5},{12,0},{13,9},{2,6},{3,15},{... | collective-permute-start | bytes 1572872 | tf_op jit(solution)/shard_map/ppermute | solution.py:325
  75.0 9.5 %collective-permute-start.19 = (bf16[128,2048]{1,0:T(8,128)(2,1)S(1)}, bf16[128,2048]{1,0:T(8,128)(2,1)S(1)}, u32[]{:S(2)}, u32[]{:S(2)}) collective-permute-start(bf16[128,2048]{1,0:T(8,128)(2,1)S(1)} %collective-permute-done.11.refs_0_), channel_id=1, source_target_pairs={{0,32},{1,97},{32,64},{33,1},{64,96},{65,33},{96,0},{97,65},{2,34}... | collective-permute-start | bytes 1572872 | tf_op jit(solution)/shard_map/ppermute | solution.py:325
  84.8 4.0 %collective-permute-start.23 = (bf16[64,4096]{1,0:T(8,128)(2,1)S(1)}, bf16[64,4096]{1,0:T(8,128)(2,1)S(1)}, u32[]{:S(2)}, u32[]{:S(2)}) collective-permute-start(bf16[64,4096]{1,0:T(8,128)(2,1)S(1)} %collective-permute-done.16.refs_9_), channel_id=1, source_target_pairs={{0,1},{1,0},{2,3},{3,2},{4,5},{5,4},{6,7},{7,6},{8,9},{9,8},{10,11... | collective-permute-start | bytes 1572872 | tf_op jit(solution)/shard_map/ppermute | solution.py:17
  85.0 3.8 %collective-permute-start.25 = (bf16[64,4096]{1,0:T(8,128)(2,1)S(1)}, bf16[64,4096]{1,0:T(8,128)(2,1)S(1)}, u32[]{:S(2)}, u32[]{:S(2)}) collective-permute-start(bf16[64,4096]{1,0:T(8,128)(2,1)S(1)} %collective-permute-done.24.refs_11_), channel_id=1, source_target_pairs={{0,1},{1,0},{2,3},{3,2},{4,5},{5,4},{6,7},{7,6},{8,9},{9,8},{10,11... | collective-permute-start | bytes 1572872 | tf_op jit(solution)/shard_map/ppermute | solution.py:17
  (8 other events, 77.3 us)

commit v6 on v5

--- a/solution.py
+++ b/solution.py
@@ -332,11 +332,12 @@
     c = lax.axis_index("c")
     factors = pltpu.with_memory_space_constraint(factors, pltpu.HBM)
 
+    mine, other = move_call(
+        functools.partial(pick_kernel, rows_here), "pick", [(cols_here, aux)] * 2, 1, 2)(window_offsets, factors)
+    mine, other, amplitudes = lax.optimization_barrier((mine, other, amplitudes))
+    swapped = core_swap(other)
     tau = amplitudes[0].T.reshape(8, cols_here, virt)
     tau = lax.all_to_all(tau, PAIR, split_axis=0, concat_axis=0, tiled=True)
-    mine, other = move_call(
-        functools.partial(pick_kernel, rows_here), "pick", [(cols_here, aux)] * 2, 1, 2)(window_offsets, factors)
-    swapped = core_swap(other)
     keep, send = move_call(
         functools.partial(halve_kernel, rows_here), "halve", [(cols_here // 2, aux)] * 2, 2, 2)(
             window_offsets, mine, swapped)

time: 110 us -> 109 us (level)
  waiting for transfers between devices: 23.2 us -> 28.7 us
  starting transfers between devices: 41.7 us -> 38.1 us
  blocking collectives: 16.3 us -> 14.7 us
    ppermute x16, waiting for transfers between devices: 10.2 us -> 14.3 us  [shift(): return lax.ppermute(x, axis, [(i, (i + step) % size) for i in range(size)])]
    ppermute x16, starting transfers between devices: 16.9 us -> 14.9 us  [shift(): return lax.ppermute(x, axis, [(i, (i + step) % size) for i in range(size)])]
    all_to_all x1, blocking collectives: 16.3 us -> 14.7 us  [local(): lax.all_to_all(partial.reshape(128, 2 * rows_here), TILE + PAIR, split_ax...]
    ppermute x7, waiting for transfers between devices: 7.28 us -> 8.54 us  [both_ways(): return lax.ppermute(x, (axis, 'c'), pairs)]
    ppermute x7, starting transfers between devices: 15.3 us -> 14.2 us  [both_ways(): return lax.ppermute(x, (axis, 'c'), pairs)]
  transfers between devices with their start and end apart: 27 -> 27, of which waited for: 10 -> 10; matrix products, arithmetic and copies ran while one was open for 0% -> 0% of each run, Pallas kernels for 19% -> 17%
where the time goes in v6:
time: 109 us; the launch traced here: 108 us
  starting transfers between devices  38.1 us (35%)
  waiting for transfers between devices  28.7 us (26%)
  Pallas kernels  24.4 us (22%)
  blocking collectives  14.7 us (13%)
  local copies, waits for them, and re-layouts  1.67 us (2%)
    ppermute x16, starting transfers between devices, shift(): return lax.ppermute(x, axis, [(i, (i + step) % size) for i in range(size)])  14.9 us
    all_to_all x1, blocking collectives, local(): lax.all_to_all(partial.reshape(128, 2 * rows_here), TILE + PAIR, split_ax...  14.7 us
    ppermute x16, waiting for transfers between devices, shift(): return lax.ppermute(x, axis, [(i, (i + step) % size) for i in range(size)])  14.3 us
    ppermute x7, starting transfers between devices, both_ways(): return lax.ppermute(x, (axis, 'c'), pairs)  14.2 us
    pallas_call x3, Pallas kernels, integrals_of(): pl.pallas_call(first_kernel if load else functools.partial(next_kernel, f...  9.26 us
    ppermute x7, waiting for transfers between devices, both_ways(): return lax.ppermute(x, (axis, 'c'), pairs)  8.54 us
    all_to_all x1, starting transfers between devices, local(): tau = lax.all_to_all(tau, PAIR, split_axis=0, concat_axis=0, tiled=True)  5.86 us
    ppermute x3, waiting for transfers between devices, shift_y(): lax.ppermute(x, ('yl', 'yh'), [(at[y], at[(y + step) % 4]) for y in range...  5.79 us
  transfers between devices with their start and end apart: 27, of which 10 were waited for; matrix products, arithmetic and copies ran while one was open for 0% of the time, Pallas kernels for 17%

profile of v6, /device:TPU:1, one launch (start us, length us, event | category | flops | bytes accessed | tf_op | source)
XLA Modules:
  0.0 108.5 jit_solution(8294417028972418498)
XLA Ops:
  1.3 1.6 %pick.1 = (bf16[64,2048]{1,0:T(8,128)(2,1)S(1)}, bf16[64,2048]{1,0:T(8,128)(2,1)S(1)}) custom-call(s32[2]{0:T(128)S(1)} %copy-done, bf16[32,64,2048]{2,1,0:T(8,128)(2,1)} %source), custom_call_target="tpu_custom_call" | custom-call | bytes 1048576 | tf_op jit(solution)/shard_map/pick/pallas_call | solution.py:335
  3.9 5.9 %all-to-all-start = ((bf16[8,64,512]{2,1,0:T(8,128)(2,1)}), bf16[8,64,512]{2,1,0:T(8,128)(2,1)S(1)}, u32[]{:S(2)}, u32[]{:S(2)}) async-start(bf16[8,64,512]{2,1,0:T(8,128)(2,1)} %bitcast.2), calls=%async_computation | async-start | bytes 1048576 | tf_op jit(solution)/shard_map/all_to_all | solution.py:340
  12.8 2.7 %collective-permute-start.1 = (bf16[32,2048]{1,0:T(8,128)(2,1)S(1)}, bf16[32,2048]{1,0:T(8,128)(2,1)S(1)}, u32[]{:S(2)}, u32[]{:S(2)}) collective-permute-start(bf16[32,2048]{1,0:T(8,128)(2,1)S(1)} %get-tuple-element.33), channel_id=1, source_target_pairs={{0,2},{2,0},{1,3},{3,1},{4,6},{6,4},{5,7},{7,5},{8,10},{10,8},{9,1... | collective-permute-start | bytes 393224 | tf_op jit(solution)/shard_map/ppermute | solution.py:17
  15.5 7.1 %collective-permute-done.1.got = bf16[32,2048]{1,0:T(8,128)(2,1)S(1)} collective-permute-done((bf16[32,2048]{1,0:T(8,128)(2,1)S(1)}, bf16[32,2048]{1,0:T(8,128)(2,1)S(1)}, u32[]{:S(2)}, u32[]{:S(2)}) %collective-permute-start.1) | collective-permute-done | bytes 131104 | tf_op jit(solution)/shard_map/ppermute | solution.py:17
  24.5 1.6 %collective-permute-start.2 = (bf16[32,2048]{1,0:T(8,128)(2,1)S(1)}, bf16[32,2048]{1,0:T(8,128)(2,1)S(1)}, u32[]{:S(2)}, u32[]{:S(2)}) collective-permute-start(bf16[32,2048]{1,0:T(8,128)(2,1)S(1)} %choose.1.own), channel_id=1, source_target_pairs={{0,4},{4,8},{8,12},{12,0},{1,5},{5,9},{9,13},{13,1},{2,6},{6,10},{... | collective-permute-start | bytes 393224 | tf_op jit(solution)/shard_map/ppermute | solution.py:17
  26.1 2.1 %collective-permute-start.3 = (bf16[32,2048]{1,0:T(8,128)(2,1)S(1)}, bf16[32,2048]{1,0:T(8,128)(2,1)S(1)}, u32[]{:S(2)}, u32[]{:S(2)}) collective-permute-start(bf16[32,2048]{1,0:T(8,128)(2,1)S(1)} %choose.1.own), channel_id=1, source_target_pairs={{0,12},{4,0},{8,4},{12,8},{1,13},{5,1},{9,5},{13,9},{2,14},{6,2},{... | collective-permute-start | bytes 393224 | tf_op jit(solution)/shard_map/ppermute | solution.py:17
  29.6 3.4 %hold.1.held = bf16[32,64,2048]{2,1,0:T(8,128)(2,1)S(1)} custom-call(bf16[32,64,2048]{2,1,0:T(8,128)(2,1)} %source), custom_call_target="tpu_custom_call" | custom-call | bytes 16777216 | tf_op jit(solution)/shard_map/hold/pallas_call | solution.py:117
  33.0 2.5 %collective-permute-done.4.far = bf16[32,2048]{1,0:T(8,128)(2,1)S(1)} collective-permute-done((bf16[32,2048]{1,0:T(8,128)(2,1)S(1)}, bf16[32,2048]{1,0:T(8,128)(2,1)S(1)}, u32[]{:S(2)}, u32[]{:S(2)}) %collective-permute-start.4) | collective-permute-done | bytes 131104 | tf_op jit(solution)/shard_map/ppermute | solution.py:17
  36.4 2.5 %collective-permute-done.6.first = bf16[8,64,512]{2,1,0:T(8,128)(2,1)S(1)} collective-permute-done((bf16[8,64,512]{2,1,0:T(8,128)(2,1)S(1)}, bf16[8,64,512]{2,1,0:T(8,128)(2,1)S(1)}, u32[]{:S(2)}, u32[]{:S(2)}) %collective-permute-start.6) | collective-permute-done | bytes 524320 | tf_op jit(solution)/shard_map/ppermute | solution.py:17
  39.8 3.8 %collective-permute-start.14 = (bf16[128,4096]{1,0:T(8,128)(2,1)S(1)}, bf16[128,4096]{1,0:T(8,128)(2,1)S(1)}, u32[]{:S(2)}, u32[]{:S(2)}) collective-permute-start(bf16[128,4096]{1,0:T(8,128)(2,1)S(1)} %lay.2.refs_2_.refs_3_), channel_id=1, source_target_pairs={{0,4},{1,13},{4,8},{5,1},{8,12},{9,5},{12,0},{13,9},{2,6},{3,15},{... | collective-permute-start | bytes 3145736 | tf_op jit(solution)/shard_map/ppermute | solution.py:325
  43.7 1.6 %collective-permute-start.15 = (bf16[128,4096]{1,0:T(8,128)(2,1)S(1)}, bf16[128,4096]{1,0:T(8,128)(2,1)S(1)}, u32[]{:S(2)}, u32[]{:S(2)}) collective-permute-start(bf16[128,4096]{1,0:T(8,128)(2,1)S(1)} %lay.3.refs_3_.refs_4_), channel_id=1, source_target_pairs={{0,4},{1,13},{4,8},{5,1},{8,12},{9,5},{12,0},{13,9},{2,6},{3,15},{... | collective-permute-start | bytes 3145736 | tf_op jit(solution)/shard_map/ppermute | solution.py:325
  48.5 2.6 %collective-permute-done.7.up = bf16[32,2048]{1,0:T(8,128)(2,1)S(1)} collective-permute-done((bf16[32,2048]{1,0:T(8,128)(2,1)S(1)}, bf16[32,2048]{1,0:T(8,128)(2,1)S(1)}, u32[]{:S(2)}, u32[]{:S(2)}) %collective-permute-start.7) | collective-permute-done | bytes 131104 | tf_op jit(solution)/shard_map/ppermute | solution.py:22
  52.2 2.1 %collective-permute-done.9.far = bf16[32,2048]{1,0:T(8,128)(2,1)S(1)} collective-permute-done((bf16[32,2048]{1,0:T(8,128)(2,1)S(1)}, bf16[32,2048]{1,0:T(8,128)(2,1)S(1)}, u32[]{:S(2)}, u32[]{:S(2)}) %collective-permute-start.9) | collective-permute-done | bytes 131104 | tf_op jit(solution)/shard_map/ppermute | solution.py:22
  55.4 2.0 %collective-permute-start.11 = (bf16[128,2048]{1,0:T(8,128)(2,1)S(1)}, bf16[128,2048]{1,0:T(8,128)(2,1)S(1)}, u32[]{:S(2)}, u32[]{:S(2)}) collective-permute-start(bf16[128,2048]{1,0:T(8,128)(2,1)S(1)} %place.1.refs_0_), channel_id=1, source_target_pairs={{0,32},{1,97},{32,64},{33,1},{64,96},{65,33},{96,0},{97,65},{2,34}... | collective-permute-start | bytes 1572872 | tf_op jit(solution)/shard_map/ppermute | solution.py:325
  59.9 6.6 %collective-permute-done.15.refs_6_.source.refs_7_ = bf16[128,4096]{1,0:T(8,128)(2,1)S(1)} collective-permute-done((bf16[128,4096]{1,0:T(8,128)(2,1)S(1)}, bf16[128,4096]{1,0:T(8,128)(2,1)S(1)}, u32[]{:S(2)}, u32[]{:S(2)}) %collective-permute-start.15) | collective-permute-done | bytes 1048608 | tf_op jit(solution)/shard_map/ppermute | solution.py:325
  67.9 2.4 %integrals_near.1.refs_0_ = bf16[1,512,1024]{2,1,0:T(8,128)(2,1)S(1)} custom-call(bf16[32,64,2048]{2,1,0:T(8,128)(2,1)S(1)} %hold.1.held, bf16[128,2048]{1,0:T(8,128)(2,1)S(1)} %place.1.refs_0_, bf16[128,2048]{1,0:T(8,128)(2,1)S(1)} %collective-permute-done.12.refs_1_), custom_call_target="tpu_custom_call" | custom-call | flops 2147483648 | bytes 10485760 | tf_op jit(solution)/shard_map/integrals_near/pallas_call | solution.py:205
  70.2 1.9 %collective-permute-done.16.refs_9_ = bf16[64,4096]{1,0:T(8,128)(2,1)S(1)} collective-permute-done((bf16[64,4096]{1,0:T(8,128)(2,1)S(1)}, bf16[64,4096]{1,0:T(8,128)(2,1)S(1)}, u32[]{:S(2)}, u32[]{:S(2)}) %collective-permute-start.16) | collective-permute-done | bytes 524320 | tf_op jit(solution)/shard_map/ppermute | solution.py:325
  73.5 2.4 %collective-permute-start.24 = (bf16[64,4096]{1,0:T(8,128)(2,1)S(1)}, bf16[64,4096]{1,0:T(8,128)(2,1)S(1)}, u32[]{:S(2)}, u32[]{:S(2)}) collective-permute-start(bf16[64,4096]{1,0:T(8,128)(2,1)S(1)} %take.3), channel_id=1, source_target_pairs={{0,4},{1,13},{4,8},{5,1},{8,12},{9,5},{12,0},{13,9},{2,6},{3,15},{... | collective-permute-start | bytes 1572872 | tf_op jit(solution)/shard_map/ppermute | solution.py:325
  75.9 2.0 %collective-permute-start.19 = (bf16[128,2048]{1,0:T(8,128)(2,1)S(1)}, bf16[128,2048]{1,0:T(8,128)(2,1)S(1)}, u32[]{:S(2)}, u32[]{:S(2)}) collective-permute-start(bf16[128,2048]{1,0:T(8,128)(2,1)S(1)} %collective-permute-done.11.refs_0_), channel_id=1, source_target_pairs={{0,32},{1,97},{32,64},{33,1},{64,96},{65,33},{96,0},{97,65},{2,34}... | collective-permute-start | bytes 1572872 | tf_op jit(solution)/shard_map/ppermute | solution.py:325
  77.9 4.5 %integrals_side.1.refs_1_ = bf16[2,512,1024]{2,1,0:T(8,128)(2,1)S(1)} custom-call(bf16[32,64,2048]{2,1,0:T(8,128)(2,1)S(1)} %hold.1.held, bf16[128,2048]{1,0:T(8,128)(2,1)S(1)} %collective-permute-done.11.refs_0_, bf16[128,2048]{1,0:T(8,128)(2,1)S(1)} %collective-permute-done.13.refs_1_, bf16[128,2048]{1,0:T(8,128)(2,1)S(1)} %collective-permute-done.17.refs_2_, ...), custom_call_target="tpu_custom_call" | custom-call | flops 4294967296 | bytes 10485760 | tf_op jit(solution)/shard_map/integrals_side/pallas_call | solution.py:205
  82.4 2.6 %contract_early.1.refs_13_ = f32[3,2,512,128]{3,2,1,0:T(8,128)S(1)} custom-call(bf16[1,512,1024]{2,1,0:T(8,128)(2,1)S(1)} %integrals_near.1.refs_0_, bf16[2,512,1024]{2,1,0:T(8,128)(2,1)S(1)} %integrals_side.1.refs_1_, bf16[128,4096]{1,0:T(8,128)(2,1)S(1)} %lay.2.refs_2_.refs_3_, bf16[128,4096]{1,0:T(8,128)(2,1)S(1)} %lay.3.refs_3_.refs_4_, ...), custom_call_target="tpu_custom_call" | custom-call | flops 2415919104 | bytes 8388608 | tf_op jit(solution)/shard_map/contract_early/pallas_call | solution.py:294
  87.3 2.4 %integrals_far.1.refs_2_ = bf16[1,512,1024]{2,1,0:T(8,128)(2,1)S(1)} custom-call(bf16[32,64,2048]{2,1,0:T(8,128)(2,1)S(1)} %hold.1.held, bf16[128,2048]{1,0:T(8,128)(2,1)S(1)} %collective-permute-done.19.refs_0_, bf16[128,2048]{1,0:T(8,128)(2,1)S(1)} %collective-permute-done.22.refs_1_), custom_call_target="tpu_custom_call" | custom-call | flops 2147483648 | bytes 10485760 | tf_op jit(solution)/shard_map/integrals_far/pallas_call | solution.py:205
  89.7 2.7 %contract_late.1 = f32[16,8,64]{2,1,0:T(8,128)S(1)} custom-call(bf16[1,512,1024]{2,1,0:T(8,128)(2,1)S(1)} %integrals_near.1.refs_0_, bf16[2,512,1024]{2,1,0:T(8,128)(2,1)S(1)} %integrals_side.1.refs_1_, bf16[1,512,1024]{2,1,0:T(8,128)(2,1)S(1)} %integrals_far.1.refs_2_, bf16[128,4096]{1,0:T(8,128)(2,1)S(1)} %lay.2.refs_2_.refs_3_, ...), custom_call_target="tpu_custom_call" | custom-call | flops 1879048192 | bytes 8388608 | tf_op jit(solution)/shard_map/contract_late/pallas_call | solution.py:294
  92.5 14.7 %all_to_all.16 = f32[128,1,64]{2,1,0:T(1,128)S(1)} all-to-all(f32[128,1,64]{2,1,0:T(1,128)S(1)} %bitcast.8), channel_id=1, replica_groups=mesh['x'=4,'yl'=2,'z'=4,'yh'=2,'c'=2] {'z','yh','c','x','yl'}, dimensions={0} | all-to-all | bytes 65536 | tf_op jit(solution)/shard_map/all_to_all | solution.py:385
  (60 shorter events, 23.9 us)
Async XLA Ops:
  3.9 19.5 %all-to-all-start = ((bf16[8,64,512]{2,1,0:T(8,128)(2,1)}), bf16[8,64,512]{2,1,0:T(8,128)(2,1)S(1)}, u32[]{:S(2)}, u32[]{:S(2)}) async-start(bf16[8,64,512]{2,1,0:T(8,128)(2,1)} %bitcast.2), calls=%async_computation | async-start | bytes 1048576 | tf_op jit(solution)/shard_map/all_to_all | solution.py:340
  12.8 9.8 %collective-permute-start.1 = (bf16[32,2048]{1,0:T(8,128)(2,1)S(1)}, bf16[32,2048]{1,0:T(8,128)(2,1)S(1)}, u32[]{:S(2)}, u32[]{:S(2)}) collective-permute-start(bf16[32,2048]{1,0:T(8,128)(2,1)S(1)} %get-tuple-element.33), channel_id=1, source_target_pairs={{0,2},{2,0},{1,3},{3,1},{4,6},{6,4},{5,7},{7,5},{8,10},{10,8},{9,1... | collective-permute-start | bytes 393224 | tf_op jit(solution)/shard_map/ppermute | solution.py:17
  23.4 12.9 %collective-permute-start.5 = (bf16[8,64,512]{2,1,0:T(8,128)(2,1)S(1)}, bf16[8,64,512]{2,1,0:T(8,128)(2,1)S(1)}, u32[]{:S(2)}, u32[]{:S(2)}) collective-permute-start(bf16[8,64,512]{2,1,0:T(8,128)(2,1)S(1)} %all-to-all-done.first), channel_id=1, source_target_pairs={{0,1},{1,0},{2,3},{3,2},{4,5},{5,4},{6,7},{7,6},{8,9},{9,8},{10,11... | collective-permute-start | bytes 1572872 | tf_op jit(solution)/shard_map/ppermute | solution.py:17
  23.9 15.0 %collective-permute-start.6 = (bf16[8,64,512]{2,1,0:T(8,128)(2,1)S(1)}, bf16[8,64,512]{2,1,0:T(8,128)(2,1)S(1)}, u32[]{:S(2)}, u32[]{:S(2)}) collective-permute-start(bf16[8,64,512]{2,1,0:T(8,128)(2,1)S(1)} %all-to-all-done.first), channel_id=1, source_target_pairs={{0,2},{2,0},{1,3},{3,1},{4,6},{6,4},{5,7},{7,5},{8,10},{10,8},{9,1... | collective-permute-start | bytes 1572872 | tf_op jit(solution)/shard_map/ppermute | solution.py:17
  24.5 8.5 %collective-permute-start.2 = (bf16[32,2048]{1,0:T(8,128)(2,1)S(1)}, bf16[32,2048]{1,0:T(8,128)(2,1)S(1)}, u32[]{:S(2)}, u32[]{:S(2)}) collective-permute-start(bf16[32,2048]{1,0:T(8,128)(2,1)S(1)} %choose.1.own), channel_id=1, source_target_pairs={{0,4},{4,8},{8,12},{12,0},{1,5},{5,9},{9,13},{13,1},{2,6},{6,10},{... | collective-permute-start | bytes 393224 | tf_op jit(solution)/shard_map/ppermute | solution.py:17
  26.1 6.8 %collective-permute-start.3 = (bf16[32,2048]{1,0:T(8,128)(2,1)S(1)}, bf16[32,2048]{1,0:T(8,128)(2,1)S(1)}, u32[]{:S(2)}, u32[]{:S(2)}) collective-permute-start(bf16[32,2048]{1,0:T(8,128)(2,1)S(1)} %choose.1.own), channel_id=1, source_target_pairs={{0,12},{4,0},{8,4},{12,8},{1,13},{5,1},{9,5},{13,9},{2,14},{6,2},{... | collective-permute-start | bytes 393224 | tf_op jit(solution)/shard_map/ppermute | solution.py:17
  28.3 7.2 %collective-permute-start.4 = (bf16[32,2048]{1,0:T(8,128)(2,1)S(1)}, bf16[32,2048]{1,0:T(8,128)(2,1)S(1)}, u32[]{:S(2)}, u32[]{:S(2)}) collective-permute-start(bf16[32,2048]{1,0:T(8,128)(2,1)S(1)} %choose.1.own), channel_id=1, source_target_pairs={{0,8},{4,12},{8,0},{12,4},{1,9},{5,13},{9,1},{13,5},{2,10},{6,14},... | collective-permute-start | bytes 393224 | tf_op jit(solution)/shard_map/ppermute | solution.py:17
  38.9 4.6 %collective-permute-start.10 = (bf16[8,64,512]{2,1,0:T(8,128)(2,1)S(1)}, bf16[8,64,512]{2,1,0:T(8,128)(2,1)S(1)}, u32[]{:S(2)}, u32[]{:S(2)}) collective-permute-start(bf16[8,64,512]{2,1,0:T(8,128)(2,1)S(1)} %collective-permute-done.6.first), channel_id=1, source_target_pairs={{0,1},{1,0},{2,3},{3,2},{4,5},{5,4},{6,7},{7,6},{8,9},{9,8},{10,11... | collective-permute-start | bytes 1572872 | tf_op jit(solution)/shard_map/ppermute | solution.py:17
  39.8 19.1 %collective-permute-start.14 = (bf16[128,4096]{1,0:T(8,128)(2,1)S(1)}, bf16[128,4096]{1,0:T(8,128)(2,1)S(1)}, u32[]{:S(2)}, u32[]{:S(2)}) collective-permute-start(bf16[128,4096]{1,0:T(8,128)(2,1)S(1)} %lay.2.refs_2_.refs_3_), channel_id=1, source_target_pairs={{0,4},{1,13},{4,8},{5,1},{8,12},{9,5},{12,0},{13,9},{2,6},{3,15},{... | collective-permute-start | bytes 3145736 | tf_op jit(solution)/shard_map/ppermute | solution.py:325
  43.7 22.8 %collective-permute-start.15 = (bf16[128,4096]{1,0:T(8,128)(2,1)S(1)}, bf16[128,4096]{1,0:T(8,128)(2,1)S(1)}, u32[]{:S(2)}, u32[]{:S(2)}) collective-permute-start(bf16[128,4096]{1,0:T(8,128)(2,1)S(1)} %lay.3.refs_3_.refs_4_), channel_id=1, source_target_pairs={{0,4},{1,13},{4,8},{5,1},{8,12},{9,5},{12,0},{13,9},{2,6},{3,15},{... | collective-permute-start | bytes 3145736 | tf_op jit(solution)/shard_map/ppermute | solution.py:325
  45.3 5.7 %collective-permute-start.7 = (bf16[32,2048]{1,0:T(8,128)(2,1)S(1)}, bf16[32,2048]{1,0:T(8,128)(2,1)S(1)}, u32[]{:S(2)}, u32[]{:S(2)}) collective-permute-start(bf16[32,2048]{1,0:T(8,128)(2,1)S(1)} %choose_z.1.own), channel_id=1, source_target_pairs={{0,16},{16,2},{2,18},{18,0},{1,17},{17,3},{3,19},{19,1},{4,20},{20... | collective-permute-start | bytes 393224 | tf_op jit(solution)/shard_map/ppermute | solution.py:22
  46.7 5.5 %collective-permute-start.8 = (bf16[32,2048]{1,0:T(8,128)(2,1)S(1)}, bf16[32,2048]{1,0:T(8,128)(2,1)S(1)}, u32[]{:S(2)}, u32[]{:S(2)}) collective-permute-start(bf16[32,2048]{1,0:T(8,128)(2,1)S(1)} %choose_z.1.own), channel_id=1, source_target_pairs={{0,18},{16,0},{2,16},{18,2},{1,19},{17,1},{3,17},{19,3},{4,22},{20... | collective-permute-start | bytes 393224 | tf_op jit(solution)/shard_map/ppermute | solution.py:22
  48.0 6.3 %collective-permute-start.9 = (bf16[32,2048]{1,0:T(8,128)(2,1)S(1)}, bf16[32,2048]{1,0:T(8,128)(2,1)S(1)}, u32[]{:S(2)}, u32[]{:S(2)}) collective-permute-start(bf16[32,2048]{1,0:T(8,128)(2,1)S(1)} %choose_z.1.own), channel_id=1, source_target_pairs={{0,2},{16,18},{2,0},{18,16},{1,3},{17,19},{3,1},{19,17},{4,6},{20,... | collective-permute-start | bytes 393224 | tf_op jit(solution)/shard_map/ppermute | solution.py:22
  55.4 14.8 %collective-permute-start.11 = (bf16[128,2048]{1,0:T(8,128)(2,1)S(1)}, bf16[128,2048]{1,0:T(8,128)(2,1)S(1)}, u32[]{:S(2)}, u32[]{:S(2)}) collective-permute-start(bf16[128,2048]{1,0:T(8,128)(2,1)S(1)} %place.1.refs_0_), channel_id=1, source_target_pairs={{0,32},{1,97},{32,64},{33,1},{64,96},{65,33},{96,0},{97,65},{2,34}... | collective-permute-start | bytes 1572872 | tf_op jit(solution)/shard_map/ppermute | solution.py:325
  57.3 12.9 %collective-permute-start.13 = (bf16[128,2048]{1,0:T(8,128)(2,1)S(1)}, bf16[128,2048]{1,0:T(8,128)(2,1)S(1)}, u32[]{:S(2)}, u32[]{:S(2)}) collective-permute-start(bf16[128,2048]{1,0:T(8,128)(2,1)S(1)} %collective-permute-done.12.refs_1_), channel_id=1, source_target_pairs={{0,32},{1,97},{32,64},{33,1},{64,96},{65,33},{96,0},{97,65},{2,34}... | collective-permute-start | bytes 1572872 | tf_op jit(solution)/shard_map/ppermute | solution.py:325
  59.0 13.2 %collective-permute-start.16 = (bf16[64,4096]{1,0:T(8,128)(2,1)S(1)}, bf16[64,4096]{1,0:T(8,128)(2,1)S(1)}, u32[]{:S(2)}, u32[]{:S(2)}) collective-permute-start(bf16[64,4096]{1,0:T(8,128)(2,1)S(1)} %take.2), channel_id=1, source_target_pairs={{0,4},{1,13},{4,8},{5,1},{8,12},{9,5},{12,0},{13,9},{2,6},{3,15},{... | collective-permute-start | bytes 1572872 | tf_op jit(solution)/shard_map/ppermute | solution.py:325
  66.5 15.9 %collective-permute-start.20 = (bf16[128,4096]{1,0:T(8,128)(2,1)S(1)}, bf16[128,4096]{1,0:T(8,128)(2,1)S(1)}, u32[]{:S(2)}, u32[]{:S(2)}) collective-permute-start(bf16[128,4096]{1,0:T(8,128)(2,1)S(1)} %collective-permute-done.14.source.refs_4_.refs_5_), channel_id=1, source_target_pairs={{0,1},{1,0},{2,3},{3,2},{4,5},{5,4},{6,7},{7,6},{8,9},{9,8},{10,11... | collective-permute-start | bytes 3145736 | tf_op jit(solution)/shard_map/ppermute | solution.py:17
  67.9 14.6 %collective-permute-start.21 = (bf16[128,4096]{1,0:T(8,128)(2,1)S(1)}, bf16[128,4096]{1,0:T(8,128)(2,1)S(1)}, u32[]{:S(2)}, u32[]{:S(2)}) collective-permute-start(bf16[128,4096]{1,0:T(8,128)(2,1)S(1)} %collective-permute-done.15.refs_6_.source.refs_7_), channel_id=1, source_target_pairs={{0,1},{1,0},{2,3},{3,2},{4,5},{5,4},{6,7},{7,6},{8,9},{9,8},{10,11... | collective-permute-start | bytes 3145736 | tf_op jit(solution)/shard_map/ppermute | solution.py:17
  72.2 3.8 %collective-permute-start.17 = (bf16[128,2048]{1,0:T(8,128)(2,1)S(1)}, bf16[128,2048]{1,0:T(8,128)(2,1)S(1)}, u32[]{:S(2)}, u32[]{:S(2)}) collective-permute-start(bf16[128,2048]{1,0:T(8,128)(2,1)S(1)} %collective-permute-done.11.refs_0_), channel_id=1, source_target_pairs={{0,1},{1,0},{2,3},{3,2},{4,5},{5,4},{6,7},{7,6},{8,9},{9,8},{10,11... | collective-permute-start | bytes 1572872 | tf_op jit(solution)/shard_map/ppermute | solution.py:17
  73.5 4.4 %collective-permute-start.18 = (bf16[128,2048]{1,0:T(8,128)(2,1)S(1)}, bf16[128,2048]{1,0:T(8,128)(2,1)S(1)}, u32[]{:S(2)}, u32[]{:S(2)}) collective-permute-start(bf16[128,2048]{1,0:T(8,128)(2,1)S(1)} %collective-permute-done.13.refs_1_), channel_id=1, source_target_pairs={{0,1},{1,0},{2,3},{3,2},{4,5},{5,4},{6,7},{7,6},{8,9},{9,8},{10,11... | collective-permute-start | bytes 1572872 | tf_op jit(solution)/shard_map/ppermute | solution.py:17
  73.5 12.3 %collective-permute-start.24 = (bf16[64,4096]{1,0:T(8,128)(2,1)S(1)}, bf16[64,4096]{1,0:T(8,128)(2,1)S(1)}, u32[]{:S(2)}, u32[]{:S(2)}) collective-permute-start(bf16[64,4096]{1,0:T(8,128)(2,1)S(1)} %take.3), channel_id=1, source_target_pairs={{0,4},{1,13},{4,8},{5,1},{8,12},{9,5},{12,0},{13,9},{2,6},{3,15},{... | collective-permute-start | bytes 1572872 | tf_op jit(solution)/shard_map/ppermute | solution.py:325
  75.9 9.2 %collective-permute-start.19 = (bf16[128,2048]{1,0:T(8,128)(2,1)S(1)}, bf16[128,2048]{1,0:T(8,128)(2,1)S(1)}, u32[]{:S(2)}, u32[]{:S(2)}) collective-permute-start(bf16[128,2048]{1,0:T(8,128)(2,1)S(1)} %collective-permute-done.11.refs_0_), channel_id=1, source_target_pairs={{0,32},{1,97},{32,64},{33,1},{64,96},{65,33},{96,0},{97,65},{2,34}... | collective-permute-start | bytes 1572872 | tf_op jit(solution)/shard_map/ppermute | solution.py:325
  85.8 3.9 %collective-permute-start.23 = (bf16[64,4096]{1,0:T(8,128)(2,1)S(1)}, bf16[64,4096]{1,0:T(8,128)(2,1)S(1)}, u32[]{:S(2)}, u32[]{:S(2)}) collective-permute-start(bf16[64,4096]{1,0:T(8,128)(2,1)S(1)} %collective-permute-done.16.refs_9_), channel_id=1, source_target_pairs={{0,1},{1,0},{2,3},{3,2},{4,5},{5,4},{6,7},{7,6},{8,9},{9,8},{10,11... | collective-permute-start | bytes 1572872 | tf_op jit(solution)/shard_map/ppermute | solution.py:17
  85.8 3.9 %collective-permute-start.25 = (bf16[64,4096]{1,0:T(8,128)(2,1)S(1)}, bf16[64,4096]{1,0:T(8,128)(2,1)S(1)}, u32[]{:S(2)}, u32[]{:S(2)}) collective-permute-start(bf16[64,4096]{1,0:T(8,128)(2,1)S(1)} %collective-permute-done.24.refs_11_), channel_id=1, source_target_pairs={{0,1},{1,0},{2,3},{3,2},{4,5},{5,4},{6,7},{7,6},{8,9},{9,8},{10,11... | collective-permute-start | bytes 1572872 | tf_op jit(solution)/shard_map/ppermute | solution.py:17
  (9 other events, 72.1 us)
